TPU v7x, 512 devices: a whole 4x8x8 slice. The times are simulated.
512 devices in a mesh: ctx: 32 (over z_hi, y), head: 16 (over x, z_lo, core).
Axes of the slice: x: 4, y: 8, z: 8 (z_hi: 4, z_lo: 2; z = z_hi * 2 + z_lo), core: 2. Of those that a mesh axis runs over, the one named last changes fastest.
Arguments:
- queries: bfloat16 [5120, 8192], P('ctx', 'head'), may hold values from -6 to 6
- keys: bfloat16 [5120, 2048], P('ctx', 'head'), may hold values from -6 to 6
- values: bfloat16 [5120, 2048], P('ctx', 'head'), may hold values from -6 to 6
- out_grad: bfloat16 [5120, 8192], P('ctx', 'head'), may hold values from -6 to 6
- order: int32 [64], replicated, may hold values from 0 to 63, as said below
Outputs:
- attention: bfloat16 [5120, 8192], P('ctx', 'head')
- grad_queries: bfloat16 [5120, 8192], P('ctx', 'head')
- grad_keys: bfloat16 [5120, 2048], P('ctx', 'head')
- grad_values: bfloat16 [5120, 2048], P('ctx', 'head')
Inputs may be any that keep to these rules, and one draw needn't show every extreme that they name: order is a permutation of the 64 spans; row blocks 2i and 2i + 1 (the rows of index i of ctx) hold spans c and 63 - c for some c, in either order.
All inputs are finite; a program needn't handle non-finite values.
Results may differ from a plain program's by a relative error of at most 0.03.
Values may be sent and summed in bfloat16 or wider, within the bound.
No kernel may reach another device: no remote copies, remote signals or barrier semaphores. Data moves between devices by JAX's collectives and lax.ppermute only.
A program may use at most 64 MiB of HBM per device.

v0:
```python
import math

import jax
import jax.numpy as jnp
from jax import lax
from jax.sharding import PartitionSpec as P

HEADS = 32
KV_HEADS = 8
HEAD_DIM = 128


NEG = -1e30


def shifted(array, axis, by):
    length = lax.axis_size(axis)
    return lax.ppermute(array, axis, [(i, (i + by) % length) for i in range(length)])


def attend(carry_state, q_part, q_pos, k_part, v_part, k_pos, score_scale):
    row_top, row_total, weighted = carry_state
    scores = (
        jnp.einsum("acxgd,bsxd->axgcbs", q_part, k_part, preferred_element_type=jnp.float32)
        * score_scale
    )
    visible = k_pos[None, None, None, None, :, :] <= q_pos[:, None, None, :, None, None]
    scores = jnp.where(visible, scores, NEG)
    block_top = jnp.max(scores, axis=5)
    block_weights = jnp.where(visible, jnp.exp(scores - block_top[..., None]), 0.0)
    block_total = jnp.sum(block_weights, axis=5)
    block_sums = jnp.einsum(
        "axgcbs,bsxd->axgcbd",
        block_weights.astype(jnp.bfloat16),
        v_part,
        preferred_element_type=jnp.float32,
    )
    new_top = jnp.maximum(row_top, jnp.max(block_top, axis=4))
    rescale = jnp.exp(row_top - new_top)
    block_factor = jnp.exp(block_top - new_top[..., None])
    row_total = row_total * rescale + jnp.sum(block_factor * block_total, axis=4)
    weighted = weighted * rescale[..., None] + jnp.sum(block_factor[..., None] * block_sums, axis=4)
    return (new_top, row_total, weighted)


def attend_back(q_part, g_part, log_total, row_dot, q_pos, k_part, v_part, k_pos, score_scale):
    scores = (
        jnp.einsum("acxgd,bsxd->axgcbs", q_part, k_part, preferred_element_type=jnp.float32)
        * score_scale
    )
    visible = k_pos[None, None, None, None, :, :] <= q_pos[:, None, None, :, None, None]
    probs = jnp.where(
        visible, jnp.exp(jnp.where(visible, scores, NEG) - log_total[..., None, None]), 0.0
    )
    grad_value = jnp.einsum(
        "axgcbs,acxgd->bsxd", probs.astype(jnp.bfloat16), g_part, preferred_element_type=jnp.float32
    )
    grad_probs = jnp.einsum(
        "acxgd,bsxd->axgcbs", g_part, v_part, preferred_element_type=jnp.float32
    )
    grad_scores = (probs * (grad_probs - row_dot[..., None, None])).astype(jnp.bfloat16)
    grad_query = jnp.einsum(
        "axgcbs,bsxd->acxgd", grad_scores, k_part, preferred_element_type=jnp.float32
    )
    grad_key = jnp.einsum(
        "axgcbs,acxgd->bsxd", grad_scores, q_part, preferred_element_type=jnp.float32
    )
    return (grad_query, jnp.stack([grad_key, grad_value]))


def on_device(queries, keys, values, out_grad, order):
    row_count = queries.shape[0]
    block_rows = row_count // 2
    head_width = HEAD_DIM
    score_scale = 1.0 / math.sqrt(head_width)
    cycle_size = lax.axis_size("ctx")
    span_count = 2 * cycle_size
    my_index = lax.axis_index("ctx")
    key_value = jnp.stack([keys, values])
    kv_local = keys.shape[1] // head_width
    q_heads = queries.shape[1] // head_width
    group_size = HEADS // KV_HEADS
    native = key_value.reshape(2, 2, block_rows, kv_local, head_width)
    order_pairs = order.reshape(cycle_size, 2)
    span_low = jnp.min(order_pairs, axis=1)
    low_first = order_pairs[:, 0] < order_pairs[:, 1]
    offsets = jnp.arange(block_rows, dtype=jnp.int32)
    my_low = span_low[my_index]
    my_flag = low_first[my_index]

    def span_positions(low_span):
        return (
            jnp.stack([low_span, span_count - 1 - low_span])[:, None] * block_rows
            + offsets[None, :]
        )

    def sort_kv(blocks, source):
        return jnp.where(low_first[source], blocks, blocks[:, ::-1])

    def store(buffer, blocks, source):
        return lax.dynamic_update_index_in_dim(buffer, blocks, source, 0)

    q_blocks = queries.reshape(2, block_rows, kv_local, group_size, head_width)
    g_blocks = out_grad.reshape(2, block_rows, kv_local, group_size, head_width)
    q_sorted = jnp.where(my_flag, q_blocks, q_blocks[::-1])
    g_sorted = jnp.where(my_flag, g_blocks, g_blocks[::-1])
    q_pos = span_positions(my_low)

    def forward_step(carry_state, kv_sorted, source):
        src_low = span_low[source]
        k_pos = span_positions(src_low)

        def forward_own_case(state_in):
            return attend(state_in, q_sorted, q_pos, kv_sorted[0], kv_sorted[1], k_pos, score_scale)

        def forward_early_case(state_in):
            return attend(
                state_in,
                q_sorted,
                q_pos,
                kv_sorted[0, :1],
                kv_sorted[1, :1],
                k_pos[:1],
                score_scale,
            )

        def forward_late_case(state_in):
            upper_state = attend(
                tuple((member[1:] for member in state_in)),
                q_sorted[1:],
                q_pos[1:],
                kv_sorted[0],
                kv_sorted[1],
                k_pos,
                score_scale,
            )
            return tuple(
                (
                    jnp.concatenate([member[:1], fresh_member], 0)
                    for member, fresh_member in zip(state_in, upper_state)
                )
            )

        branch = jnp.where(source == my_index, 0, jnp.where(src_low < my_low, 1, 2))
        return lax.switch(
            branch, (forward_own_case, forward_early_case, forward_late_case), carry_state
        )

    state_shape = (2, kv_local, group_size, block_rows)
    start_state = (
        jnp.full(state_shape, NEG, jnp.float32),
        jnp.zeros(state_shape, jnp.float32),
        jnp.zeros(state_shape + (head_width,), jnp.float32),
    )
    own_kv = sort_kv(native, my_index)
    kept_blocks = store(jnp.zeros((cycle_size,) + own_kv.shape, jnp.bfloat16), own_kv, my_index)
    fwd_state = forward_step(start_state, own_kv, my_index)

    def cycle_turn(turn_index, loop_carry):
        held, stored, state_now = loop_carry
        held = shifted(held, "ctx", 1)
        source = (my_index - turn_index) % cycle_size
        kv_sorted = sort_kv(held, source)
        return (held, store(stored, kv_sorted, source), forward_step(state_now, kv_sorted, source))

    held_last, kept_blocks, fwd_state = lax.fori_loop(
        1, cycle_size, cycle_turn, (native, kept_blocks, fwd_state)
    )
    row_top, row_total, weighted = fwd_state
    attention_sorted = (weighted / row_total[..., None]).astype(jnp.bfloat16)
    log_total = row_top + jnp.log(row_total)
    grad_heads = g_sorted.transpose(0, 2, 3, 1, 4)
    row_dot = jnp.sum(grad_heads.astype(jnp.float32) * attention_sorted.astype(jnp.float32), axis=4)
    attention_rows = attention_sorted.transpose(0, 3, 1, 2, 4)
    attention_out = jnp.where(my_flag, attention_rows, attention_rows[::-1]).reshape(
        row_count, q_heads * head_width
    )

    def backward_pieces(source):
        kv_sorted = lax.dynamic_index_in_dim(kept_blocks, source, 0, keepdims=False)
        src_low = span_low[source]
        k_pos = span_positions(src_low)

        def backward_own_case():
            return attend_back(
                q_sorted,
                g_sorted,
                log_total,
                row_dot,
                q_pos,
                kv_sorted[0],
                kv_sorted[1],
                k_pos,
                score_scale,
            )

        def backward_early_case():
            query_part, kv_part = attend_back(
                q_sorted,
                g_sorted,
                log_total,
                row_dot,
                q_pos,
                kv_sorted[0, :1],
                kv_sorted[1, :1],
                k_pos[:1],
                score_scale,
            )
            return (query_part, jnp.concatenate([kv_part, jnp.zeros_like(kv_part)], 1))

        def backward_late_case():
            query_part, kv_part = attend_back(
                q_sorted[1:],
                g_sorted[1:],
                log_total[1:],
                row_dot[1:],
                q_pos[1:],
                kv_sorted[0],
                kv_sorted[1],
                k_pos,
                score_scale,
            )
            return (jnp.concatenate([jnp.zeros_like(query_part), query_part], 0), kv_part)

        branch = jnp.where(source == my_index, 0, jnp.where(src_low < my_low, 1, 2))
        return lax.switch(branch, (backward_own_case, backward_early_case, backward_late_case))

    zero_grads = jnp.zeros((2, 2, block_rows, kv_local, head_width), jnp.float32)
    zero_query = jnp.zeros(q_sorted.shape, jnp.float32)

    def grads_turn(turn_index, loop_carry):
        moving, query_sum = loop_carry
        source = (my_index - turn_index) % cycle_size
        query_part, kv_part = backward_pieces(source)
        moving = shifted(moving + kv_part, "ctx", 1)
        return (moving, query_sum + query_part)

    key_grads, query_grads = lax.fori_loop(0, cycle_size, grads_turn, (zero_grads, zero_query))
    key_grads = jnp.where(my_flag, key_grads, key_grads[:, ::-1]).reshape(
        2, row_count, kv_local * head_width
    )
    grad_keys = (score_scale * key_grads[0]).astype(jnp.bfloat16)
    grad_values = key_grads[1].astype(jnp.bfloat16)
    query_rows = jnp.where(my_flag, query_grads, query_grads[::-1]).reshape(
        row_count, q_heads * head_width
    )
    grad_queries = (score_scale * query_rows).astype(jnp.bfloat16)
    return (attention_out, grad_queries, grad_keys, grad_values)


def solution(mesh):
    return jax.shard_map(
        on_device,
        mesh=mesh,
        in_specs=(P("ctx", "head"), P("ctx", "head"), P("ctx", "head"), P("ctx", "head"), P()),
        out_specs=(P("ctx", "head"), P("ctx", "head"), P("ctx", "head"), P("ctx", "head")),
        check_vma=False,
    )
```

profile of v0, /device:TPU:6, one launch (start us, length us, event | category | flops | bytes accessed | tf_op | source)
XLA Modules:
  0.0 1092.8 jit_solution(5961479573004555817)
XLA Ops:
  11.2 494.1 %while.42 = (s32[]{:T(128)}, bf16[2,2,80,1,128]{4,2,1,3,0:T(8,128)(2,1)S(1)}, bf16[32,2,2,80,1,128]{5,3,2,1,4,0:T(8,128)(2,1)}, f32[2,1,4,80]{3,2,1,0:T(4,128)S(...) while((s32[]{:T(128)}, ...), condition=%wide.region_22.23_spmd.clone, body=%wide.region_6.22_spmd.clone.sunk | while | flops 53932504 | bytes 3990638 | solution.py:166
  18.9 10.5 collective-permute-done
  506.8 581.8 %while.43 = (s32[]{:T(128)}, f32[2,2,80,1,128]{4,2,1,3,0:T(8,128)S(1)}, f32[2,80,1,4,128]{4,1,3,0,2:T(8,128)S(1)}, s32[]{:T(128)}, s32[32]{0:T(128)S(1)}, /*inde...) while((s32[]{:T(128)}, ...), condition=%wide.region_28.29_spmd.clone, body=%wide.region_24.28_spmd.clone.sunk | while | flops 132162904 | bytes 7491634 | solution.py:238
  514.8 10.2 collective-permute-done.1
  532.7 10.8 collective-permute-done.1
  551.2 10.6 collective-permute-done.1
  569.5 10.6 collective-permute-done.1
  587.8 11.4 %collective-permute-done.1 = f32[2,2,80,1,128]{4,2,1,3,0:T(8,128)S(1)} collective-permute-done((f32[2,2,80,1,128]{4,2,1,3,0:T(8,128)S(1)}, f32[2,2,80,1,128]{4,2,1,3,0:T(8,128)S(1)}, u32[]{:S(2)}, u32[]{:S(2)}) %collective-permute-start.1) | collective-permute-done | bytes 163872 | tf_op jit(solution)/shard_map/while/body/eval_jaxpr/ppermute | solution.py:18
  606.8 11.2 %collective-permute-done.1 = f32[2,2,80,1,128]{4,2,1,3,0:T(8,128)S(1)} collective-permute-done((f32[2,2,80,1,128]{4,2,1,3,0:T(8,128)S(1)}, f32[2,2,80,1,128]{4,2,1,3,0:T(8,128)S(1)}, u32[]{:S(2)}, u32[]{:S(2)}) %collective-permute-start.1) | collective-permute-done | bytes 163872 | tf_op jit(solution)/shard_map/while/body/eval_jaxpr/ppermute | solution.py:18
  625.7 10.5 collective-permute-done.1
  712.6 10.4 collective-permute-done.1
  730.6 10.6 collective-permute-done.1
  748.9 10.4 collective-permute-done.1
  766.9 11.1 %collective-permute-done.1 = f32[2,2,80,1,128]{4,2,1,3,0:T(8,128)S(1)} collective-permute-done((f32[2,2,80,1,128]{4,2,1,3,0:T(8,128)S(1)}, f32[2,2,80,1,128]{4,2,1,3,0:T(8,128)S(1)}, u32[]{:S(2)}, u32[]{:S(2)}) %collective-permute-start.1) | collective-permute-done | bytes 163872 | tf_op jit(solution)/shard_map/while/body/eval_jaxpr/ppermute | solution.py:18
  785.7 10.9 collective-permute-done.1
  804.3 10.7 collective-permute-done.1
  822.6 10.6 collective-permute-done.1
  840.9 10.7 collective-permute-done.1
  859.3 10.8 collective-permute-done.1
  877.8 10.9 %collective-permute-done.1 = f32[2,2,80,1,128]{4,2,1,3,0:T(8,128)S(1)} collective-permute-done((f32[2,2,80,1,128]{4,2,1,3,0:T(8,128)S(1)}, f32[2,2,80,1,128]{4,2,1,3,0:T(8,128)S(1)}, u32[]{:S(2)}, u32[]{:S(2)}) %collective-permute-start.1) | collective-permute-done | bytes 163872 | tf_op jit(solution)/shard_map/while/body/eval_jaxpr/ppermute | solution.py:18
  896.4 11.3 %collective-permute-done.1 = f32[2,2,80,1,128]{4,2,1,3,0:T(8,128)S(1)} collective-permute-done((f32[2,2,80,1,128]{4,2,1,3,0:T(8,128)S(1)}, f32[2,2,80,1,128]{4,2,1,3,0:T(8,128)S(1)}, u32[]{:S(2)}, u32[]{:S(2)}) %collective-permute-start.1) | collective-permute-done | bytes 163872 | tf_op jit(solution)/shard_map/while/body/eval_jaxpr/ppermute | solution.py:18
  915.4 11.9 %collective-permute-done.1 = f32[2,2,80,1,128]{4,2,1,3,0:T(8,128)S(1)} collective-permute-done((f32[2,2,80,1,128]{4,2,1,3,0:T(8,128)S(1)}, f32[2,2,80,1,128]{4,2,1,3,0:T(8,128)S(1)}, u32[]{:S(2)}, u32[]{:S(2)}) %collective-permute-start.1) | collective-permute-done | bytes 163872 | tf_op jit(solution)/shard_map/while/body/eval_jaxpr/ppermute | solution.py:18
  934.9 13.1 %collective-permute-done.1 = f32[2,2,80,1,128]{4,2,1,3,0:T(8,128)S(1)} collective-permute-done((f32[2,2,80,1,128]{4,2,1,3,0:T(8,128)S(1)}, f32[2,2,80,1,128]{4,2,1,3,0:T(8,128)S(1)}, u32[]{:S(2)}, u32[]{:S(2)}) %collective-permute-start.1) | collective-permute-done | bytes 163872 | tf_op jit(solution)/shard_map/while/body/eval_jaxpr/ppermute | solution.py:18
  955.7 12.8 %collective-permute-done.1 = f32[2,2,80,1,128]{4,2,1,3,0:T(8,128)S(1)} collective-permute-done((f32[2,2,80,1,128]{4,2,1,3,0:T(8,128)S(1)}, f32[2,2,80,1,128]{4,2,1,3,0:T(8,128)S(1)}, u32[]{:S(2)}, u32[]{:S(2)}) %collective-permute-start.1) | collective-permute-done | bytes 163872 | tf_op jit(solution)/shard_map/while/body/eval_jaxpr/ppermute | solution.py:18
  (1198 shorter events, 843.7 us)
Async XLA Ops:
  11.2 18.2 %collective-permute-start = (bf16[2,2,80,1,128]{4,2,1,3,0:T(8,128)(2,1)S(1)}, bf16[2,2,80,1,128]{4,2,1,3,0:T(8,128)(2,1)S(1)}, u32[]{:S(2)}, u32[]{:S(2)}) collective-permute-start(bf16[2,2,80,1,128]{4,2,1,3,0:T(8,128)(2,1)S(1)} %get-tuple-element.1362), channel_id=1, source_target_pairs={{0,16},{16,32},{32,48},{48,64},{64,80},{80,96},{96,112},{112,128},... | collective-permute-start | bytes 245768 | tf_op jit(solution)/shard_map/while/body/eval_jaxpr/ppermute | solution.py:18
  206.7 12.3 %collective-permute-start = (bf16[2,2,80,1,128]{4,2,1,3,0:T(8,128)(2,1)S(1)}, bf16[2,2,80,1,128]{4,2,1,3,0:T(8,128)(2,1)S(1)}, u32[]{:S(2)}, u32[]{:S(2)}) collective-permute-start(bf16[2,2,80,1,128]{4,2,1,3,0:T(8,128)(2,1)S(1)} %get-tuple-element.1362), channel_id=1, source_target_pairs={{0,16},{16,32},{32,48},{48,64},{64,80},{80,96},{96,112},{112,128},... | collective-permute-start | bytes 245768 | tf_op jit(solution)/shard_map/while/body/eval_jaxpr/ppermute | solution.py:18
  223.9 12.3 %collective-permute-start = (bf16[2,2,80,1,128]{4,2,1,3,0:T(8,128)(2,1)S(1)}, bf16[2,2,80,1,128]{4,2,1,3,0:T(8,128)(2,1)S(1)}, u32[]{:S(2)}, u32[]{:S(2)}) collective-permute-start(bf16[2,2,80,1,128]{4,2,1,3,0:T(8,128)(2,1)S(1)} %get-tuple-element.1362), channel_id=1, source_target_pairs={{0,16},{16,32},{32,48},{48,64},{64,80},{80,96},{96,112},{112,128},... | collective-permute-start | bytes 245768 | tf_op jit(solution)/shard_map/while/body/eval_jaxpr/ppermute | solution.py:18
  512.8 12.2 %collective-permute-start.1 = (f32[2,2,80,1,128]{4,2,1,3,0:T(8,128)S(1)}, f32[2,2,80,1,128]{4,2,1,3,0:T(8,128)S(1)}, u32[]{:S(2)}, u32[]{:S(2)}) collective-permute-start(f32[2,2,80,1,128]{4,2,1,3,0:T(8,128)S(1)} %add.394), channel_id=1, source_target_pairs={{0,16},{16,32},{32,48},{48,64},{64,80},{80,96},{96,112},{112,128},... | collective-permute-start | bytes 491528 | tf_op jit(solution)/shard_map/while/body/eval_jaxpr/ppermute | solution.py:18
  530.7 12.9 %collective-permute-start.1 = (f32[2,2,80,1,128]{4,2,1,3,0:T(8,128)S(1)}, f32[2,2,80,1,128]{4,2,1,3,0:T(8,128)S(1)}, u32[]{:S(2)}, u32[]{:S(2)}) collective-permute-start(f32[2,2,80,1,128]{4,2,1,3,0:T(8,128)S(1)} %add.394), channel_id=1, source_target_pairs={{0,16},{16,32},{32,48},{48,64},{64,80},{80,96},{96,112},{112,128},... | collective-permute-start | bytes 491528 | tf_op jit(solution)/shard_map/while/body/eval_jaxpr/ppermute | solution.py:18
  549.2 12.6 %collective-permute-start.1 = (f32[2,2,80,1,128]{4,2,1,3,0:T(8,128)S(1)}, f32[2,2,80,1,128]{4,2,1,3,0:T(8,128)S(1)}, u32[]{:S(2)}, u32[]{:S(2)}) collective-permute-start(f32[2,2,80,1,128]{4,2,1,3,0:T(8,128)S(1)} %add.394), channel_id=1, source_target_pairs={{0,16},{16,32},{32,48},{48,64},{64,80},{80,96},{96,112},{112,128},... | collective-permute-start | bytes 491528 | tf_op jit(solution)/shard_map/while/body/eval_jaxpr/ppermute | solution.py:18
  567.4 12.6 %collective-permute-start.1 = (f32[2,2,80,1,128]{4,2,1,3,0:T(8,128)S(1)}, f32[2,2,80,1,128]{4,2,1,3,0:T(8,128)S(1)}, u32[]{:S(2)}, u32[]{:S(2)}) collective-permute-start(f32[2,2,80,1,128]{4,2,1,3,0:T(8,128)S(1)} %add.394), channel_id=1, source_target_pairs={{0,16},{16,32},{32,48},{48,64},{64,80},{80,96},{96,112},{112,128},... | collective-permute-start | bytes 491528 | tf_op jit(solution)/shard_map/while/body/eval_jaxpr/ppermute | solution.py:18
  585.7 13.4 %collective-permute-start.1 = (f32[2,2,80,1,128]{4,2,1,3,0:T(8,128)S(1)}, f32[2,2,80,1,128]{4,2,1,3,0:T(8,128)S(1)}, u32[]{:S(2)}, u32[]{:S(2)}) collective-permute-start(f32[2,2,80,1,128]{4,2,1,3,0:T(8,128)S(1)} %add.394), channel_id=1, source_target_pairs={{0,16},{16,32},{32,48},{48,64},{64,80},{80,96},{96,112},{112,128},... | collective-permute-start | bytes 491528 | tf_op jit(solution)/shard_map/while/body/eval_jaxpr/ppermute | solution.py:18
  604.8 13.3 %collective-permute-start.1 = (f32[2,2,80,1,128]{4,2,1,3,0:T(8,128)S(1)}, f32[2,2,80,1,128]{4,2,1,3,0:T(8,128)S(1)}, u32[]{:S(2)}, u32[]{:S(2)}) collective-permute-start(f32[2,2,80,1,128]{4,2,1,3,0:T(8,128)S(1)} %add.394), channel_id=1, source_target_pairs={{0,16},{16,32},{32,48},{48,64},{64,80},{80,96},{96,112},{112,128},... | collective-permute-start | bytes 491528 | tf_op jit(solution)/shard_map/while/body/eval_jaxpr/ppermute | solution.py:18
  623.7 12.6 %collective-permute-start.1 = (f32[2,2,80,1,128]{4,2,1,3,0:T(8,128)S(1)}, f32[2,2,80,1,128]{4,2,1,3,0:T(8,128)S(1)}, u32[]{:S(2)}, u32[]{:S(2)}) collective-permute-start(f32[2,2,80,1,128]{4,2,1,3,0:T(8,128)S(1)} %add.394), channel_id=1, source_target_pairs={{0,16},{16,32},{32,48},{48,64},{64,80},{80,96},{96,112},{112,128},... | collective-permute-start | bytes 491528 | tf_op jit(solution)/shard_map/while/body/eval_jaxpr/ppermute | solution.py:18
  710.5 12.4 %collective-permute-start.1 = (f32[2,2,80,1,128]{4,2,1,3,0:T(8,128)S(1)}, f32[2,2,80,1,128]{4,2,1,3,0:T(8,128)S(1)}, u32[]{:S(2)}, u32[]{:S(2)}) collective-permute-start(f32[2,2,80,1,128]{4,2,1,3,0:T(8,128)S(1)} %add.394), channel_id=1, source_target_pairs={{0,16},{16,32},{32,48},{48,64},{64,80},{80,96},{96,112},{112,128},... | collective-permute-start | bytes 491528 | tf_op jit(solution)/shard_map/while/body/eval_jaxpr/ppermute | solution.py:18
  728.6 12.6 %collective-permute-start.1 = (f32[2,2,80,1,128]{4,2,1,3,0:T(8,128)S(1)}, f32[2,2,80,1,128]{4,2,1,3,0:T(8,128)S(1)}, u32[]{:S(2)}, u32[]{:S(2)}) collective-permute-start(f32[2,2,80,1,128]{4,2,1,3,0:T(8,128)S(1)} %add.394), channel_id=1, source_target_pairs={{0,16},{16,32},{32,48},{48,64},{64,80},{80,96},{96,112},{112,128},... | collective-permute-start | bytes 491528 | tf_op jit(solution)/shard_map/while/body/eval_jaxpr/ppermute | solution.py:18
  746.9 12.4 %collective-permute-start.1 = (f32[2,2,80,1,128]{4,2,1,3,0:T(8,128)S(1)}, f32[2,2,80,1,128]{4,2,1,3,0:T(8,128)S(1)}, u32[]{:S(2)}, u32[]{:S(2)}) collective-permute-start(f32[2,2,80,1,128]{4,2,1,3,0:T(8,128)S(1)} %add.394), channel_id=1, source_target_pairs={{0,16},{16,32},{32,48},{48,64},{64,80},{80,96},{96,112},{112,128},... | collective-permute-start | bytes 491528 | tf_op jit(solution)/shard_map/while/body/eval_jaxpr/ppermute | solution.py:18
  764.9 13.1 %collective-permute-start.1 = (f32[2,2,80,1,128]{4,2,1,3,0:T(8,128)S(1)}, f32[2,2,80,1,128]{4,2,1,3,0:T(8,128)S(1)}, u32[]{:S(2)}, u32[]{:S(2)}) collective-permute-start(f32[2,2,80,1,128]{4,2,1,3,0:T(8,128)S(1)} %add.394), channel_id=1, source_target_pairs={{0,16},{16,32},{32,48},{48,64},{64,80},{80,96},{96,112},{112,128},... | collective-permute-start | bytes 491528 | tf_op jit(solution)/shard_map/while/body/eval_jaxpr/ppermute | solution.py:18
  783.7 12.9 %collective-permute-start.1 = (f32[2,2,80,1,128]{4,2,1,3,0:T(8,128)S(1)}, f32[2,2,80,1,128]{4,2,1,3,0:T(8,128)S(1)}, u32[]{:S(2)}, u32[]{:S(2)}) collective-permute-start(f32[2,2,80,1,128]{4,2,1,3,0:T(8,128)S(1)} %add.394), channel_id=1, source_target_pairs={{0,16},{16,32},{32,48},{48,64},{64,80},{80,96},{96,112},{112,128},... | collective-permute-start | bytes 491528 | tf_op jit(solution)/shard_map/while/body/eval_jaxpr/ppermute | solution.py:18
  802.2 12.7 %collective-permute-start.1 = (f32[2,2,80,1,128]{4,2,1,3,0:T(8,128)S(1)}, f32[2,2,80,1,128]{4,2,1,3,0:T(8,128)S(1)}, u32[]{:S(2)}, u32[]{:S(2)}) collective-permute-start(f32[2,2,80,1,128]{4,2,1,3,0:T(8,128)S(1)} %add.394), channel_id=1, source_target_pairs={{0,16},{16,32},{32,48},{48,64},{64,80},{80,96},{96,112},{112,128},... | collective-permute-start | bytes 491528 | tf_op jit(solution)/shard_map/while/body/eval_jaxpr/ppermute | solution.py:18
  820.6 12.6 %collective-permute-start.1 = (f32[2,2,80,1,128]{4,2,1,3,0:T(8,128)S(1)}, f32[2,2,80,1,128]{4,2,1,3,0:T(8,128)S(1)}, u32[]{:S(2)}, u32[]{:S(2)}) collective-permute-start(f32[2,2,80,1,128]{4,2,1,3,0:T(8,128)S(1)} %add.394), channel_id=1, source_target_pairs={{0,16},{16,32},{32,48},{48,64},{64,80},{80,96},{96,112},{112,128},... | collective-permute-start | bytes 491528 | tf_op jit(solution)/shard_map/while/body/eval_jaxpr/ppermute | solution.py:18
  838.9 12.7 %collective-permute-start.1 = (f32[2,2,80,1,128]{4,2,1,3,0:T(8,128)S(1)}, f32[2,2,80,1,128]{4,2,1,3,0:T(8,128)S(1)}, u32[]{:S(2)}, u32[]{:S(2)}) collective-permute-start(f32[2,2,80,1,128]{4,2,1,3,0:T(8,128)S(1)} %add.394), channel_id=1, source_target_pairs={{0,16},{16,32},{32,48},{48,64},{64,80},{80,96},{96,112},{112,128},... | collective-permute-start | bytes 491528 | tf_op jit(solution)/shard_map/while/body/eval_jaxpr/ppermute | solution.py:18
  857.3 12.9 %collective-permute-start.1 = (f32[2,2,80,1,128]{4,2,1,3,0:T(8,128)S(1)}, f32[2,2,80,1,128]{4,2,1,3,0:T(8,128)S(1)}, u32[]{:S(2)}, u32[]{:S(2)}) collective-permute-start(f32[2,2,80,1,128]{4,2,1,3,0:T(8,128)S(1)} %add.394), channel_id=1, source_target_pairs={{0,16},{16,32},{32,48},{48,64},{64,80},{80,96},{96,112},{112,128},... | collective-permute-start | bytes 491528 | tf_op jit(solution)/shard_map/while/body/eval_jaxpr/ppermute | solution.py:18
  875.8 13.0 %collective-permute-start.1 = (f32[2,2,80,1,128]{4,2,1,3,0:T(8,128)S(1)}, f32[2,2,80,1,128]{4,2,1,3,0:T(8,128)S(1)}, u32[]{:S(2)}, u32[]{:S(2)}) collective-permute-start(f32[2,2,80,1,128]{4,2,1,3,0:T(8,128)S(1)} %add.394), channel_id=1, source_target_pairs={{0,16},{16,32},{32,48},{48,64},{64,80},{80,96},{96,112},{112,128},... | collective-permute-start | bytes 491528 | tf_op jit(solution)/shard_map/while/body/eval_jaxpr/ppermute | solution.py:18
  894.4 13.3 %collective-permute-start.1 = (f32[2,2,80,1,128]{4,2,1,3,0:T(8,128)S(1)}, f32[2,2,80,1,128]{4,2,1,3,0:T(8,128)S(1)}, u32[]{:S(2)}, u32[]{:S(2)}) collective-permute-start(f32[2,2,80,1,128]{4,2,1,3,0:T(8,128)S(1)} %add.394), channel_id=1, source_target_pairs={{0,16},{16,32},{32,48},{48,64},{64,80},{80,96},{96,112},{112,128},... | collective-permute-start | bytes 491528 | tf_op jit(solution)/shard_map/while/body/eval_jaxpr/ppermute | solution.py:18
  913.3 13.9 %collective-permute-start.1 = (f32[2,2,80,1,128]{4,2,1,3,0:T(8,128)S(1)}, f32[2,2,80,1,128]{4,2,1,3,0:T(8,128)S(1)}, u32[]{:S(2)}, u32[]{:S(2)}) collective-permute-start(f32[2,2,80,1,128]{4,2,1,3,0:T(8,128)S(1)} %add.394), channel_id=1, source_target_pairs={{0,16},{16,32},{32,48},{48,64},{64,80},{80,96},{96,112},{112,128},... | collective-permute-start | bytes 491528 | tf_op jit(solution)/shard_map/while/body/eval_jaxpr/ppermute | solution.py:18
  932.9 15.1 %collective-permute-start.1 = (f32[2,2,80,1,128]{4,2,1,3,0:T(8,128)S(1)}, f32[2,2,80,1,128]{4,2,1,3,0:T(8,128)S(1)}, u32[]{:S(2)}, u32[]{:S(2)}) collective-permute-start(f32[2,2,80,1,128]{4,2,1,3,0:T(8,128)S(1)} %add.394), channel_id=1, source_target_pairs={{0,16},{16,32},{32,48},{48,64},{64,80},{80,96},{96,112},{112,128},... | collective-permute-start | bytes 491528 | tf_op jit(solution)/shard_map/while/body/eval_jaxpr/ppermute | solution.py:18
  953.7 14.8 %collective-permute-start.1 = (f32[2,2,80,1,128]{4,2,1,3,0:T(8,128)S(1)}, f32[2,2,80,1,128]{4,2,1,3,0:T(8,128)S(1)}, u32[]{:S(2)}, u32[]{:S(2)}) collective-permute-start(f32[2,2,80,1,128]{4,2,1,3,0:T(8,128)S(1)} %add.394), channel_id=1, source_target_pairs={{0,16},{16,32},{32,48},{48,64},{64,80},{80,96},{96,112},{112,128},... | collective-permute-start | bytes 491528 | tf_op jit(solution)/shard_map/while/body/eval_jaxpr/ppermute | solution.py:18
  (41 other events, 940.6 us)
where the time goes:
time: 1100 us; the launch traced here: 1090 us
  waiting for transfers between devices  503 us (46%)
  other arithmetic  164 us (15%)
  loops' own time  128 us (12%)
  starting transfers between devices  122 us (11%)
  local copies, waits for them, and re-layouts  113 us (10%)
  matrix products  60.2 us (5%)
    ppermute x63, waiting for transfers between devices, shifted(): lax.ppermute(array, axis, [(i, (i + by) % length) for i in range(length)])  503 us
    ppermute x63, starting transfers between devices, shifted(): lax.ppermute(array, axis, [(i, (i + by) % length) for i in range(length)])  122 us
    another operation x1, loops' own time, on_device(): lax.fori_loop(0, cycle_size, grads_turn, (zero_grads, zero_query))  64 us
    another operation x1, loops' own time, on_device(): lax.fori_loop(1, cycle_size, cycle_turn, (native, kept_blocks, fwd_state))  61.4 us
    mul x64, other arithmetic, span_positions(): jnp.stack([low_span, span_count - 1 - low_span])[:, None] * block_rows  45.7 us
    dynamic_update_slice x32, other arithmetic, store(): return lax.dynamic_update_index_in_dim(buffer, blocks, source, 0)  41.5 us
    squeeze x32, local copies, waits for them, and re-layouts, backward_pieces(): kv_sorted = lax.dynamic_index_in_dim(kept_blocks, source, 0, keepdims=False)  28.6 us
  transfers between devices with their start and end apart: 63, of which 63 were waited for; matrix products, arithmetic and copies ran while one was open for 6% of the time, Pallas kernels for 0%

commit v1 on v0

v1 whole, which is shorter than its diff:
```python
import math

import jax
import jax.numpy as jnp
from jax import lax
from jax.experimental import pallas as pl
from jax.experimental.pallas import tpu as pltpu
from jax.sharding import PartitionSpec as P

HEADS = 32
KV_HEADS = 8
HEAD_DIM = 128
SPAN = 80
KEY_BLOCK = 512

NEG = -1e30


def attention_kernel(
    limits_ref, q_ref, g_ref, kv_ref, qpos_ref,
    out_ref, dq_ref, dkv_ref,
    top_ref, total_ref, acc_ref, lse_ref, dot_ref, dqacc_ref,
):
    rows = q_ref.shape[0]
    half = rows // 2
    width = HEAD_DIM
    scale = 1.0 / math.sqrt(width)
    early_blocks = limits_ref[0]
    late_blocks = limits_ref[1]

    top_ref[...] = jnp.full(top_ref.shape, NEG, jnp.float32)
    total_ref[...] = jnp.zeros(total_ref.shape, jnp.float32)
    acc_ref[...] = jnp.zeros(acc_ref.shape, jnp.float32)

    def scores_of(lo, count, start):
        q = q_ref[lo:lo + count, :]
        k = kv_ref[pl.ds(start, KEY_BLOCK), 0:width]
        s = lax.dot_general(q, k, (((1,), (1,)), ((), ())), preferred_element_type=jnp.float32) * scale
        kpos = start + lax.broadcasted_iota(jnp.int32, (1, KEY_BLOCK), 1)
        visible = kpos <= qpos_ref[lo:lo + count, :]
        return s, visible

    def forward_block(lo, count, block):
        start = pl.multiple_of(block * KEY_BLOCK, KEY_BLOCK)
        s, visible = scores_of(lo, count, start)
        s = jnp.where(visible, s, NEG)
        old_top = top_ref[lo:lo + count, :]
        new_top = jnp.maximum(old_top, jnp.max(s, axis=1, keepdims=True))
        p = jnp.where(visible, jnp.exp(s - new_top), 0.0)
        rescale = jnp.exp(old_top - new_top)
        total_ref[lo:lo + count, :] = total_ref[lo:lo + count, :] * rescale + jnp.sum(p, axis=1, keepdims=True)
        v = kv_ref[pl.ds(start, KEY_BLOCK), width:2 * width]
        pv = jnp.dot(p.astype(jnp.bfloat16), v, preferred_element_type=jnp.float32)
        acc_ref[lo:lo + count, :] = acc_ref[lo:lo + count, :] * rescale + pv
        top_ref[lo:lo + count, :] = new_top

    def fwd_both(block, carry):
        forward_block(0, rows, block)
        return carry

    def fwd_late(block, carry):
        forward_block(half, half, block)
        return carry

    lax.fori_loop(0, early_blocks, fwd_both, 0)
    lax.fori_loop(early_blocks, late_blocks, fwd_late, 0)

    attention = (acc_ref[...] / total_ref[...]).astype(jnp.bfloat16)
    out_ref[...] = attention
    lse_ref[...] = top_ref[...] + jnp.log(total_ref[...])
    dot_ref[...] = jnp.sum(
        g_ref[...].astype(jnp.float32) * attention.astype(jnp.float32), axis=1, keepdims=True
    )
    dqacc_ref[...] = jnp.zeros(dqacc_ref.shape, jnp.float32)
    dkv_ref[...] = jnp.zeros(dkv_ref.shape, jnp.float32)

    def backward_block(lo, count, block):
        start = pl.multiple_of(block * KEY_BLOCK, KEY_BLOCK)
        s, visible = scores_of(lo, count, start)
        probs = jnp.where(visible, jnp.exp(s - lse_ref[lo:lo + count, :]), 0.0)
        g = g_ref[lo:lo + count, :]
        k = kv_ref[pl.ds(start, KEY_BLOCK), 0:width]
        v = kv_ref[pl.ds(start, KEY_BLOCK), width:2 * width]
        grad_probs = lax.dot_general(g, v, (((1,), (1,)), ((), ())), preferred_element_type=jnp.float32)
        grad_scores = (probs * (grad_probs - dot_ref[lo:lo + count, :])).astype(jnp.bfloat16)
        dqacc_ref[lo:lo + count, :] += jnp.dot(grad_scores, k, preferred_element_type=jnp.float32)
        q = q_ref[lo:lo + count, :]
        dk = lax.dot_general(grad_scores, q, (((0,), (0,)), ((), ())), preferred_element_type=jnp.float32)
        dv = lax.dot_general(
            probs.astype(jnp.bfloat16), g, (((0,), (0,)), ((), ())), preferred_element_type=jnp.float32
        )
        dkv_ref[pl.ds(start, KEY_BLOCK), 0:width] += dk
        dkv_ref[pl.ds(start, KEY_BLOCK), width:2 * width] += dv

    def bwd_both(block, carry):
        backward_block(0, rows, block)
        return carry

    def bwd_late(block, carry):
        backward_block(half, half, block)
        return carry

    lax.fori_loop(0, early_blocks, bwd_both, 0)
    lax.fori_loop(early_blocks, late_blocks, bwd_late, 0)
    dq_ref[...] = (dqacc_ref[...] * scale).astype(jnp.bfloat16)


def local_attention(limits, q_rows, g_rows, kv_sorted, q_pos):
    rows, width = q_rows.shape
    keys = kv_sorted.shape[0]
    vmem = pltpu.VMEM
    flops = 2 * rows * keys * width * 7 // 2
    return pl.pallas_call(
        attention_kernel,
        out_shape=(
            jax.ShapeDtypeStruct((rows, width), jnp.bfloat16),
            jax.ShapeDtypeStruct((rows, width), jnp.bfloat16),
            jax.ShapeDtypeStruct((keys, 2 * width), jnp.float32),
        ),
        in_specs=[
            pl.BlockSpec(memory_space=pltpu.SMEM),
            pl.BlockSpec(memory_space=vmem),
            pl.BlockSpec(memory_space=vmem),
            pl.BlockSpec(memory_space=vmem),
            pl.BlockSpec(memory_space=vmem),
        ],
        out_specs=(
            pl.BlockSpec(memory_space=vmem),
            pl.BlockSpec(memory_space=vmem),
            pl.BlockSpec(memory_space=vmem),
        ),
        scratch_shapes=[
            pltpu.VMEM((rows, 1), jnp.float32),
            pltpu.VMEM((rows, 1), jnp.float32),
            pltpu.VMEM((rows, width), jnp.float32),
            pltpu.VMEM((rows, 1), jnp.float32),
            pltpu.VMEM((rows, 1), jnp.float32),
            pltpu.VMEM((rows, width), jnp.float32),
        ],
        cost_estimate=pl.CostEstimate(
            flops=flops, transcendentals=rows * keys, bytes_accessed=keys * width * 12
        ),
    )(limits, q_rows, g_rows, kv_sorted, q_pos)


def on_device(queries, keys, values, out_grad, order):
    row_count = queries.shape[0]
    width = HEAD_DIM
    score_scale = 1.0 / math.sqrt(width)
    cycle_size = lax.axis_size("ctx")
    span_count = 2 * cycle_size
    my_index = lax.axis_index("ctx")
    q_heads = queries.shape[1] // width

    kv_local = jnp.concatenate([keys, values], axis=1)
    kv_all = lax.all_gather(kv_local, "ctx", axis=0, tiled=True)
    inverse = jnp.zeros((span_count,), jnp.int32).at[order].set(jnp.arange(span_count, dtype=jnp.int32))
    kv_sorted = kv_all.reshape(span_count, SPAN, 2 * width)[inverse].reshape(span_count * SPAN, 2 * width)

    pair = lax.dynamic_slice_in_dim(order, 2 * my_index, 2)
    low_first = pair[0] < pair[1]
    my_low = jnp.minimum(pair[0], pair[1])
    early_keys = (my_low + 1) * SPAN
    late_keys = (span_count - my_low) * SPAN
    limits = jnp.stack(
        [(early_keys + KEY_BLOCK - 1) // KEY_BLOCK, (late_keys + KEY_BLOCK - 1) // KEY_BLOCK]
    ).astype(jnp.int32)

    def to_rows(array):
        blocks = array.reshape(2, SPAN, q_heads, width)
        blocks = jnp.where(low_first, blocks, blocks[::-1])
        return blocks.transpose(0, 2, 1, 3).reshape(2 * q_heads * SPAN, width)

    def from_rows(array):
        blocks = array.reshape(2, q_heads, SPAN, width).transpose(0, 2, 1, 3)
        blocks = jnp.where(low_first, blocks, blocks[::-1])
        return blocks.reshape(row_count, q_heads * width)

    offsets = jnp.arange(SPAN, dtype=jnp.int32)
    span_pos = jnp.stack([my_low, span_count - 1 - my_low])[:, None] * SPAN + offsets[None, :]
    q_pos = jnp.broadcast_to(span_pos[:, None, :], (2, q_heads, SPAN)).reshape(-1, 1)

    attention_rows, dq_rows, dkv_sorted = local_attention(
        limits, to_rows(queries), to_rows(out_grad), kv_sorted, q_pos
    )
    dkv_all = dkv_sorted.reshape(span_count, SPAN, 2 * width)[order].reshape(-1, 2 * width)
    dkv_mine = lax.psum_scatter(dkv_all, "ctx", scatter_dimension=0, tiled=True)
    grad_keys = (score_scale * dkv_mine[:, :width]).astype(jnp.bfloat16)
    grad_values = dkv_mine[:, width:].astype(jnp.bfloat16)
    return (from_rows(attention_rows), from_rows(dq_rows), grad_keys, grad_values)


def solution(mesh):
    return jax.shard_map(
        on_device,
        mesh=mesh,
        in_specs=(P("ctx", "head"), P("ctx", "head"), P("ctx", "head"), P("ctx", "head"), P()),
        out_specs=(P("ctx", "head"), P("ctx", "head"), P("ctx", "head"), P("ctx", "head")),
        check_vma=False,
    )
```

time: 1100 us -> 382 us (0.35)
  waiting for transfers between devices: 503 us -> 319 us
  other arithmetic: 164 us -> 5.85 us
  loops' own time: 128 us -> 0 us
  starting transfers between devices: 122 us -> 0.08 us
  local copies, waits for them, and re-layouts: 113 us -> 18.6 us
  matrix products: 60.2 us -> 0 us
  Pallas kernels: 0 us -> 21.2 us
  between operations: 1.47 us -> 16.8 us
    ppermute x63 -> x0, waiting for transfers between devices: 503 us -> none  [shifted(): lax.ppermute(array, axis, [(i, (i + by) % length) for i in range(length)])]
    reduce_scatter x0 -> x1, waiting for transfers between devices: none -> 232 us  [on_device(): dkv_mine = lax.psum_scatter(dkv_all, 'ctx', scatter_dimension=0, tiled=True)]
    another operation x65 -> x0, loops' own time: 128 us -> none  [the longest x1 64 us: on_device(): lax.fori_loop(0, cycle_size, grads_turn, (zero_grads, zero_query))]
    ppermute x63 -> x0, starting transfers between devices: 122 us -> none  [shifted(): lax.ppermute(array, axis, [(i, (i + by) % length) for i in range(length)])]
    all_gather x0 -> x1, waiting for transfers between devices: none -> 87.7 us  [on_device(): kv_all = lax.all_gather(kv_local, 'ctx', axis=0, tiled=True)]
    dot_general x224 -> x0, matrix products: 60.2 us -> none  [the longest x32 12.1 us: attend(): jnp.einsum('axgcbs,bsxd->axgcbd', block_weights.astype(jnp.bfloat16), v_p...]
    mul x95 -> x1, other arithmetic: 59 us -> 0.08 us  [on_device(): jnp.stack([my_low, span_count - 1 - my_low])[:, None] * SPAN]
    dynamic_slice x96 -> x1, local copies, waits for them, and re-layouts: 58.1 us -> 0.73 us  [on_device(): pair = lax.dynamic_slice_in_dim(order, 2 * my_index, 2)]
  transfers between devices with their start and end apart: 63 -> 2, of which waited for: 63 -> 2; matrix products, arithmetic and copies ran while one was open for 6% -> 2% of each run, Pallas kernels for 0% -> 0%
where the time goes in v1:
time: 382 us
  waiting for transfers between devices  319 us (84%)
  Pallas kernels  21.2 us (6%)
  local copies, waits for them, and re-layouts  18.6 us (5%)
  between operations  16.8 us (4%)
  other arithmetic  5.85 us (2%)
    reduce_scatter x1, waiting for transfers between devices, on_device(): dkv_mine = lax.psum_scatter(dkv_all, 'ctx', scatter_dimension=0, tiled=True)  232 us
    all_gather x1, waiting for transfers between devices, on_device(): kv_all = lax.all_gather(kv_local, 'ctx', axis=0, tiled=True)  87.7 us
    pallas_call x1, Pallas kernels, local_attention(): pl.pallas_call(attention_kernel, out_shape=(jax.ShapeDtypeStruct((rows, w...  21.2 us
  transfers between devices with their start and end apart: 2, of which 2 were waited for; matrix products, arithmetic and copies ran while one was open for 2% of the time, Pallas kernels for 0%

profile of v1, /device:TPU:6, one launch (start us, length us, event | category | flops | bytes accessed | tf_op | source)
XLA Modules:
  0.0 381.8 jit_solution(18044261338420715272)
XLA Ops:
  7.2 1.4 pad_maximum_fusion
  8.7 0.7 dynamic_slice.3
  9.5 0.6 fusion.3
  12.7 1.0 reshape.100
  13.7 1.0 reshape.102
  14.7 0.1 add_multiply_fusion
  14.8 0.1 iota_add_fusion
  14.8 0.9 reshape.140.qpos_ref
  15.7 0.7 compare_select_fusion.1
  16.4 0.8 scatter_custom_fusion
  17.2 0.6 pad_add_fusion.limits_ref
  17.8 0.7 reverse_select_fusion.3
  18.5 0.7 reverse_select_fusion.2
  19.2 87.7 %all-gather.2.cloned.1.call-done = bf16[5120,256]{1,0:T(8,128)(2,1)} async-done(((bf16[160,256]{1,0:T(8,128)(2,1)}), bf16[5120,256]{1,0:T(8,128)(2,1)}) %all-gather.2.cloned.1.call-update) | async-done | bytes 2621456 | tf_op jit(solution)/shard_map/all_gather | solution.py:156
  107.0 3.9 %gather_fusion = bf16[64,80,256]{2,1,0:T(8,128)(2,1)} fusion(bf16[64,80,256]{2,1,0:T(8,128)(2,1)} %bitcast.34, s32[1024]{0:T(1024)S(1)} %pad_clamp_fusion.1), kind=kCustom, calls=%fused_computation | custom fusion | bytes 5243136 | tf_op jit(solution)/shard_map/gather | solution.py:158
  110.9 21.2 %shard_map.84 = (bf16[640,128]{1,0:T(8,128)(2,1)}, bf16[640,128]{1,0:T(8,128)(2,1)}, f32[5120,256]{1,0:T(8,128)}) custom-call(s32[2]{0:T(128)} %pad_add_fusion.limits_ref, bf16[640,128]{1,0:T(8,128)(2,1)} %bitcast.39, bf16[640,128]{1,0:T(8,128)(2,1)} %bitcast.40, bf16[5120,256]{1,0:T(8,128)(2,1)} %bitcast.35, s32[640,1]{1,0:T(8,128)} %reshape.140.qpos_ref), custom_call_target="tpu_custom_call" | custom-call | flops 2936012800 | bytes 7864320 | tf_op jit(solution)/shard_map/pallas_call | solution.py:113
  132.1 5.7 %gather_fusion.1 = f32[64,80,256]{2,1,0:T(8,128)} fusion(f32[64,80,256]{2,1,0:T(8,128)} %bitcast.33, s32[1024]{0:T(1024)S(1)} %pad_clamp_fusion), kind=kCustom, calls=%fused_computation.1 | custom fusion | bytes 10486016 | tf_op jit(solution)/shard_map/gather | solution.py:186
  137.9 0.9 copy-done
  138.8 0.1 copy-done.1
  139.0 0.7 copy.26
  139.7 0.7 copy.27
  140.4 231.5 %reduce-scatter.2.cloned.1.call-done = f32[160,256]{1,0:T(8,128)} async-done(((f32[5120,256]{1,0:T(8,128)}), f32[160,256]{1,0:T(8,128)}) %reduce-scatter.2.cloned.1.call-update) | async-done | bytes 163856 | tf_op jit(solution)/shard_map/reduce_scatter | solution.py:187
  371.9 1.5 slice.29
  373.5 1.5 fusion
  (16 shorter events, 0.4 us)
Async XLA Ops:
  7.2 99.8 %all-gather.2.cloned.1.call-start = ((), (), s32[]{:S(2)}) async-start(), calls=%async_computation.1 | async-start | bytes 2703360 | tf_op jit(solution)/shard_map/all_gather | solution.py:156
  8.7 363.3 %reduce-scatter.2.cloned.1.call-start = ((), (), s32[]{:S(2)}) async-start(), calls=%async_computation.2 | async-start | bytes 5406720 | tf_op jit(solution)/shard_map/reduce_scatter | solution.py:187
  137.8 0.9 copy-start
  137.8 1.0 copy-start.1
Sparse Core Ops, SparseCore 0:
  11.2 95.7 all-gather.1
  138.0 233.9 reduce-scatter.1

commit v2 on v1

--- a/solution.py
+++ b/solution.py
@@ -5,6 +5,7 @@
 from jax import lax
 from jax.experimental import pallas as pl
 from jax.experimental.pallas import tpu as pltpu
+from jax.sharding import Mesh
 from jax.sharding import PartitionSpec as P
 
 HEADS = 32
@@ -14,6 +15,7 @@
 KEY_BLOCK = 512
 
 NEG = -1e30
+CTX = ("zh", "y")
 
 
 def attention_kernel(
@@ -147,13 +149,16 @@
     row_count = queries.shape[0]
     width = HEAD_DIM
     score_scale = 1.0 / math.sqrt(width)
-    cycle_size = lax.axis_size("ctx")
+    cycle_size = lax.axis_size(CTX)
     span_count = 2 * cycle_size
-    my_index = lax.axis_index("ctx")
+    my_index = lax.axis_index(CTX)
     q_heads = queries.shape[1] // width
 
+    outer = lax.axis_size("zh")
+    inner = lax.axis_size("y")
     kv_local = jnp.concatenate([keys, values], axis=1)
-    kv_all = lax.all_gather(kv_local, "ctx", axis=0, tiled=True)
+    kv_all = lax.all_gather(lax.all_gather(kv_local, "zh", axis=0, tiled=True), "y", axis=0, tiled=True)
+    kv_all = kv_all.reshape(inner, outer, 2 * SPAN, 2 * width).transpose(1, 0, 2, 3)
     inverse = jnp.zeros((span_count,), jnp.int32).at[order].set(jnp.arange(span_count, dtype=jnp.int32))
     kv_sorted = kv_all.reshape(span_count, SPAN, 2 * width)[inverse].reshape(span_count * SPAN, 2 * width)
 
@@ -183,18 +188,25 @@
     attention_rows, dq_rows, dkv_sorted = local_attention(
         limits, to_rows(queries), to_rows(out_grad), kv_sorted, q_pos
     )
-    dkv_all = dkv_sorted.reshape(span_count, SPAN, 2 * width)[order].reshape(-1, 2 * width)
-    dkv_mine = lax.psum_scatter(dkv_all, "ctx", scatter_dimension=0, tiled=True)
+    dkv_all = dkv_sorted.reshape(span_count, SPAN, 2 * width)[order].reshape(cycle_size, 2 * SPAN, 2 * width)
+    dkv_parts = lax.all_to_all(dkv_all.astype(jnp.bfloat16), CTX, 0, 0, tiled=False)
+    dkv_mine = jnp.sum(dkv_parts.astype(jnp.float32), axis=0)
     grad_keys = (score_scale * dkv_mine[:, :width]).astype(jnp.bfloat16)
     grad_values = dkv_mine[:, width:].astype(jnp.bfloat16)
     return (from_rows(attention_rows), from_rows(dq_rows), grad_keys, grad_values)
 
 
 def solution(mesh):
+    ctx_size = mesh.shape["ctx"]
+    outer = 4 if ctx_size % 4 == 0 else 1
+    split = Mesh(
+        mesh.devices.reshape(outer, ctx_size // outer, mesh.shape["head"]), ("zh", "y", "head")
+    )
+    rows = P(CTX, "head")
     return jax.shard_map(
         on_device,
-        mesh=mesh,
-        in_specs=(P("ctx", "head"), P("ctx", "head"), P("ctx", "head"), P("ctx", "head"), P()),
-        out_specs=(P("ctx", "head"), P("ctx", "head"), P("ctx", "head"), P("ctx", "head")),
+        mesh=split,
+        in_specs=(rows, rows, rows, rows, P()),
+        out_specs=(rows, rows, rows, rows),
         check_vma=False,
     )

time: 382 us -> 206 us (0.54)
  the two profiles are of different devices: /device:TPU:6 before, /device:TPU:22 now
where the time goes in v2:
time: 206 us; the launch traced here: 205 us
  waiting for transfers between devices  115 us (56%)
  Pallas kernels  22.9 us (11%)
  blocking collectives  20.6 us (10%)
  between operations  16.8 us (8%)
  local copies, waits for them, and re-layouts  16 us (8%)
  starting transfers between devices  10.2 us (5%)
  other arithmetic  4.04 us (2%)
    all_to_all x1, waiting for transfers between devices, on_device(): lax.all_to_all(dkv_all.astype(jnp.bfloat16), CTX, 0, 0, tiled=False)  80.5 us
    all_gather x1, waiting for transfers between devices, on_device(): lax.all_gather(lax.all_gather(kv_local, 'zh', axis=0, tiled=True), 'y', a...  34.3 us
    pallas_call x1, Pallas kernels, local_attention(): pl.pallas_call(attention_kernel, out_shape=(jax.ShapeDtypeStruct((rows, w...  22.9 us
    all_gather x1, blocking collectives, on_device(): lax.all_gather(kv_local, 'zh', axis=0, tiled=True)  20.6 us
    all_to_all x1, starting transfers between devices, on_device(): lax.all_to_all(dkv_all.astype(jnp.bfloat16), CTX, 0, 0, tiled=False)  10.2 us
    gather x1, local copies, waits for them, and re-layouts, on_device(): dkv_sorted.reshape(span_count, SPAN, 2 * width)[order]  4.78 us
  transfers between devices with their start and end apart: 2, of which 2 were waited for; matrix products, arithmetic and copies ran while one was open for 4% of the time, Pallas kernels for 0%

profile of v2, /device:TPU:22, one launch (start us, length us, event | category | flops | bytes accessed | tf_op | source)
XLA Modules:
  0.0 205.4 jit_solution(15036181200649785924)
XLA Ops:
  7.2 0.8 pad_maximum_fusion
  8.0 20.6 %all_gather.6 = bf16[640,256]{1,0:T(8,128)(2,1)} all-gather(bf16[160,256]{1,0:T(8,128)(2,1)S(1)} %pad_maximum_fusion), channel_id=1, replica_groups=mesh['zh'=4,'y'=8,'head'=16] {'zh'}, dimensions={0}, use_global_device_ids=true | all-gather | bytes 409600 | tf_op jit(solution)/shard_map/all_gather | solution.py:160
  28.7 0.7 dynamic_slice.3
  29.4 0.6 fusion.3
  32.6 0.1 add_multiply_fusion
  32.8 0.9 reshape.142.qpos_ref
  33.7 1.0 reshape.102
  34.7 1.0 reshape.104
  35.7 0.8 scatter_custom_fusion
  36.5 0.6 pad_add_fusion.limits_ref
  37.1 0.7 reverse_select_fusion.3
  37.8 0.7 reverse_select_fusion.2
  38.5 34.3 %all-gather.2.cloned.1.call-done = bf16[5120,256]{1,0:T(8,128)(2,1)} async-done(((bf16[640,256]{1,0:T(8,128)(2,1)}), bf16[5120,256]{1,0:T(8,128)(2,1)}) %all-gather.2.cloned.1.call-update) | async-done | bytes 2621456 | tf_op jit(solution)/shard_map/all_gather | solution.py:160
  72.8 1.9 copy.26
  74.8 2.2 %gather_fusion = bf16[64,80,256]{2,1,0:T(8,128)(2,1)} fusion(bf16[64,80,256]{2,1,0:T(8,128)(2,1)S(1)} %bitcast.35, s32[1024]{0:T(1024)S(1)} %pad_clamp_fusion.1), kind=kCustom, calls=%fused_computation | custom fusion | bytes 5243136 | tf_op jit(solution)/shard_map/gather | solution.py:163
  77.0 22.9 %shard_map.84 = (bf16[640,128]{1,0:T(8,128)(2,1)}, bf16[640,128]{1,0:T(8,128)(2,1)}, f32[5120,256]{1,0:T(8,128)}) custom-call(s32[2]{0:T(128)} %pad_add_fusion.limits_ref, bf16[640,128]{1,0:T(8,128)(2,1)} %bitcast.42, bf16[640,128]{1,0:T(8,128)(2,1)} %bitcast.44, bf16[5120,256]{1,0:T(8,128)(2,1)} %bitcast.37, s32[640,1]{1,0:T(8,128)} %reshape.142.qpos_ref), custom_call_target="tpu_custom_call" | custom-call | flops 2936012800 | bytes 7864320 | tf_op jit(solution)/shard_map/pallas_call | solution.py:115
  99.9 4.8 %gather_fusion.1 = bf16[64,80,256]{2,1,0:T(8,128)(2,1)} fusion(f32[64,80,256]{2,1,0:T(8,128)} %bitcast.38, s32[1024]{0:T(1024)S(1)} %pad_clamp_fusion), kind=kCustom, calls=%fused_computation.1 | custom fusion | bytes 5243136 | tf_op jit(solution)/shard_map/gather | solution.py:191
  104.7 10.2 %all-to-all-start = ((bf16[32,160,256]{2,1,0:T(8,128)(2,1)}), bf16[32,160,256]{2,1,0:T(8,128)(2,1)S(1)}, u32[]{:S(2)}, u32[]{:S(2)}) async-start(bf16[32,160,256]{2,1,0:T(8,128)(2,1)} %bitcast.34), calls=%async_computation | async-start | bytes 5242880 | tf_op jit(solution)/shard_map/all_to_all | solution.py:192
  115.0 0.7 copy.34
  115.8 0.7 copy.35
  116.5 80.5 %all-to-all-done = bf16[32,160,256]{2,1,0:T(8,128)(2,1)S(1)} async-done(((bf16[32,160,256]{2,1,0:T(8,128)(2,1)}), bf16[32,160,256]{2,1,0:T(8,128)(2,1)S(1)}, u32[]{:S(2)}, u32[]{:S(2)}) %all-to-all-start) | async-done | bytes 2621472 | tf_op jit(solution)/shard_map/all_to_all | solution.py:192
  197.0 0.4 convert_reduce_fusion
  197.3 0.6 fusion
  197.9 0.6 slice.29
  (20 shorter events, 0.4 us)
Async XLA Ops:
  7.2 28.5 %copy-start.2 = (s32[64]{0:T(128)S(1)}, s32[64]{0:T(128)}, u32[]{:S(2)}) copy-start(s32[64]{0:T(128)} %param.9) | copy-start | bytes 772
  7.2 65.7 %all-gather.2.cloned.1.call-start = ((), (), s32[]{:S(2)}) async-start(), calls=%async_computation.1 | async-start | bytes 2949120 | tf_op jit(solution)/shard_map/all_gather | solution.py:160
  104.7 10.2 %copy-start = (bf16[640,128]{1,0:T(8,128)(2,1)S(1)}, bf16[640,128]{1,0:T(8,128)(2,1)}, u32[]{:S(2)}) copy-start(bf16[640,128]{1,0:T(8,128)(2,1)} %get-tuple-element.7) | copy-start | bytes 491524
  104.7 10.2 %copy-start.1 = (bf16[640,128]{1,0:T(8,128)(2,1)S(1)}, bf16[640,128]{1,0:T(8,128)(2,1)}, u32[]{:S(2)}) copy-start(bf16[640,128]{1,0:T(8,128)(2,1)} %get-tuple-element.8) | copy-start | bytes 491524
  104.7 92.3 %all-to-all-start = ((bf16[32,160,256]{2,1,0:T(8,128)(2,1)}), bf16[32,160,256]{2,1,0:T(8,128)(2,1)S(1)}, u32[]{:S(2)}, u32[]{:S(2)}) async-start(bf16[32,160,256]{2,1,0:T(8,128)(2,1)} %bitcast.34), calls=%async_computation | async-start | bytes 5242880 | tf_op jit(solution)/shard_map/all_to_all | solution.py:192
Sparse Core Ops, SparseCore 0:
  28.8 43.9 all-gather.1

commit v3 on v2

--- a/solution.py
+++ b/solution.py
@@ -188,8 +188,10 @@
     attention_rows, dq_rows, dkv_sorted = local_attention(
         limits, to_rows(queries), to_rows(out_grad), kv_sorted, q_pos
     )
-    dkv_all = dkv_sorted.reshape(span_count, SPAN, 2 * width)[order].reshape(cycle_size, 2 * SPAN, 2 * width)
-    dkv_parts = lax.all_to_all(dkv_all.astype(jnp.bfloat16), CTX, 0, 0, tiled=False)
+    dkv_all = dkv_sorted.reshape(span_count, SPAN, 2 * width)[order].reshape(outer, inner, 2 * SPAN, 2 * width)
+    row_parts = lax.all_to_all(dkv_all.astype(jnp.bfloat16), "y", 1, 1, tiled=False)
+    row_sums = jnp.sum(row_parts.astype(jnp.float32), axis=1)
+    dkv_parts = lax.all_to_all(row_sums.astype(jnp.bfloat16), "zh", 0, 0, tiled=False)
     dkv_mine = jnp.sum(dkv_parts.astype(jnp.float32), axis=0)
     grad_keys = (score_scale * dkv_mine[:, :width]).astype(jnp.bfloat16)
     grad_values = dkv_mine[:, width:].astype(jnp.bfloat16)

time: 206 us -> 194 us (0.942)
  the two profiles are of different devices: /device:TPU:22 before, /device:TPU:6 now
where the time goes in v3:
time: 194 us; the launch traced here: 193 us
  blocking collectives  85.2 us (44%)
  waiting for transfers between devices  43.1 us (22%)
  Pallas kernels  21.3 us (11%)
  between operations  16.8 us (9%)
  local copies, waits for them, and re-layouts  14.7 us (8%)
  starting transfers between devices  6.96 us (4%)
  other arithmetic  4.94 us (3%)
    all_to_all x1, blocking collectives, on_device(): lax.all_to_all(dkv_all.astype(jnp.bfloat16), 'y', 1, 1, tiled=False)  64.6 us
    all_gather x1, waiting for transfers between devices, on_device(): lax.all_gather(lax.all_gather(kv_local, 'zh', axis=0, tiled=True), 'y', a...  35.1 us
    pallas_call x1, Pallas kernels, local_attention(): pl.pallas_call(attention_kernel, out_shape=(jax.ShapeDtypeStruct((rows, w...  21.3 us
    all_gather x1, blocking collectives, on_device(): lax.all_gather(kv_local, 'zh', axis=0, tiled=True)  20.6 us
    all_to_all x1, waiting for transfers between devices, on_device(): lax.all_to_all(row_sums.astype(jnp.bfloat16), 'zh', 0, 0, tiled=False)  8 us
    all_to_all x1, starting transfers between devices, on_device(): lax.all_to_all(row_sums.astype(jnp.bfloat16), 'zh', 0, 0, tiled=False)  6.92 us
  transfers between devices with their start and end apart: 2, of which 2 were waited for; matrix products, arithmetic and copies ran while one was open for 5% of the time, Pallas kernels for 0%

profile of v3, /device:TPU:6, one launch (start us, length us, event | category | flops | bytes accessed | tf_op | source)
XLA Modules:
  0.0 193.0 jit_solution(14866109108677296142)
XLA Ops:
  7.2 0.8 pad_maximum_fusion
  8.0 20.6 %all_gather.6 = bf16[640,256]{1,0:T(8,128)(2,1)} all-gather(bf16[160,256]{1,0:T(8,128)(2,1)S(1)} %pad_maximum_fusion), channel_id=1, replica_groups=mesh['zh'=4,'y'=8,'head'=16] {'zh'}, dimensions={0}, use_global_device_ids=true | all-gather | bytes 409600 | tf_op jit(solution)/shard_map/all_gather | solution.py:160
  28.7 0.7 dynamic_slice.3
  29.4 0.6 fusion.3
  32.8 0.9 reshape.142.qpos_ref
  33.7 1.0 reshape.102
  34.7 1.0 reshape.104
  35.7 0.8 scatter_custom_fusion
  36.5 0.7 pad_add_fusion.limits_ref
  37.2 0.7 reverse_select_fusion.3
  37.9 0.7 reverse_select_fusion.2
  38.6 35.1 %all-gather.2.cloned.1.call-done = bf16[5120,256]{1,0:T(8,128)(2,1)} async-done(((bf16[640,256]{1,0:T(8,128)(2,1)}), bf16[5120,256]{1,0:T(8,128)(2,1)}) %all-gather.2.cloned.1.call-update) | async-done | bytes 2621456 | tf_op jit(solution)/shard_map/all_gather | solution.py:160
  73.6 1.9 copy.51
  75.6 2.2 %gather_fusion = bf16[64,80,256]{2,1,0:T(8,128)(2,1)} fusion(bf16[64,80,256]{2,1,0:T(8,128)(2,1)S(1)} %bitcast.34, s32[1024]{0:T(1024)S(1)} %pad_clamp_fusion.1), kind=kCustom, calls=%fused_computation | custom fusion | bytes 5243136 | tf_op jit(solution)/shard_map/gather | solution.py:163
  77.8 21.3 %shard_map.84 = (bf16[640,128]{1,0:T(8,128)(2,1)}, bf16[640,128]{1,0:T(8,128)(2,1)}, f32[5120,256]{1,0:T(8,128)}) custom-call(s32[2]{0:T(128)} %pad_add_fusion.limits_ref, bf16[640,128]{1,0:T(8,128)(2,1)} %bitcast.42, bf16[640,128]{1,0:T(8,128)(2,1)} %bitcast.44, bf16[5120,256]{1,0:T(8,128)(2,1)} %bitcast.37, s32[640,1]{1,0:T(8,128)} %reshape.142.qpos_ref), custom_call_target="tpu_custom_call" | custom-call | flops 2936012800 | bytes 7864320 | tf_op jit(solution)/shard_map/pallas_call | solution.py:115
  99.1 3.3 %gather_fusion.1 = bf16[64,80,256]{2,1,0:T(8,128)(2,1)S(1)} fusion(f32[64,80,256]{2,1,0:T(8,128)} %bitcast.38, s32[1024]{0:T(1024)S(1)} %pad_clamp_fusion), kind=kCustom, calls=%fused_computation.1 | custom fusion | bytes 5243136 | tf_op jit(solution)/shard_map/gather | solution.py:191
  102.6 64.6 %all_to_all.10 = bf16[4,8,160,256]{3,2,0,1:T(8,128)(2,1)S(1)} all-to-all(bf16[4,8,160,256]{3,2,0,1:T(8,128)(2,1)S(1)} %copy.55), channel_id=1, replica_groups=mesh['zh'=4,'y'=8,'head'=16] {'y'}, dimensions={1} | all-to-all | bytes 5242880 | tf_op jit(solution)/shard_map/all_to_all | solution.py:192
  167.2 1.2 reduce_sum.21
  168.3 6.9 %all-to-all-start.1 = ((bf16[4,160,256]{2,1,0:T(8,128)(2,1)}), bf16[4,160,256]{2,1,0:T(8,128)(2,1)S(1)}, u32[]{:S(2)}, u32[]{:S(2)}) async-start(bf16[4,160,256]{2,1,0:T(8,128)(2,1)} %reduce_sum.21), calls=%async_computation.1 | async-start | bytes 655360 | tf_op jit(solution)/shard_map/all_to_all | solution.py:194
  175.4 0.7 copy.60
  176.2 0.7 copy.61
  176.9 8.0 %all-to-all-done.1 = bf16[4,160,256]{2,1,0:T(8,128)(2,1)S(1)} async-done(((bf16[4,160,256]{2,1,0:T(8,128)(2,1)}), bf16[4,160,256]{2,1,0:T(8,128)(2,1)S(1)}, u32[]{:S(2)}, u32[]{:S(2)}) %all-to-all-start.1) | async-done | bytes 327712 | tf_op jit(solution)/shard_map/all_to_all | solution.py:194
  184.9 0.6 fusion
  185.5 0.6 slice.29
  (23 shorter events, 0.7 us)
Async XLA Ops:
  7.2 28.5 %copy-start.2 = (s32[64]{0:T(128)S(1)}, s32[64]{0:T(128)}, u32[]{:S(2)}) copy-start(s32[64]{0:T(128)} %param.9) | copy-start | bytes 772
  7.2 66.5 %all-gather.2.cloned.1.call-start = ((), (), s32[]{:S(2)}) async-start(), calls=%async_computation.2 | async-start | bytes 2949120 | tf_op jit(solution)/shard_map/all_gather | solution.py:160
  167.2 8.1 %copy-start = (bf16[640,128]{1,0:T(8,128)(2,1)S(1)}, bf16[640,128]{1,0:T(8,128)(2,1)}, u32[]{:S(2)}) copy-start(bf16[640,128]{1,0:T(8,128)(2,1)} %get-tuple-element.7) | copy-start | bytes 491524
  167.2 8.1 %copy-start.1 = (bf16[640,128]{1,0:T(8,128)(2,1)S(1)}, bf16[640,128]{1,0:T(8,128)(2,1)}, u32[]{:S(2)}) copy-start(bf16[640,128]{1,0:T(8,128)(2,1)} %get-tuple-element.8) | copy-start | bytes 491524
  168.3 16.5 %all-to-all-start.1 = ((bf16[4,160,256]{2,1,0:T(8,128)(2,1)}), bf16[4,160,256]{2,1,0:T(8,128)(2,1)S(1)}, u32[]{:S(2)}, u32[]{:S(2)}) async-start(bf16[4,160,256]{2,1,0:T(8,128)(2,1)} %reduce_sum.21), calls=%async_computation.1 | async-start | bytes 655360 | tf_op jit(solution)/shard_map/all_to_all | solution.py:194
Sparse Core Ops, SparseCore 0:
  28.8 44.8 all-gather.1

commit v4 on v3

--- a/solution.py
+++ b/solution.py
@@ -12,7 +12,7 @@
 KV_HEADS = 8
 HEAD_DIM = 128
 SPAN = 80
-KEY_BLOCK = 512
+KEY_BLOCK = 5120
 
 NEG = -1e30
 CTX = ("zh", "y")

time: 194 us -> 194 us (level)
  transfers between devices with their start and end apart: 2 -> 2, of which waited for: 2 -> 2; matrix products, arithmetic and copies ran while one was open for 5% -> 4% of each run, Pallas kernels for 0% -> 0%
where the time goes in v4:
time: 194 us
  blocking collectives  84.3 us (43%)
  waiting for transfers between devices  43.1 us (22%)
  Pallas kernels  22.4 us (12%)
  between operations  16.8 us (9%)
  local copies, waits for them, and re-layouts  14.7 us (8%)
  starting transfers between devices  7.41 us (4%)
  other arithmetic  4.86 us (3%)
    all_to_all x1, blocking collectives, on_device(): lax.all_to_all(dkv_all.astype(jnp.bfloat16), 'y', 1, 1, tiled=False)  63.7 us
    all_gather x1, waiting for transfers between devices, on_device(): lax.all_gather(lax.all_gather(kv_local, 'zh', axis=0, tiled=True), 'y', a...  35.1 us
    pallas_call x1, Pallas kernels, local_attention(): pl.pallas_call(attention_kernel, out_shape=(jax.ShapeDtypeStruct((rows, w...  22.4 us
    all_gather x1, blocking collectives, on_device(): lax.all_gather(kv_local, 'zh', axis=0, tiled=True)  20.6 us
    all_to_all x1, waiting for transfers between devices, on_device(): lax.all_to_all(row_sums.astype(jnp.bfloat16), 'zh', 0, 0, tiled=False)  8 us
    all_to_all x1, starting transfers between devices, on_device(): lax.all_to_all(row_sums.astype(jnp.bfloat16), 'zh', 0, 0, tiled=False)  7.37 us
  transfers between devices with their start and end apart: 2, of which 2 were waited for; matrix products, arithmetic and copies ran while one was open for 4% of the time, Pallas kernels for 0%

profile of v4, /device:TPU:6, one launch (start us, length us, event | category | flops | bytes accessed | tf_op | source)
XLA Modules:
  0.0 193.7 jit_solution(14862980851759807372)
XLA Ops:
  7.2 0.8 pad_maximum_fusion
  8.0 20.6 %all_gather.6 = bf16[640,256]{1,0:T(8,128)(2,1)} all-gather(bf16[160,256]{1,0:T(8,128)(2,1)S(1)} %pad_maximum_fusion), channel_id=1, replica_groups=mesh['zh'=4,'y'=8,'head'=16] {'zh'}, dimensions={0}, use_global_device_ids=true | all-gather | bytes 409600 | tf_op jit(solution)/shard_map/all_gather | solution.py:160
  28.7 0.7 dynamic_slice.3
  29.4 0.6 fusion.3
  32.8 0.9 reshape.162.qpos_ref
  33.7 1.0 reshape.104
  34.7 1.0 reshape.102
  35.7 0.8 scatter_custom_fusion
  36.5 0.6 pad_add_fusion.limits_ref
  37.1 0.7 reverse_select_fusion.2
  37.8 0.7 reverse_select_fusion.3
  38.5 35.1 %all-gather.2.cloned.1.call-done = bf16[5120,256]{1,0:T(8,128)(2,1)} async-done(((bf16[640,256]{1,0:T(8,128)(2,1)}), bf16[5120,256]{1,0:T(8,128)(2,1)}) %all-gather.2.cloned.1.call-update) | async-done | bytes 2621456 | tf_op jit(solution)/shard_map/all_gather | solution.py:160
  73.6 1.9 copy.51
  75.6 2.2 %gather_fusion = bf16[64,80,256]{2,1,0:T(8,128)(2,1)} fusion(bf16[64,80,256]{2,1,0:T(8,128)(2,1)S(1)} %bitcast.36, s32[1024]{0:T(1024)S(1)} %pad_clamp_fusion.1), kind=kCustom, calls=%fused_computation | custom fusion | bytes 5243136 | tf_op jit(solution)/shard_map/gather | solution.py:163
  77.8 22.4 %shard_map.84 = (bf16[640,128]{1,0:T(8,128)(2,1)}, bf16[640,128]{1,0:T(8,128)(2,1)}, f32[5120,256]{1,0:T(8,128)}) custom-call(s32[2]{0:T(128)} %pad_add_fusion.limits_ref, bf16[640,128]{1,0:T(8,128)(2,1)} %bitcast.46, bf16[640,128]{1,0:T(8,128)(2,1)} %bitcast.44, bf16[5120,256]{1,0:T(8,128)(2,1)} %bitcast.39, s32[640,1]{1,0:T(8,128)} %reshape.162.qpos_ref), custom_call_target="tpu_custom_call" | custom-call | flops 2936012800 | bytes 7864320 | tf_op jit(solution)/shard_map/pallas_call | solution.py:115
  100.2 3.3 %gather_fusion.1 = bf16[64,80,256]{2,1,0:T(8,128)(2,1)S(1)} fusion(f32[64,80,256]{2,1,0:T(8,128)} %bitcast.40, s32[1024]{0:T(1024)S(1)} %pad_clamp_fusion), kind=kCustom, calls=%fused_computation.1 | custom fusion | bytes 5243136 | tf_op jit(solution)/shard_map/gather | solution.py:191
  103.7 63.7 %all_to_all.10 = bf16[4,8,160,256]{3,2,0,1:T(8,128)(2,1)S(1)} all-to-all(bf16[4,8,160,256]{3,2,0,1:T(8,128)(2,1)S(1)} %copy.55), channel_id=1, replica_groups=mesh['zh'=4,'y'=8,'head'=16] {'y'}, dimensions={1} | all-to-all | bytes 5242880 | tf_op jit(solution)/shard_map/all_to_all | solution.py:192
  167.4 1.2 reduce_sum.21
  168.6 7.4 %all-to-all-start.1 = ((bf16[4,160,256]{2,1,0:T(8,128)(2,1)}), bf16[4,160,256]{2,1,0:T(8,128)(2,1)S(1)}, u32[]{:S(2)}, u32[]{:S(2)}) async-start(bf16[4,160,256]{2,1,0:T(8,128)(2,1)} %reduce_sum.21), calls=%async_computation.1 | async-start | bytes 655360 | tf_op jit(solution)/shard_map/all_to_all | solution.py:194
  176.1 0.7 copy.60
  176.8 0.7 copy.61
  177.5 8.0 %all-to-all-done.1 = bf16[4,160,256]{2,1,0:T(8,128)(2,1)S(1)} async-done(((bf16[4,160,256]{2,1,0:T(8,128)(2,1)}), bf16[4,160,256]{2,1,0:T(8,128)(2,1)S(1)}, u32[]{:S(2)}, u32[]{:S(2)}) %all-to-all-start.1) | async-done | bytes 327712 | tf_op jit(solution)/shard_map/all_to_all | solution.py:194
  185.6 0.6 fusion
  186.2 0.6 slice.29
  (23 shorter events, 0.7 us)
Async XLA Ops:
  7.2 28.5 %copy-start.2 = (s32[64]{0:T(128)S(1)}, s32[64]{0:T(128)}, u32[]{:S(2)}) copy-start(s32[64]{0:T(128)} %param.9) | copy-start | bytes 772
  7.2 66.5 %all-gather.2.cloned.1.call-start = ((), (), s32[]{:S(2)}) async-start(), calls=%async_computation.2 | async-start | bytes 2949120 | tf_op jit(solution)/shard_map/all_gather | solution.py:160
  167.4 8.5 %copy-start = (bf16[640,128]{1,0:T(8,128)(2,1)S(1)}, bf16[640,128]{1,0:T(8,128)(2,1)}, u32[]{:S(2)}) copy-start(bf16[640,128]{1,0:T(8,128)(2,1)} %get-tuple-element.7) | copy-start | bytes 491524
  167.4 8.5 %copy-start.1 = (bf16[640,128]{1,0:T(8,128)(2,1)S(1)}, bf16[640,128]{1,0:T(8,128)(2,1)}, u32[]{:S(2)}) copy-start(bf16[640,128]{1,0:T(8,128)(2,1)} %get-tuple-element.8) | copy-start | bytes 491524
  168.6 17.0 %all-to-all-start.1 = ((bf16[4,160,256]{2,1,0:T(8,128)(2,1)}), bf16[4,160,256]{2,1,0:T(8,128)(2,1)S(1)}, u32[]{:S(2)}, u32[]{:S(2)}) async-start(bf16[4,160,256]{2,1,0:T(8,128)(2,1)} %reduce_sum.21), calls=%async_computation.1 | async-start | bytes 655360 | tf_op jit(solution)/shard_map/all_to_all | solution.py:194
Sparse Core Ops, SparseCore 0:
  28.8 44.8 all-gather.1

commit v5 on v4

--- a/solution.py
+++ b/solution.py
@@ -12,7 +12,7 @@
 KV_HEADS = 8
 HEAD_DIM = 128
 SPAN = 80
-KEY_BLOCK = 5120
+KEY_BLOCK = 1024
 
 NEG = -1e30
 CTX = ("zh", "y")
@@ -29,26 +29,27 @@
     scale = 1.0 / math.sqrt(width)
     early_blocks = limits_ref[0]
     late_blocks = limits_ref[1]
+    early_first = limits_ref[2]
+    late_first = limits_ref[3]
 
     top_ref[...] = jnp.full(top_ref.shape, NEG, jnp.float32)
     total_ref[...] = jnp.zeros(total_ref.shape, jnp.float32)
     acc_ref[...] = jnp.zeros(acc_ref.shape, jnp.float32)
 
-    def scores_of(lo, count, start):
+    def scores_of(lo, count, start, masked):
         q = q_ref[lo:lo + count, :]
         k = kv_ref[pl.ds(start, KEY_BLOCK), 0:width]
         s = lax.dot_general(q, k, (((1,), (1,)), ((), ())), preferred_element_type=jnp.float32) * scale
-        kpos = start + lax.broadcasted_iota(jnp.int32, (1, KEY_BLOCK), 1)
-        visible = kpos <= qpos_ref[lo:lo + count, :]
-        return s, visible
-
-    def forward_block(lo, count, block):
-        start = pl.multiple_of(block * KEY_BLOCK, KEY_BLOCK)
-        s, visible = scores_of(lo, count, start)
-        s = jnp.where(visible, s, NEG)
+        if masked:
+            kpos = start + lax.broadcasted_iota(jnp.int32, (1, KEY_BLOCK), 1)
+            s = jnp.where(kpos <= qpos_ref[lo:lo + count, :], s, NEG)
+        return s
+
+    def forward_masked(lo, count, start, masked):
+        s = scores_of(lo, count, start, masked)
         old_top = top_ref[lo:lo + count, :]
         new_top = jnp.maximum(old_top, jnp.max(s, axis=1, keepdims=True))
-        p = jnp.where(visible, jnp.exp(s - new_top), 0.0)
+        p = jnp.exp(s - new_top)
         rescale = jnp.exp(old_top - new_top)
         total_ref[lo:lo + count, :] = total_ref[lo:lo + count, :] * rescale + jnp.sum(p, axis=1, keepdims=True)
         v = kv_ref[pl.ds(start, KEY_BLOCK), width:2 * width]
@@ -56,12 +57,27 @@
         acc_ref[lo:lo + count, :] = acc_ref[lo:lo + count, :] * rescale + pv
         top_ref[lo:lo + count, :] = new_top
 
+    def split_by_mask(body, lo, count, block, first_row):
+        start = pl.multiple_of(block * KEY_BLOCK, KEY_BLOCK)
+        needs_mask = start + KEY_BLOCK - 1 > first_row
+
+        @pl.when(needs_mask)
+        def _():
+            body(lo, count, start, True)
+
+        @pl.when(jnp.logical_not(needs_mask))
+        def _():
+            body(lo, count, start, False)
+
+    def forward_block(lo, count, block, first_row):
+        split_by_mask(forward_masked, lo, count, block, first_row)
+
     def fwd_both(block, carry):
-        forward_block(0, rows, block)
+        forward_block(0, rows, block, early_first)
         return carry
 
     def fwd_late(block, carry):
-        forward_block(half, half, block)
+        forward_block(half, half, block, late_first)
         return carry
 
     lax.fori_loop(0, early_blocks, fwd_both, 0)
@@ -76,10 +92,9 @@
     dqacc_ref[...] = jnp.zeros(dqacc_ref.shape, jnp.float32)
     dkv_ref[...] = jnp.zeros(dkv_ref.shape, jnp.float32)
 
-    def backward_block(lo, count, block):
-        start = pl.multiple_of(block * KEY_BLOCK, KEY_BLOCK)
-        s, visible = scores_of(lo, count, start)
-        probs = jnp.where(visible, jnp.exp(s - lse_ref[lo:lo + count, :]), 0.0)
+    def backward_masked(lo, count, start, masked):
+        s = scores_of(lo, count, start, masked)
+        probs = jnp.exp(s - lse_ref[lo:lo + count, :])
         g = g_ref[lo:lo + count, :]
         k = kv_ref[pl.ds(start, KEY_BLOCK), 0:width]
         v = kv_ref[pl.ds(start, KEY_BLOCK), width:2 * width]
@@ -95,11 +110,11 @@
         dkv_ref[pl.ds(start, KEY_BLOCK), width:2 * width] += dv
 
     def bwd_both(block, carry):
-        backward_block(0, rows, block)
+        split_by_mask(backward_masked, 0, rows, block, early_first)
         return carry
 
     def bwd_late(block, carry):
-        backward_block(half, half, block)
+        split_by_mask(backward_masked, half, half, block, late_first)
         return carry
 
     lax.fori_loop(0, early_blocks, bwd_both, 0)
@@ -158,9 +173,10 @@
     inner = lax.axis_size("y")
     kv_local = jnp.concatenate([keys, values], axis=1)
     kv_all = lax.all_gather(lax.all_gather(kv_local, "zh", axis=0, tiled=True), "y", axis=0, tiled=True)
-    kv_all = kv_all.reshape(inner, outer, 2 * SPAN, 2 * width).transpose(1, 0, 2, 3)
     inverse = jnp.zeros((span_count,), jnp.int32).at[order].set(jnp.arange(span_count, dtype=jnp.int32))
-    kv_sorted = kv_all.reshape(span_count, SPAN, 2 * width)[inverse].reshape(span_count * SPAN, 2 * width)
+    holder = inverse // 2
+    gathered_at = 2 * ((holder % inner) * outer + holder // inner) + inverse % 2
+    kv_sorted = kv_all.reshape(span_count, SPAN, 2 * width)[gathered_at].reshape(span_count * SPAN, 2 * width)
 
     pair = lax.dynamic_slice_in_dim(order, 2 * my_index, 2)
     low_first = pair[0] < pair[1]
@@ -168,7 +184,12 @@
     early_keys = (my_low + 1) * SPAN
     late_keys = (span_count - my_low) * SPAN
     limits = jnp.stack(
-        [(early_keys + KEY_BLOCK - 1) // KEY_BLOCK, (late_keys + KEY_BLOCK - 1) // KEY_BLOCK]
+        [
+            (early_keys + KEY_BLOCK - 1) // KEY_BLOCK,
+            (late_keys + KEY_BLOCK - 1) // KEY_BLOCK,
+            my_low * SPAN,
+            (span_count - 1 - my_low) * SPAN,
+        ]
     ).astype(jnp.int32)
 
     def to_rows(array):

time: 194 us -> 190 us (0.979)
  Pallas kernels: 22.4 us -> 17.2 us
    pallas_call x1, Pallas kernels: 22.4 us -> 17.2 us  [local_attention(): pl.pallas_call(attention_kernel, out_shape=(jax.ShapeDtypeStruct((rows, w...]
  transfers between devices with their start and end apart: 2 -> 2, of which waited for: 2 -> 2; matrix products, arithmetic and copies ran while one was open for 4% -> 5% of each run, Pallas kernels for 0% -> 0%
where the time goes in v5:
time: 190 us
  blocking collectives  84.3 us (44%)
  waiting for transfers between devices  43.2 us (23%)
  Pallas kernels  17.2 us (9%)
  between operations  16.8 us (9%)
  local copies, waits for them, and re-layouts  14.5 us (8%)
  starting transfers between devices  8.98 us (5%)
  other arithmetic  4.96 us (3%)
    all_to_all x1, blocking collectives, on_device(): lax.all_to_all(dkv_all.astype(jnp.bfloat16), 'y', 1, 1, tiled=False)  63.7 us
    all_gather x1, waiting for transfers between devices, on_device(): lax.all_gather(lax.all_gather(kv_local, 'zh', axis=0, tiled=True), 'y', a...  35 us
    all_gather x1, blocking collectives, on_device(): lax.all_gather(kv_local, 'zh', axis=0, tiled=True)  20.6 us
    pallas_call x1, Pallas kernels, local_attention(): pl.pallas_call(attention_kernel, out_shape=(jax.ShapeDtypeStruct((rows, w...  17.2 us
    all_to_all x1, starting transfers between devices, on_device(): lax.all_to_all(row_sums.astype(jnp.bfloat16), 'zh', 0, 0, tiled=False)  8.94 us
    all_to_all x1, waiting for transfers between devices, on_device(): lax.all_to_all(row_sums.astype(jnp.bfloat16), 'zh', 0, 0, tiled=False)  8.14 us
    gather x1, local copies, waits for them, and re-layouts, on_device(): kv_all.reshape(span_count, SPAN, 2 * width)[gathered_at]  3.96 us
  transfers between devices with their start and end apart: 2, of which 2 were waited for; matrix products, arithmetic and copies ran while one was open for 5% of the time, Pallas kernels for 0%

profile of v5, /device:TPU:6, one launch (start us, length us, event | category | flops | bytes accessed | tf_op | source)
XLA Modules:
  0.0 190.0 jit_solution(17546987798938698076)
XLA Ops:
  7.2 0.8 pad_maximum_fusion
  8.0 20.6 %all_gather.6 = bf16[640,256]{1,0:T(8,128)(2,1)} all-gather(bf16[160,256]{1,0:T(8,128)(2,1)S(1)} %pad_maximum_fusion), channel_id=1, replica_groups=mesh['zh'=4,'y'=8,'head'=16] {'zh'}, dimensions={0}, use_global_device_ids=true | all-gather | bytes 409600 | tf_op jit(solution)/shard_map/all_gather | solution.py:175
  28.7 0.7 dynamic_slice.3
  29.4 0.6 fusion.6
  32.8 0.9 reshape.144.qpos_ref
  33.7 1.0 reshape.105
  34.7 1.0 reshape.107
  35.7 0.8 scatter_custom_fusion
  36.5 0.7 pad_add_fusion.limits_ref
  37.2 0.7 reverse_select_fusion.3
  37.9 0.7 reverse_select_fusion.2
  38.6 35.0 %all-gather.2.cloned.1.call-done = bf16[5120,256]{1,0:T(8,128)(2,1)} async-done(((bf16[640,256]{1,0:T(8,128)(2,1)}), bf16[5120,256]{1,0:T(8,128)(2,1)}) %all-gather.2.cloned.1.call-update) | async-done | bytes 2621456 | tf_op jit(solution)/shard_map/all_gather | solution.py:175
  73.6 4.0 %gather_fusion = bf16[64,80,256]{2,1,0:T(8,128)(2,1)} fusion(bf16[64,80,256]{2,1,0:T(8,128)(2,1)} %bitcast.32, s32[1024]{0:T(1024)S(1)} %pad_clamp_fusion.1), kind=kCustom, calls=%fused_computation | custom fusion | bytes 5243136 | tf_op jit(solution)/shard_map/gather | solution.py:179
  77.6 17.2 %shard_map.84 = (bf16[640,128]{1,0:T(8,128)(2,1)}, bf16[640,128]{1,0:T(8,128)(2,1)}, f32[5120,256]{1,0:T(8,128)}) custom-call(s32[4]{0:T(128)} %pad_add_fusion.limits_ref, bf16[640,128]{1,0:T(8,128)(2,1)} %bitcast.39, bf16[640,128]{1,0:T(8,128)(2,1)} %bitcast.40, bf16[5120,256]{1,0:T(8,128)(2,1)} %bitcast.33, s32[640,1]{1,0:T(8,128)} %reshape.144.qpos_ref), custom_call_target="tpu_custom_call" | custom-call | flops 2936012800 | bytes 7864320 | tf_op jit(solution)/shard_map/pallas_call | solution.py:130
  94.8 3.3 %gather_fusion.1 = bf16[64,80,256]{2,1,0:T(8,128)(2,1)S(1)} fusion(f32[64,80,256]{2,1,0:T(8,128)} %bitcast.34, s32[1024]{0:T(1024)S(1)} %pad_clamp_fusion), kind=kCustom, calls=%fused_computation.1 | custom fusion | bytes 5243136 | tf_op jit(solution)/shard_map/gather | solution.py:212
  98.1 0.2 copy.44
  98.3 63.7 %all_to_all.10 = bf16[4,8,160,256]{3,2,0,1:T(8,128)(2,1)S(1)} all-to-all(bf16[4,8,160,256]{3,2,0,1:T(8,128)(2,1)S(1)} %copy.44), channel_id=1, replica_groups=mesh['zh'=4,'y'=8,'head'=16] {'y'}, dimensions={1} | all-to-all | bytes 5242880 | tf_op jit(solution)/shard_map/all_to_all | solution.py:213
  162.0 1.2 reduce_sum.21
  163.1 8.9 %all-to-all-start.1 = ((bf16[4,160,256]{2,1,0:T(8,128)(2,1)}), bf16[4,160,256]{2,1,0:T(8,128)(2,1)S(1)}, u32[]{:S(2)}, u32[]{:S(2)}) async-start(bf16[4,160,256]{2,1,0:T(8,128)(2,1)} %reduce_sum.21), calls=%async_computation.1 | async-start | bytes 655360 | tf_op jit(solution)/shard_map/all_to_all | solution.py:215
  172.2 0.7 copy.49
  173.0 0.7 copy.50
  173.7 8.1 %all-to-all-done.1 = bf16[4,160,256]{2,1,0:T(8,128)(2,1)S(1)} async-done(((bf16[4,160,256]{2,1,0:T(8,128)(2,1)}), bf16[4,160,256]{2,1,0:T(8,128)(2,1)S(1)}, u32[]{:S(2)}, u32[]{:S(2)}) %all-to-all-start.1) | async-done | bytes 327712 | tf_op jit(solution)/shard_map/all_to_all | solution.py:215
  181.9 0.6 fusion
  182.5 0.6 slice.29
  (22 shorter events, 0.6 us)
Async XLA Ops:
  7.2 28.5 %copy-start.2 = (s32[64]{0:T(128)S(1)}, s32[64]{0:T(128)}, u32[]{:S(2)}) copy-start(s32[64]{0:T(128)} %param.9) | copy-start | bytes 772
  7.2 66.5 %all-gather.2.cloned.1.call-start = ((), (), s32[]{:S(2)}) async-start(), calls=%async_computation.2 | async-start | bytes 2949120 | tf_op jit(solution)/shard_map/all_gather | solution.py:175
  162.0 10.1 %copy-start = (bf16[640,128]{1,0:T(8,128)(2,1)S(1)}, bf16[640,128]{1,0:T(8,128)(2,1)}, u32[]{:S(2)}) copy-start(bf16[640,128]{1,0:T(8,128)(2,1)} %get-tuple-element.7) | copy-start | bytes 491524
  162.0 10.1 %copy-start.1 = (bf16[640,128]{1,0:T(8,128)(2,1)S(1)}, bf16[640,128]{1,0:T(8,128)(2,1)}, u32[]{:S(2)}) copy-start(bf16[640,128]{1,0:T(8,128)(2,1)} %get-tuple-element.8) | copy-start | bytes 491524
  163.1 18.7 %all-to-all-start.1 = ((bf16[4,160,256]{2,1,0:T(8,128)(2,1)}), bf16[4,160,256]{2,1,0:T(8,128)(2,1)S(1)}, u32[]{:S(2)}, u32[]{:S(2)}) async-start(bf16[4,160,256]{2,1,0:T(8,128)(2,1)} %reduce_sum.21), calls=%async_computation.1 | async-start | bytes 655360 | tf_op jit(solution)/shard_map/all_to_all | solution.py:215
Sparse Core Ops, SparseCore 0:
  28.8 44.8 all-gather.1

commit v6 on v5

--- a/solution.py
+++ b/solution.py
@@ -122,6 +122,11 @@
     dq_ref[...] = (dqacc_ref[...] * scale).astype(jnp.bfloat16)
 
 
+def shifted(array, axis, by):
+    length = lax.axis_size(axis)
+    return lax.ppermute(array, axis, [(i, (i + by) % length) for i in range(length)])
+
+
 def local_attention(limits, q_rows, g_rows, kv_sorted, q_pos):
     rows, width = q_rows.shape
     keys = kv_sorted.shape[0]
@@ -172,10 +177,20 @@
     outer = lax.axis_size("zh")
     inner = lax.axis_size("y")
     kv_local = jnp.concatenate([keys, values], axis=1)
-    kv_all = lax.all_gather(lax.all_gather(kv_local, "zh", axis=0, tiled=True), "y", axis=0, tiled=True)
+    column = lax.all_gather(kv_local, "zh", axis=0, tiled=True)
+    rightward = [column]
+    leftward = [column]
+    for _ in range(inner // 2):
+        rightward.append(shifted(rightward[-1], "y", 1))
+    for _ in range((inner - 1) // 2):
+        leftward.append(shifted(leftward[-1], "y", -1))
+    by_distance = leftward + rightward[1:][::-1]
+    kv_all = jnp.concatenate(by_distance, axis=0)
+    my_y = lax.axis_index("y")
     inverse = jnp.zeros((span_count,), jnp.int32).at[order].set(jnp.arange(span_count, dtype=jnp.int32))
     holder = inverse // 2
-    gathered_at = 2 * ((holder % inner) * outer + holder // inner) + inverse % 2
+    distance = (holder % inner - my_y + inner) % inner
+    gathered_at = 2 * (distance * outer + holder // inner) + inverse % 2
     kv_sorted = kv_all.reshape(span_count, SPAN, 2 * width)[gathered_at].reshape(span_count * SPAN, 2 * width)
 
     pair = lax.dynamic_slice_in_dim(order, 2 * my_index, 2)

time: 190 us -> 172 us (0.905)
  waiting for transfers between devices: 43.2 us -> 21.2 us
  starting transfers between devices: 8.98 us -> 26.8 us
  between operations: 16.8 us -> 3.5 us
    all_gather x1 -> x0, waiting for transfers between devices: 35 us -> none  [on_device(): lax.all_gather(lax.all_gather(kv_local, 'zh', axis=0, tiled=True), 'y', a...]
    ppermute x0 -> x7, starting transfers between devices: none -> 23.3 us  [shifted(): lax.ppermute(array, axis, [(i, (i + by) % length) for i in range(length)])]
    ppermute x0 -> x7, waiting for transfers between devices: none -> 12.9 us  [shifted(): lax.ppermute(array, axis, [(i, (i + by) % length) for i in range(length)])]
    all_to_all x1, starting transfers between devices: 8.94 us -> 3.51 us  [on_device(): lax.all_to_all(row_sums.astype(jnp.bfloat16), 'zh', 0, 0, tiled=False)]
  transfers between devices with their start and end apart: 2 -> 8, of which waited for: 2 -> 4; matrix products, arithmetic and copies ran while one was open for 5% -> 6% of each run, Pallas kernels for 0% -> 0%
where the time goes in v6:
time: 172 us
  blocking collectives  82.8 us (48%)
  starting transfers between devices  26.8 us (16%)
  waiting for transfers between devices  21.2 us (12%)
  Pallas kernels  16.8 us (10%)
  local copies, waits for them, and re-layouts  14.9 us (9%)
  other arithmetic  5.59 us (3%)
  between operations  3.5 us (2%)
    all_to_all x1, blocking collectives, on_device(): lax.all_to_all(dkv_all.astype(jnp.bfloat16), 'y', 1, 1, tiled=False)  62.8 us
    ppermute x7, starting transfers between devices, shifted(): lax.ppermute(array, axis, [(i, (i + by) % length) for i in range(length)])  23.3 us
    all_gather x1, blocking collectives, on_device(): column = lax.all_gather(kv_local, 'zh', axis=0, tiled=True)  20 us
    pallas_call x1, Pallas kernels, local_attention(): pl.pallas_call(attention_kernel, out_shape=(jax.ShapeDtypeStruct((rows, w...  16.8 us
    ppermute x7, waiting for transfers between devices, shifted(): lax.ppermute(array, axis, [(i, (i + by) % length) for i in range(length)])  12.9 us
    all_to_all x1, waiting for transfers between devices, on_device(): lax.all_to_all(row_sums.astype(jnp.bfloat16), 'zh', 0, 0, tiled=False)  8.31 us
    all_to_all x1, starting transfers between devices, on_device(): lax.all_to_all(row_sums.astype(jnp.bfloat16), 'zh', 0, 0, tiled=False)  3.51 us
  transfers between devices with their start and end apart: 8, of which 4 were waited for; matrix products, arithmetic and copies ran while one was open for 6% of the time, Pallas kernels for 0%

profile of v6, /device:TPU:6, one launch (start us, length us, event | category | flops | bytes accessed | tf_op | source)
XLA Modules:
  0.0 171.6 jit_solution(261136485582728127)
XLA Ops:
  0.6 0.8 pad_maximum_fusion
  1.4 20.0 %all_gather.3 = bf16[640,256]{1,0:T(8,128)(2,1)S(1)} all-gather(bf16[160,256]{1,0:T(8,128)(2,1)S(1)} %pad_maximum_fusion), channel_id=1, replica_groups=mesh['zh'=4,'y'=8,'head'=16] {'zh'}, dimensions={0}, use_global_device_ids=true | all-gather | bytes 409600 | tf_op jit(solution)/shard_map/all_gather | solution.py:180
  21.4 5.4 %collective-permute-start = (bf16[640,256]{1,0:T(8,128)(2,1)S(1)}, bf16[640,256]{1,0:T(8,128)(2,1)}, u32[]{:S(2)}, u32[]{:S(2)}) collective-permute-start(bf16[640,256]{1,0:T(8,128)(2,1)S(1)} %all_gather.3), channel_id=1, source_target_pairs={{0,112},{16,0},{32,16},{48,32},{64,48},{80,64},{96,80},{112,96},{1... | collective-permute-start | bytes 983048 | tf_op jit(solution)/shard_map/ppermute | solution.py:127
  26.8 1.9 %collective-permute-start.3 = (bf16[640,256]{1,0:T(8,128)(2,1)S(1)}, bf16[640,256]{1,0:T(8,128)(2,1)}, u32[]{:S(2)}, u32[]{:S(2)}) collective-permute-start(bf16[640,256]{1,0:T(8,128)(2,1)S(1)} %all_gather.3), channel_id=1, source_target_pairs={{0,16},{16,32},{32,48},{48,64},{64,80},{80,96},{96,112},{112,0},{1... | collective-permute-start | bytes 983048 | tf_op jit(solution)/shard_map/ppermute | solution.py:127
  33.5 0.9 reshape.144.qpos_ref
  34.4 1.0 reshape.105
  35.4 1.0 reshape.107
  37.9 2.0 %collective-permute-start.4 = (bf16[640,256]{1,0:T(8,128)(2,1)}, bf16[640,256]{1,0:T(8,128)(2,1)S(1)}, u32[]{:S(2)}, u32[]{:S(2)}) collective-permute-start(bf16[640,256]{1,0:T(8,128)(2,1)} %collective-permute-done.3), channel_id=1, source_target_pairs={{0,16},{16,32},{32,48},{48,64},{64,80},{80,96},{96,112},{112,0},{1... | collective-permute-start | bytes 983048 | tf_op jit(solution)/shard_map/ppermute | solution.py:127
  40.0 5.0 %collective-permute-start.1 = (bf16[640,256]{1,0:T(8,128)(2,1)}, bf16[640,256]{1,0:T(8,128)(2,1)S(1)}, u32[]{:S(2)}, u32[]{:S(2)}) collective-permute-start(bf16[640,256]{1,0:T(8,128)(2,1)} %collective-permute-done), channel_id=1, source_target_pairs={{0,112},{16,0},{32,16},{48,32},{64,48},{80,64},{96,80},{112,96},{1... | collective-permute-start | bytes 983048 | tf_op jit(solution)/shard_map/ppermute | solution.py:127
  45.1 3.9 %collective-permute-done.4 = bf16[640,256]{1,0:T(8,128)(2,1)S(1)} collective-permute-done((bf16[640,256]{1,0:T(8,128)(2,1)}, bf16[640,256]{1,0:T(8,128)(2,1)S(1)}, u32[]{:S(2)}, u32[]{:S(2)}) %collective-permute-start.4) | collective-permute-done | bytes 327712 | tf_op jit(solution)/shard_map/ppermute | solution.py:127
  49.0 1.9 %collective-permute-start.5 = (bf16[640,256]{1,0:T(8,128)(2,1)S(1)}, bf16[640,256]{1,0:T(8,128)(2,1)S(1)}, u32[]{:S(2)}, u32[]{:S(2)}) collective-permute-start(bf16[640,256]{1,0:T(8,128)(2,1)S(1)} %collective-permute-done.4), channel_id=1, source_target_pairs={{0,16},{16,32},{32,48},{48,64},{64,80},{80,96},{96,112},{112,0},{1... | collective-permute-start | bytes 983048 | tf_op jit(solution)/shard_map/ppermute | solution.py:127
  51.6 5.1 %collective-permute-start.2 = (bf16[640,256]{1,0:T(8,128)(2,1)S(1)}, bf16[640,256]{1,0:T(8,128)(2,1)S(1)}, u32[]{:S(2)}, u32[]{:S(2)}) collective-permute-start(bf16[640,256]{1,0:T(8,128)(2,1)S(1)} %collective-permute-done.1), channel_id=1, source_target_pairs={{0,112},{16,0},{32,16},{48,32},{64,48},{80,64},{96,80},{112,96},{1... | collective-permute-start | bytes 983048 | tf_op jit(solution)/shard_map/ppermute | solution.py:127
  57.4 1.8 %collective-permute-done.5 = bf16[640,256]{1,0:T(8,128)(2,1)S(1)} collective-permute-done((bf16[640,256]{1,0:T(8,128)(2,1)S(1)}, bf16[640,256]{1,0:T(8,128)(2,1)S(1)}, u32[]{:S(2)}, u32[]{:S(2)}) %collective-permute-start.5) | collective-permute-done | bytes 327712 | tf_op jit(solution)/shard_map/ppermute | solution.py:127
  59.2 1.9 %collective-permute-start.6 = (bf16[640,256]{1,0:T(8,128)(2,1)S(1)}, bf16[640,256]{1,0:T(8,128)(2,1)S(1)}, u32[]{:S(2)}, u32[]{:S(2)}) collective-permute-start(bf16[640,256]{1,0:T(8,128)(2,1)S(1)} %collective-permute-done.5), channel_id=1, source_target_pairs={{0,16},{16,32},{32,48},{48,64},{64,80},{80,96},{96,112},{112,0},{1... | collective-permute-start | bytes 983048 | tf_op jit(solution)/shard_map/ppermute | solution.py:127
  61.1 1.0 constant_dynamic-update-slice_fusion.6
  62.2 7.2 %collective-permute-done.6 = bf16[640,256]{1,0:T(8,128)(2,1)S(1)} collective-permute-done((bf16[640,256]{1,0:T(8,128)(2,1)S(1)}, bf16[640,256]{1,0:T(8,128)(2,1)S(1)}, u32[]{:S(2)}, u32[]{:S(2)}) %collective-permute-start.6) | collective-permute-done | bytes 327712 | tf_op jit(solution)/shard_map/ppermute | solution.py:127
  69.4 1.0 constant_dynamic-update-slice_fusion
  70.4 2.2 %gather_fusion = bf16[64,80,256]{2,1,0:T(8,128)(2,1)} fusion(bf16[64,80,256]{2,1,0:T(8,128)(2,1)S(1)} %bitcast.32, s32[1024]{0:T(1024)S(1)} %pad_clamp_fusion.1), kind=kCustom, calls=%fused_computation | custom fusion | bytes 5243136 | tf_op jit(solution)/shard_map/gather | solution.py:194
  72.6 16.8 %shard_map.84 = (bf16[640,128]{1,0:T(8,128)(2,1)}, bf16[640,128]{1,0:T(8,128)(2,1)}, f32[5120,256]{1,0:T(8,128)}) custom-call(s32[4]{0:T(128)} %pad_add_fusion.limits_ref, bf16[640,128]{1,0:T(8,128)(2,1)} %bitcast.37, bf16[640,128]{1,0:T(8,128)(2,1)} %bitcast.38, bf16[5120,256]{1,0:T(8,128)(2,1)} %bitcast.33, s32[640,1]{1,0:T(8,128)} %reshape.144.qpos_ref), custom_call_target="tpu_custom_call" | custom-call | flops 2936012800 | bytes 7864320 | tf_op jit(solution)/shard_map/pallas_call | solution.py:135
  89.4 3.3 %gather_fusion.1 = bf16[64,80,256]{2,1,0:T(8,128)(2,1)S(1)} fusion(f32[64,80,256]{2,1,0:T(8,128)} %bitcast.34, s32[1024]{0:T(1024)S(1)} %pad_clamp_fusion), kind=kCustom, calls=%fused_computation.1 | custom fusion | bytes 5243136 | tf_op jit(solution)/shard_map/gather | solution.py:227
  92.9 62.8 %all_to_all.10 = bf16[4,8,160,256]{3,2,0,1:T(8,128)(2,1)S(1)} all-to-all(bf16[4,8,160,256]{3,2,0,1:T(8,128)(2,1)S(1)} %copy.44), channel_id=1, replica_groups=mesh['zh'=4,'y'=8,'head'=16] {'y'}, dimensions={1} | all-to-all | bytes 5242880 | tf_op jit(solution)/shard_map/all_to_all | solution.py:228
  155.8 1.2 reduce_sum.21
  156.9 3.5 %all-to-all-start.1 = ((bf16[4,160,256]{2,1,0:T(8,128)(2,1)}), bf16[4,160,256]{2,1,0:T(8,128)(2,1)S(1)}, u32[]{:S(2)}, u32[]{:S(2)}) async-start(bf16[4,160,256]{2,1,0:T(8,128)(2,1)} %reduce_sum.21), calls=%async_computation.1 | async-start | bytes 655360 | tf_op jit(solution)/shard_map/all_to_all | solution.py:230
  162.0 8.3 %all-to-all-done.1 = bf16[4,160,256]{2,1,0:T(8,128)(2,1)S(1)} async-done(((bf16[4,160,256]{2,1,0:T(8,128)(2,1)}), bf16[4,160,256]{2,1,0:T(8,128)(2,1)S(1)}, u32[]{:S(2)}, u32[]{:S(2)}) %all-to-all-start.1) | async-done | bytes 327712 | tf_op jit(solution)/shard_map/all_to_all | solution.py:230
  (39 shorter events, 8.2 us)
Async XLA Ops:
  21.4 18.6 %collective-permute-start = (bf16[640,256]{1,0:T(8,128)(2,1)S(1)}, bf16[640,256]{1,0:T(8,128)(2,1)}, u32[]{:S(2)}, u32[]{:S(2)}) collective-permute-start(bf16[640,256]{1,0:T(8,128)(2,1)S(1)} %all_gather.3), channel_id=1, source_target_pairs={{0,112},{16,0},{32,16},{48,32},{64,48},{80,64},{96,80},{112,96},{1... | collective-permute-start | bytes 983048 | tf_op jit(solution)/shard_map/ppermute | solution.py:127
  26.8 11.1 %collective-permute-start.3 = (bf16[640,256]{1,0:T(8,128)(2,1)S(1)}, bf16[640,256]{1,0:T(8,128)(2,1)}, u32[]{:S(2)}, u32[]{:S(2)}) collective-permute-start(bf16[640,256]{1,0:T(8,128)(2,1)S(1)} %all_gather.3), channel_id=1, source_target_pairs={{0,16},{16,32},{32,48},{48,64},{64,80},{80,96},{96,112},{112,0},{1... | collective-permute-start | bytes 983048 | tf_op jit(solution)/shard_map/ppermute | solution.py:127
  37.9 11.0 %collective-permute-start.4 = (bf16[640,256]{1,0:T(8,128)(2,1)}, bf16[640,256]{1,0:T(8,128)(2,1)S(1)}, u32[]{:S(2)}, u32[]{:S(2)}) collective-permute-start(bf16[640,256]{1,0:T(8,128)(2,1)} %collective-permute-done.3), channel_id=1, source_target_pairs={{0,16},{16,32},{32,48},{48,64},{64,80},{80,96},{96,112},{112,0},{1... | collective-permute-start | bytes 983048 | tf_op jit(solution)/shard_map/ppermute | solution.py:127
  40.0 11.6 %collective-permute-start.1 = (bf16[640,256]{1,0:T(8,128)(2,1)}, bf16[640,256]{1,0:T(8,128)(2,1)S(1)}, u32[]{:S(2)}, u32[]{:S(2)}) collective-permute-start(bf16[640,256]{1,0:T(8,128)(2,1)} %collective-permute-done), channel_id=1, source_target_pairs={{0,112},{16,0},{32,16},{48,32},{64,48},{80,64},{96,80},{112,96},{1... | collective-permute-start | bytes 983048 | tf_op jit(solution)/shard_map/ppermute | solution.py:127
  49.0 10.2 %collective-permute-start.5 = (bf16[640,256]{1,0:T(8,128)(2,1)S(1)}, bf16[640,256]{1,0:T(8,128)(2,1)S(1)}, u32[]{:S(2)}, u32[]{:S(2)}) collective-permute-start(bf16[640,256]{1,0:T(8,128)(2,1)S(1)} %collective-permute-done.4), channel_id=1, source_target_pairs={{0,16},{16,32},{32,48},{48,64},{64,80},{80,96},{96,112},{112,0},{1... | collective-permute-start | bytes 983048 | tf_op jit(solution)/shard_map/ppermute | solution.py:127
  51.6 10.5 %collective-permute-start.2 = (bf16[640,256]{1,0:T(8,128)(2,1)S(1)}, bf16[640,256]{1,0:T(8,128)(2,1)S(1)}, u32[]{:S(2)}, u32[]{:S(2)}) collective-permute-start(bf16[640,256]{1,0:T(8,128)(2,1)S(1)} %collective-permute-done.1), channel_id=1, source_target_pairs={{0,112},{16,0},{32,16},{48,32},{64,48},{80,64},{96,80},{112,96},{1... | collective-permute-start | bytes 983048 | tf_op jit(solution)/shard_map/ppermute | solution.py:127
  59.2 10.2 %collective-permute-start.6 = (bf16[640,256]{1,0:T(8,128)(2,1)S(1)}, bf16[640,256]{1,0:T(8,128)(2,1)S(1)}, u32[]{:S(2)}, u32[]{:S(2)}) collective-permute-start(bf16[640,256]{1,0:T(8,128)(2,1)S(1)} %collective-permute-done.5), channel_id=1, source_target_pairs={{0,16},{16,32},{32,48},{48,64},{64,80},{80,96},{96,112},{112,0},{1... | collective-permute-start | bytes 983048 | tf_op jit(solution)/shard_map/ppermute | solution.py:127
  155.8 4.7 %copy-start = (bf16[640,128]{1,0:T(8,128)(2,1)S(1)}, bf16[640,128]{1,0:T(8,128)(2,1)}, u32[]{:S(2)}) copy-start(bf16[640,128]{1,0:T(8,128)(2,1)} %get-tuple-element.7) | copy-start | bytes 491524
  155.8 4.7 %copy-start.1 = (bf16[640,128]{1,0:T(8,128)(2,1)S(1)}, bf16[640,128]{1,0:T(8,128)(2,1)}, u32[]{:S(2)}) copy-start(bf16[640,128]{1,0:T(8,128)(2,1)} %get-tuple-element.8) | copy-start | bytes 491524
  156.9 13.4 %all-to-all-start.1 = ((bf16[4,160,256]{2,1,0:T(8,128)(2,1)}), bf16[4,160,256]{2,1,0:T(8,128)(2,1)S(1)}, u32[]{:S(2)}, u32[]{:S(2)}) async-start(bf16[4,160,256]{2,1,0:T(8,128)(2,1)} %reduce_sum.21), calls=%async_computation.1 | async-start | bytes 655360 | tf_op jit(solution)/shard_map/all_to_all | solution.py:230

commit v7 on v6

--- a/solution.py
+++ b/solution.py
@@ -224,9 +224,25 @@
     attention_rows, dq_rows, dkv_sorted = local_attention(
         limits, to_rows(queries), to_rows(out_grad), kv_sorted, q_pos
     )
-    dkv_all = dkv_sorted.reshape(span_count, SPAN, 2 * width)[order].reshape(outer, inner, 2 * SPAN, 2 * width)
-    row_parts = lax.all_to_all(dkv_all.astype(jnp.bfloat16), "y", 1, 1, tiled=False)
-    row_sums = jnp.sum(row_parts.astype(jnp.float32), axis=1)
+    owner_zh = jnp.arange(outer, dtype=jnp.int32)[:, None, None]
+    owner_y = (my_y + jnp.arange(inner, dtype=jnp.int32)[None, :, None]) % inner
+    half_block = jnp.arange(2, dtype=jnp.int32)[None, None, :]
+    by_owner = 2 * (owner_zh * inner + owner_y) + half_block
+    dkv_all = dkv_sorted.reshape(span_count, SPAN, 2 * width)[order[by_owner]]
+    dkv_all = dkv_all.reshape(outer, inner, 2 * SPAN, 2 * width)
+
+    def part(step):
+        return dkv_all[:, step % inner]
+
+    right = part(inner // 2)
+    for step in range(inner // 2 - 1, 0, -1):
+        right = shifted(right.astype(jnp.bfloat16), "y", 1).astype(jnp.float32) + part(step)
+    right = shifted(right.astype(jnp.bfloat16), "y", 1).astype(jnp.float32)
+    left = part(inner // 2 + 1)
+    for step in range(inner // 2 + 2, inner):
+        left = shifted(left.astype(jnp.bfloat16), "y", -1).astype(jnp.float32) + part(step)
+    left = shifted(left.astype(jnp.bfloat16), "y", -1).astype(jnp.float32)
+    row_sums = right + left + part(0)
     dkv_parts = lax.all_to_all(row_sums.astype(jnp.bfloat16), "zh", 0, 0, tiled=False)
     dkv_mine = jnp.sum(dkv_parts.astype(jnp.float32), axis=0)
     grad_keys = (score_scale * dkv_mine[:, :width]).astype(jnp.bfloat16)

time: 172 us -> 180 us (1.047); the launches traced: 172 us -> 177 us
  blocking collectives: 82.8 us -> 20 us
  waiting for transfers between devices: 21.2 us -> 53 us
  starting transfers between devices: 26.8 us -> 53.9 us
  other arithmetic: 5.59 us -> 11.4 us
  local copies, waits for them, and re-layouts: 14.9 us -> 18.7 us
    all_to_all x1 -> x0, blocking collectives: 62.8 us -> none  [on_device(): lax.all_to_all(dkv_all.astype(jnp.bfloat16), 'y', 1, 1, tiled=False)]
    ppermute x7 -> x14, waiting for transfers between devices: 12.9 us -> 44.7 us  [shifted(): lax.ppermute(array, axis, [(i, (i + by) % length) for i in range(length)])]
    ppermute x7 -> x14, starting transfers between devices: 23.3 us -> 42.7 us  [shifted(): lax.ppermute(array, axis, [(i, (i + by) % length) for i in range(length)])]
    all_to_all x1, starting transfers between devices: 3.51 us -> 11.2 us  [on_device(): lax.all_to_all(row_sums.astype(jnp.bfloat16), 'zh', 0, 0, tiled=False)]
    convert_element_type x0 -> x5, other arithmetic: none -> 6.84 us  [the longest x2 2.32 us: on_device(): right.astype(jnp.bfloat16)]
    gather x1 -> x3, local copies, waits for them, and re-layouts: 3.29 us -> 6.6 us  [on_device(): dkv_all = dkv_sorted.reshape(span_count, SPAN, 2 * width)[order[by_owner]]]
  transfers between devices with their start and end apart: 8 -> 15, of which waited for: 4 -> 9; matrix products, arithmetic and copies ran while one was open for 6% -> 7% of each run, Pallas kernels for 0% -> 0%
where the time goes in v7:
time: 180 us; the launch traced here: 177 us
  starting transfers between devices  53.9 us (30%)
  waiting for transfers between devices  53 us (29%)
  blocking collectives  20 us (11%)
  local copies, waits for them, and re-layouts  18.7 us (10%)
  Pallas kernels  16.2 us (9%)
  other arithmetic  11.4 us (6%)
  between operations  3.71 us (2%)
    ppermute x14, waiting for transfers between devices, shifted(): lax.ppermute(array, axis, [(i, (i + by) % length) for i in range(length)])  44.7 us
    ppermute x14, starting transfers between devices, shifted(): lax.ppermute(array, axis, [(i, (i + by) % length) for i in range(length)])  42.7 us
    all_gather x1, blocking collectives, on_device(): column = lax.all_gather(kv_local, 'zh', axis=0, tiled=True)  20 us
    pallas_call x1, Pallas kernels, local_attention(): pl.pallas_call(attention_kernel, out_shape=(jax.ShapeDtypeStruct((rows, w...  16.2 us
    all_to_all x1, starting transfers between devices, on_device(): lax.all_to_all(row_sums.astype(jnp.bfloat16), 'zh', 0, 0, tiled=False)  11.2 us
    all_to_all x1, waiting for transfers between devices, on_device(): lax.all_to_all(row_sums.astype(jnp.bfloat16), 'zh', 0, 0, tiled=False)  8.25 us
    gather x3, local copies, waits for them, and re-layouts, on_device(): dkv_all = dkv_sorted.reshape(span_count, SPAN, 2 * width)[order[by_owner]]  6.6 us
  transfers between devices with their start and end apart: 15, of which 9 were waited for; matrix products, arithmetic and copies ran while one was open for 7% of the time, Pallas kernels for 0%

profile of v7, /device:TPU:6, one launch (start us, length us, event | category | flops | bytes accessed | tf_op | source)
XLA Modules:
  0.0 176.9 jit_solution(14668767430039897153)
XLA Ops:
  1.5 20.0 %all_gather.3 = bf16[640,256]{1,0:T(8,128)(2,1)S(1)} all-gather(bf16[160,256]{1,0:T(8,128)(2,1)S(1)} %pad_maximum_fusion), channel_id=1, replica_groups=mesh['zh'=4,'y'=8,'head'=16] {'zh'}, dimensions={0}, use_global_device_ids=true | all-gather | bytes 409600 | tf_op jit(solution)/shard_map/all_gather | solution.py:180
  21.5 3.5 %collective-permute-start.3 = (bf16[640,256]{1,0:T(8,128)(2,1)S(1)}, bf16[640,256]{1,0:T(8,128)(2,1)}, u32[]{:S(2)}, u32[]{:S(2)}) collective-permute-start(bf16[640,256]{1,0:T(8,128)(2,1)S(1)} %all_gather.3), channel_id=1, source_target_pairs={{0,16},{16,32},{32,48},{48,64},{64,80},{80,96},{96,112},{112,0},{1... | collective-permute-start | bytes 983048 | tf_op jit(solution)/shard_map/ppermute | solution.py:127
  24.9 3.8 %collective-permute-start = (bf16[640,256]{1,0:T(8,128)(2,1)S(1)}, bf16[640,256]{1,0:T(8,128)(2,1)}, u32[]{:S(2)}, u32[]{:S(2)}) collective-permute-start(bf16[640,256]{1,0:T(8,128)(2,1)S(1)} %all_gather.3), channel_id=1, source_target_pairs={{0,112},{16,0},{32,16},{48,32},{64,48},{80,64},{96,80},{112,96},{1... | collective-permute-start | bytes 983048 | tf_op jit(solution)/shard_map/ppermute | solution.py:127
  37.8 2.0 %collective-permute-start.4 = (bf16[640,256]{1,0:T(8,128)(2,1)}, bf16[640,256]{1,0:T(8,128)(2,1)S(1)}, u32[]{:S(2)}, u32[]{:S(2)}) collective-permute-start(bf16[640,256]{1,0:T(8,128)(2,1)} %collective-permute-done.3), channel_id=1, source_target_pairs={{0,16},{16,32},{32,48},{48,64},{64,80},{80,96},{96,112},{112,0},{1... | collective-permute-start | bytes 983048 | tf_op jit(solution)/shard_map/ppermute | solution.py:127
  40.5 5.0 %collective-permute-start.1 = (bf16[640,256]{1,0:T(8,128)(2,1)}, bf16[640,256]{1,0:T(8,128)(2,1)S(1)}, u32[]{:S(2)}, u32[]{:S(2)}) collective-permute-start(bf16[640,256]{1,0:T(8,128)(2,1)} %collective-permute-done), channel_id=1, source_target_pairs={{0,112},{16,0},{32,16},{48,32},{64,48},{80,64},{96,80},{112,96},{1... | collective-permute-start | bytes 983048 | tf_op jit(solution)/shard_map/ppermute | solution.py:127
  45.6 3.3 %collective-permute-done.4 = bf16[640,256]{1,0:T(8,128)(2,1)S(1)} collective-permute-done((bf16[640,256]{1,0:T(8,128)(2,1)}, bf16[640,256]{1,0:T(8,128)(2,1)S(1)}, u32[]{:S(2)}, u32[]{:S(2)}) %collective-permute-start.4) | collective-permute-done | bytes 327712 | tf_op jit(solution)/shard_map/ppermute | solution.py:127
  51.5 5.1 %collective-permute-start.2 = (bf16[640,256]{1,0:T(8,128)(2,1)S(1)}, bf16[640,256]{1,0:T(8,128)(2,1)S(1)}, u32[]{:S(2)}, u32[]{:S(2)}) collective-permute-start(bf16[640,256]{1,0:T(8,128)(2,1)S(1)} %collective-permute-done.1), channel_id=1, source_target_pairs={{0,112},{16,0},{32,16},{48,32},{64,48},{80,64},{96,80},{112,96},{1... | collective-permute-start | bytes 983048 | tf_op jit(solution)/shard_map/ppermute | solution.py:127
  62.0 7.2 %collective-permute-done.6 = bf16[640,256]{1,0:T(8,128)(2,1)S(1)} collective-permute-done((bf16[640,256]{1,0:T(8,128)(2,1)S(1)}, bf16[640,256]{1,0:T(8,128)(2,1)S(1)}, u32[]{:S(2)}, u32[]{:S(2)}) %collective-permute-start.6) | collective-permute-done | bytes 327712 | tf_op jit(solution)/shard_map/ppermute | solution.py:127
  70.3 2.2 %gather_fusion = bf16[64,80,256]{2,1,0:T(8,128)(2,1)} fusion(bf16[64,80,256]{2,1,0:T(8,128)(2,1)S(1)} %bitcast.87, s32[1024]{0:T(1024)S(1)} %pad_clamp_fusion.2), kind=kCustom, calls=%fused_computation | custom fusion | bytes 5243136 | tf_op jit(solution)/shard_map/gather | solution.py:194
  72.4 16.2 %shard_map.84 = (bf16[640,128]{1,0:T(8,128)(2,1)}, bf16[640,128]{1,0:T(8,128)(2,1)}, f32[5120,256]{1,0:T(8,128)}) custom-call(s32[4]{0:T(128)} %pad_add_fusion.limits_ref, bf16[640,128]{1,0:T(8,128)(2,1)} %bitcast.91, bf16[640,128]{1,0:T(8,128)(2,1)} %bitcast.92, bf16[5120,256]{1,0:T(8,128)(2,1)} %bitcast.88, s32[640,1]{1,0:T(8,128)} %reshape.248.qpos_ref), custom_call_target="tpu_custom_call" | custom-call | flops 2936012800 | bytes 7864320 | tf_op jit(solution)/shard_map/pallas_call | solution.py:135
  88.7 5.7 %gather_fusion.2 = f32[64,80,256]{2,1,0:T(8,128)} fusion(f32[64,80,256]{2,1,0:T(8,128)} %bitcast.86, s32[1024]{0:T(1024)S(1)} %pad_clamp_fusion), kind=kCustom, calls=%fused_computation.2 | custom fusion | bytes 10486016 | tf_op jit(solution)/shard_map/gather | solution.py:231
  97.7 8.3 %collective-permute-done.7 = bf16[4,160,256]{2,1,0:T(8,128)(2,1)S(1)} collective-permute-done((bf16[4,160,256]{2,1,0:T(8,128)(2,1)S(1)}, bf16[4,160,256]{2,1,0:T(8,128)(2,1)S(1)}, u32[]{:S(2)}, u32[]{:S(2)}) %collective-permute-start.7) | collective-permute-done | bytes 327712 | tf_op jit(solution)/shard_map/ppermute | solution.py:127
  109.0 5.1 %collective-permute-start.11 = (bf16[4,160,256]{2,1,0:T(8,128)(2,1)S(1)}, bf16[4,160,256]{2,1,0:T(8,128)(2,1)S(1)}, u32[]{:S(2)}, u32[]{:S(2)}) collective-permute-start(bf16[4,160,256]{2,1,0:T(8,128)(2,1)S(1)} %get-tuple-element.13), channel_id=1, source_target_pairs={{0,112},{16,0},{32,16},{48,32},{64,48},{80,64},{96,80},{112,96},{1... | collective-permute-start | bytes 983048 | tf_op jit(solution)/shard_map/ppermute | solution.py:127
  114.2 3.4 %collective-permute-done.8 = bf16[4,160,256]{2,1,0:T(8,128)(2,1)S(1)} collective-permute-done((bf16[4,160,256]{2,1,0:T(8,128)(2,1)S(1)}, bf16[4,160,256]{2,1,0:T(8,128)(2,1)S(1)}, u32[]{:S(2)}, u32[]{:S(2)}) %collective-permute-start.8) | collective-permute-done | bytes 327712 | tf_op jit(solution)/shard_map/ppermute | solution.py:127
  118.8 2.1 %collective-permute-start.9 = (bf16[4,160,256]{2,1,0:T(8,128)(2,1)S(1)}, bf16[4,160,256]{2,1,0:T(8,128)(2,1)S(1)}, u32[]{:S(2)}, u32[]{:S(2)}) collective-permute-start(bf16[4,160,256]{2,1,0:T(8,128)(2,1)S(1)} %fusion.9), channel_id=1, source_target_pairs={{0,16},{16,32},{32,48},{48,64},{64,80},{80,96},{96,112},{112,0},{1... | collective-permute-start | bytes 983048 | tf_op jit(solution)/shard_map/ppermute | solution.py:127
  120.8 8.2 %collective-permute-done.9 = bf16[4,160,256]{2,1,0:T(8,128)(2,1)S(1)} collective-permute-done((bf16[4,160,256]{2,1,0:T(8,128)(2,1)S(1)}, bf16[4,160,256]{2,1,0:T(8,128)(2,1)S(1)}, u32[]{:S(2)}, u32[]{:S(2)}) %collective-permute-start.9) | collective-permute-done | bytes 327712 | tf_op jit(solution)/shard_map/ppermute | solution.py:127
  130.5 1.9 %collective-permute-start.12 = (bf16[4,160,256]{2,1,0:T(8,128)(2,1)S(1)}, bf16[4,160,256]{2,1,0:T(8,128)(2,1)S(1)}, u32[]{:S(2)}, u32[]{:S(2)}) collective-permute-start(bf16[4,160,256]{2,1,0:T(8,128)(2,1)S(1)} %get-tuple-element.11), channel_id=1, source_target_pairs={{0,112},{16,0},{32,16},{48,32},{64,48},{80,64},{96,80},{112,96},{1... | collective-permute-start | bytes 983048 | tf_op jit(solution)/shard_map/ppermute | solution.py:127
  132.5 3.9 %collective-permute-start.10 = (bf16[4,160,256]{2,1,0:T(8,128)(2,1)S(1)}, bf16[4,160,256]{2,1,0:T(8,128)(2,1)S(1)}, u32[]{:S(2)}, u32[]{:S(2)}) collective-permute-start(bf16[4,160,256]{2,1,0:T(8,128)(2,1)S(1)} %get-tuple-element.10), channel_id=1, source_target_pairs={{0,16},{16,32},{32,48},{48,64},{64,80},{80,96},{96,112},{112,0},{1... | collective-permute-start | bytes 983048 | tf_op jit(solution)/shard_map/ppermute | solution.py:127
  136.4 6.2 %collective-permute-done.12 = bf16[4,160,256]{2,1,0:T(8,128)(2,1)S(1)} collective-permute-done((bf16[4,160,256]{2,1,0:T(8,128)(2,1)S(1)}, bf16[4,160,256]{2,1,0:T(8,128)(2,1)S(1)}, u32[]{:S(2)}, u32[]{:S(2)}) %collective-permute-start.12) | collective-permute-done | bytes 327712 | tf_op jit(solution)/shard_map/ppermute | solution.py:127
  143.7 2.6 %collective-permute-start.13 = (bf16[4,160,256]{2,1,0:T(8,128)(2,1)S(1)}, bf16[4,160,256]{2,1,0:T(8,128)(2,1)S(1)}, u32[]{:S(2)}, u32[]{:S(2)}) collective-permute-start(bf16[4,160,256]{2,1,0:T(8,128)(2,1)S(1)} %fusion.3), channel_id=1, source_target_pairs={{0,112},{16,0},{32,16},{48,32},{64,48},{80,64},{96,80},{112,96},{1... | collective-permute-start | bytes 983048 | tf_op jit(solution)/shard_map/ppermute | solution.py:127
  146.3 6.4 %collective-permute-done.13 = bf16[4,160,256]{2,1,0:T(8,128)(2,1)S(1)} collective-permute-done((bf16[4,160,256]{2,1,0:T(8,128)(2,1)S(1)}, bf16[4,160,256]{2,1,0:T(8,128)(2,1)S(1)}, u32[]{:S(2)}, u32[]{:S(2)}) %collective-permute-start.13) | collective-permute-done | bytes 327712 | tf_op jit(solution)/shard_map/ppermute | solution.py:127
  152.7 1.9 %fusion.1 = bf16[4,160,256]{2,1,0:T(8,128)(2,1)} fusion(f32[4,8,160,256]{3,2,1,0:T(8,128)} %bitcast.85, bf16[4,160,256]{2,1,0:T(8,128)(2,1)S(1)} %collective-permute-done.13, bf16[4,160,256]{2,1,0:T(8,128)(2,1)S(1)} %collective-permute-done.10), kind=kLoop, calls=%fused_computation.6 | loop fusion | flops 819200 | bytes 1638400 | tf_op jit(solution)/shard_map/convert_element_type | solution.py:246
  154.6 11.2 %all-to-all-start = ((bf16[4,160,256]{2,1,0:T(8,128)(2,1)}), bf16[4,160,256]{2,1,0:T(8,128)(2,1)S(1)}, u32[]{:S(2)}, u32[]{:S(2)}) async-start(bf16[4,160,256]{2,1,0:T(8,128)(2,1)} %fusion.1), calls=%async_computation | async-start | bytes 655360 | tf_op jit(solution)/shard_map/all_to_all | solution.py:246
  167.4 8.2 %all-to-all-done = bf16[4,160,256]{2,1,0:T(8,128)(2,1)S(1)} async-done(((bf16[4,160,256]{2,1,0:T(8,128)(2,1)}), bf16[4,160,256]{2,1,0:T(8,128)(2,1)S(1)}, u32[]{:S(2)}, u32[]{:S(2)}) %all-to-all-start) | async-done | bytes 327712 | tf_op jit(solution)/shard_map/all_to_all | solution.py:246
  (70 shorter events, 29.8 us)
Async XLA Ops:
  0.6 33.2 %copy-start = (s32[64]{0:T(128)S(1)}, s32[64]{0:T(128)}, u32[]{:S(2)}) copy-start(s32[64]{0:T(128)} %param.9) | copy-start | bytes 772
  21.5 16.3 %collective-permute-start.3 = (bf16[640,256]{1,0:T(8,128)(2,1)S(1)}, bf16[640,256]{1,0:T(8,128)(2,1)}, u32[]{:S(2)}, u32[]{:S(2)}) collective-permute-start(bf16[640,256]{1,0:T(8,128)(2,1)S(1)} %all_gather.3), channel_id=1, source_target_pairs={{0,16},{16,32},{32,48},{48,64},{64,80},{80,96},{96,112},{112,0},{1... | collective-permute-start | bytes 983048 | tf_op jit(solution)/shard_map/ppermute | solution.py:127
  24.9 15.6 %collective-permute-start = (bf16[640,256]{1,0:T(8,128)(2,1)S(1)}, bf16[640,256]{1,0:T(8,128)(2,1)}, u32[]{:S(2)}, u32[]{:S(2)}) collective-permute-start(bf16[640,256]{1,0:T(8,128)(2,1)S(1)} %all_gather.3), channel_id=1, source_target_pairs={{0,112},{16,0},{32,16},{48,32},{64,48},{80,64},{96,80},{112,96},{1... | collective-permute-start | bytes 983048 | tf_op jit(solution)/shard_map/ppermute | solution.py:127
  33.9 1.0 copy-start.1
  37.8 11.0 %collective-permute-start.4 = (bf16[640,256]{1,0:T(8,128)(2,1)}, bf16[640,256]{1,0:T(8,128)(2,1)S(1)}, u32[]{:S(2)}, u32[]{:S(2)}) collective-permute-start(bf16[640,256]{1,0:T(8,128)(2,1)} %collective-permute-done.3), channel_id=1, source_target_pairs={{0,16},{16,32},{32,48},{48,64},{64,80},{80,96},{96,112},{112,0},{1... | collective-permute-start | bytes 983048 | tf_op jit(solution)/shard_map/ppermute | solution.py:127
  40.5 10.9 %collective-permute-start.1 = (bf16[640,256]{1,0:T(8,128)(2,1)}, bf16[640,256]{1,0:T(8,128)(2,1)S(1)}, u32[]{:S(2)}, u32[]{:S(2)}) collective-permute-start(bf16[640,256]{1,0:T(8,128)(2,1)} %collective-permute-done), channel_id=1, source_target_pairs={{0,112},{16,0},{32,16},{48,32},{64,48},{80,64},{96,80},{112,96},{1... | collective-permute-start | bytes 983048 | tf_op jit(solution)/shard_map/ppermute | solution.py:127
  48.8 10.2 %collective-permute-start.5 = (bf16[640,256]{1,0:T(8,128)(2,1)S(1)}, bf16[640,256]{1,0:T(8,128)(2,1)S(1)}, u32[]{:S(2)}, u32[]{:S(2)}) collective-permute-start(bf16[640,256]{1,0:T(8,128)(2,1)S(1)} %collective-permute-done.4), channel_id=1, source_target_pairs={{0,16},{16,32},{32,48},{48,64},{64,80},{80,96},{96,112},{112,0},{1... | collective-permute-start | bytes 983048 | tf_op jit(solution)/shard_map/ppermute | solution.py:127
  51.5 10.5 %collective-permute-start.2 = (bf16[640,256]{1,0:T(8,128)(2,1)S(1)}, bf16[640,256]{1,0:T(8,128)(2,1)S(1)}, u32[]{:S(2)}, u32[]{:S(2)}) collective-permute-start(bf16[640,256]{1,0:T(8,128)(2,1)S(1)} %collective-permute-done.1), channel_id=1, source_target_pairs={{0,112},{16,0},{32,16},{48,32},{64,48},{80,64},{96,80},{112,96},{1... | collective-permute-start | bytes 983048 | tf_op jit(solution)/shard_map/ppermute | solution.py:127
  59.0 10.2 %collective-permute-start.6 = (bf16[640,256]{1,0:T(8,128)(2,1)S(1)}, bf16[640,256]{1,0:T(8,128)(2,1)S(1)}, u32[]{:S(2)}, u32[]{:S(2)}) collective-permute-start(bf16[640,256]{1,0:T(8,128)(2,1)S(1)} %collective-permute-done.5), channel_id=1, source_target_pairs={{0,16},{16,32},{32,48},{48,64},{64,80},{80,96},{96,112},{112,0},{1... | collective-permute-start | bytes 983048 | tf_op jit(solution)/shard_map/ppermute | solution.py:127
  95.8 10.2 %collective-permute-start.7 = (bf16[4,160,256]{2,1,0:T(8,128)(2,1)S(1)}, bf16[4,160,256]{2,1,0:T(8,128)(2,1)S(1)}, u32[]{:S(2)}, u32[]{:S(2)}) collective-permute-start(bf16[4,160,256]{2,1,0:T(8,128)(2,1)S(1)} %get-tuple-element.12), channel_id=1, source_target_pairs={{0,16},{16,32},{32,48},{48,64},{64,80},{80,96},{96,112},{112,0},{1... | collective-permute-start | bytes 983048 | tf_op jit(solution)/shard_map/ppermute | solution.py:127
  107.1 10.5 %collective-permute-start.8 = (bf16[4,160,256]{2,1,0:T(8,128)(2,1)S(1)}, bf16[4,160,256]{2,1,0:T(8,128)(2,1)S(1)}, u32[]{:S(2)}, u32[]{:S(2)}) collective-permute-start(bf16[4,160,256]{2,1,0:T(8,128)(2,1)S(1)} %fusion.11), channel_id=1, source_target_pairs={{0,16},{16,32},{32,48},{48,64},{64,80},{80,96},{96,112},{112,0},{1... | collective-permute-start | bytes 983048 | tf_op jit(solution)/shard_map/ppermute | solution.py:127
  109.0 11.8 %collective-permute-start.11 = (bf16[4,160,256]{2,1,0:T(8,128)(2,1)S(1)}, bf16[4,160,256]{2,1,0:T(8,128)(2,1)S(1)}, u32[]{:S(2)}, u32[]{:S(2)}) collective-permute-start(bf16[4,160,256]{2,1,0:T(8,128)(2,1)S(1)} %get-tuple-element.13), channel_id=1, source_target_pairs={{0,112},{16,0},{32,16},{48,32},{64,48},{80,64},{96,80},{112,96},{1... | collective-permute-start | bytes 983048 | tf_op jit(solution)/shard_map/ppermute | solution.py:127
  118.8 47.0 %copy-start.2 = (bf16[640,128]{1,0:T(8,128)(2,1)S(1)}, bf16[640,128]{1,0:T(8,128)(2,1)}, u32[]{:S(2)}) copy-start(bf16[640,128]{1,0:T(8,128)(2,1)} %get-tuple-element.7) | copy-start | bytes 491524
  118.8 47.0 %copy-start.3 = (bf16[640,128]{1,0:T(8,128)(2,1)S(1)}, bf16[640,128]{1,0:T(8,128)(2,1)}, u32[]{:S(2)}) copy-start(bf16[640,128]{1,0:T(8,128)(2,1)} %get-tuple-element.8) | copy-start | bytes 491524
  118.8 10.3 %collective-permute-start.9 = (bf16[4,160,256]{2,1,0:T(8,128)(2,1)S(1)}, bf16[4,160,256]{2,1,0:T(8,128)(2,1)S(1)}, u32[]{:S(2)}, u32[]{:S(2)}) collective-permute-start(bf16[4,160,256]{2,1,0:T(8,128)(2,1)S(1)} %fusion.9), channel_id=1, source_target_pairs={{0,16},{16,32},{32,48},{48,64},{64,80},{80,96},{96,112},{112,0},{1... | collective-permute-start | bytes 983048 | tf_op jit(solution)/shard_map/ppermute | solution.py:127
  130.5 12.0 %collective-permute-start.12 = (bf16[4,160,256]{2,1,0:T(8,128)(2,1)S(1)}, bf16[4,160,256]{2,1,0:T(8,128)(2,1)S(1)}, u32[]{:S(2)}, u32[]{:S(2)}) collective-permute-start(bf16[4,160,256]{2,1,0:T(8,128)(2,1)S(1)} %get-tuple-element.11), channel_id=1, source_target_pairs={{0,112},{16,0},{32,16},{48,32},{64,48},{80,64},{96,80},{112,96},{1... | collective-permute-start | bytes 983048 | tf_op jit(solution)/shard_map/ppermute | solution.py:127
  132.5 13.8 %collective-permute-start.10 = (bf16[4,160,256]{2,1,0:T(8,128)(2,1)S(1)}, bf16[4,160,256]{2,1,0:T(8,128)(2,1)S(1)}, u32[]{:S(2)}, u32[]{:S(2)}) collective-permute-start(bf16[4,160,256]{2,1,0:T(8,128)(2,1)S(1)} %get-tuple-element.10), channel_id=1, source_target_pairs={{0,16},{16,32},{32,48},{48,64},{64,80},{80,96},{96,112},{112,0},{1... | collective-permute-start | bytes 983048 | tf_op jit(solution)/shard_map/ppermute | solution.py:127
  143.7 9.0 %collective-permute-start.13 = (bf16[4,160,256]{2,1,0:T(8,128)(2,1)S(1)}, bf16[4,160,256]{2,1,0:T(8,128)(2,1)S(1)}, u32[]{:S(2)}, u32[]{:S(2)}) collective-permute-start(bf16[4,160,256]{2,1,0:T(8,128)(2,1)S(1)} %fusion.3), channel_id=1, source_target_pairs={{0,112},{16,0},{32,16},{48,32},{64,48},{80,64},{96,80},{112,96},{1... | collective-permute-start | bytes 983048 | tf_op jit(solution)/shard_map/ppermute | solution.py:127
  154.6 21.0 %all-to-all-start = ((bf16[4,160,256]{2,1,0:T(8,128)(2,1)}), bf16[4,160,256]{2,1,0:T(8,128)(2,1)S(1)}, u32[]{:S(2)}, u32[]{:S(2)}) async-start(bf16[4,160,256]{2,1,0:T(8,128)(2,1)} %fusion.1), calls=%async_computation | async-start | bytes 655360 | tf_op jit(solution)/shard_map/all_to_all | solution.py:246

commit v8 on v6

--- a/solution.py
+++ b/solution.py
@@ -19,11 +19,19 @@
 
 
 def attention_kernel(
-    limits_ref, q_ref, g_ref, kv_ref, qpos_ref,
-    out_ref, dq_ref, dkv_ref,
-    top_ref, total_ref, acc_ref, lse_ref, dot_ref, dqacc_ref,
+    limits_ref, source_ref, target_ref, q_ref, g_ref, kv_in_ref, qpos_ref,
+    out_ref, dq_ref, dkv_out_ref,
+    top_ref, total_ref, acc_ref, lse_ref, dot_ref, dqacc_ref, kv_ref, dkv_ref,
 ):
     rows = q_ref.shape[0]
+    spans = source_ref.shape[0]
+
+    def sort_span(span, carry):
+        source = pl.multiple_of(source_ref[span] * SPAN, 16)
+        kv_ref[pl.ds(pl.multiple_of(span * SPAN, 16), SPAN), :] = kv_in_ref[pl.ds(source, SPAN), :]
+        return carry
+
+    lax.fori_loop(0, spans, sort_span, 0)
     half = rows // 2
     width = HEAD_DIM
     scale = 1.0 / math.sqrt(width)
@@ -121,15 +129,23 @@
     lax.fori_loop(early_blocks, late_blocks, bwd_late, 0)
     dq_ref[...] = (dqacc_ref[...] * scale).astype(jnp.bfloat16)
 
+    def place_span(span, carry):
+        target = pl.multiple_of(target_ref[span] * SPAN, 16)
+        block = dkv_ref[pl.ds(pl.multiple_of(span * SPAN, 16), SPAN), :]
+        dkv_out_ref[pl.ds(target, SPAN), :] = block.astype(jnp.bfloat16)
+        return carry
+
+    lax.fori_loop(0, spans, place_span, 0)
+
 
 def shifted(array, axis, by):
     length = lax.axis_size(axis)
     return lax.ppermute(array, axis, [(i, (i + by) % length) for i in range(length)])
 
 
-def local_attention(limits, q_rows, g_rows, kv_sorted, q_pos):
+def local_attention(limits, source, target, q_rows, g_rows, kv_gathered, q_pos):
     rows, width = q_rows.shape
-    keys = kv_sorted.shape[0]
+    keys = kv_gathered.shape[0]
     vmem = pltpu.VMEM
     flops = 2 * rows * keys * width * 7 // 2
     return pl.pallas_call(
@@ -137,10 +153,12 @@
         out_shape=(
             jax.ShapeDtypeStruct((rows, width), jnp.bfloat16),
             jax.ShapeDtypeStruct((rows, width), jnp.bfloat16),
-            jax.ShapeDtypeStruct((keys, 2 * width), jnp.float32),
+            jax.ShapeDtypeStruct((keys, 2 * width), jnp.bfloat16),
         ),
         in_specs=[
             pl.BlockSpec(memory_space=pltpu.SMEM),
+            pl.BlockSpec(memory_space=pltpu.SMEM),
+            pl.BlockSpec(memory_space=pltpu.SMEM),
             pl.BlockSpec(memory_space=vmem),
             pl.BlockSpec(memory_space=vmem),
             pl.BlockSpec(memory_space=vmem),
@@ -158,11 +176,13 @@
             pltpu.VMEM((rows, 1), jnp.float32),
             pltpu.VMEM((rows, 1), jnp.float32),
             pltpu.VMEM((rows, width), jnp.float32),
+            pltpu.VMEM((keys, 2 * width), jnp.bfloat16),
+            pltpu.VMEM((keys, 2 * width), jnp.float32),
         ],
         cost_estimate=pl.CostEstimate(
             flops=flops, transcendentals=rows * keys, bytes_accessed=keys * width * 12
         ),
-    )(limits, q_rows, g_rows, kv_sorted, q_pos)
+    )(limits, source, target, q_rows, g_rows, kv_gathered, q_pos)
 
 
 def on_device(queries, keys, values, out_grad, order):
@@ -191,7 +211,6 @@
     holder = inverse // 2
     distance = (holder % inner - my_y + inner) % inner
     gathered_at = 2 * (distance * outer + holder // inner) + inverse % 2
-    kv_sorted = kv_all.reshape(span_count, SPAN, 2 * width)[gathered_at].reshape(span_count * SPAN, 2 * width)
 
     pair = lax.dynamic_slice_in_dim(order, 2 * my_index, 2)
     low_first = pair[0] < pair[1]
@@ -221,11 +240,11 @@
     span_pos = jnp.stack([my_low, span_count - 1 - my_low])[:, None] * SPAN + offsets[None, :]
     q_pos = jnp.broadcast_to(span_pos[:, None, :], (2, q_heads, SPAN)).reshape(-1, 1)
 
-    attention_rows, dq_rows, dkv_sorted = local_attention(
-        limits, to_rows(queries), to_rows(out_grad), kv_sorted, q_pos
-    )
-    dkv_all = dkv_sorted.reshape(span_count, SPAN, 2 * width)[order].reshape(outer, inner, 2 * SPAN, 2 * width)
-    row_parts = lax.all_to_all(dkv_all.astype(jnp.bfloat16), "y", 1, 1, tiled=False)
+    attention_rows, dq_rows, dkv_placed = local_attention(
+        limits, gathered_at, inverse, to_rows(queries), to_rows(out_grad), kv_all, q_pos
+    )
+    dkv_all = dkv_placed.reshape(outer, inner, 2 * SPAN, 2 * width)
+    row_parts = lax.all_to_all(dkv_all, "y", 1, 1, tiled=False)
     row_sums = jnp.sum(row_parts.astype(jnp.float32), axis=1)
     dkv_parts = lax.all_to_all(row_sums.astype(jnp.bfloat16), "zh", 0, 0, tiled=False)
     dkv_mine = jnp.sum(dkv_parts.astype(jnp.float32), axis=0)

time: 172 us -> 169 us (0.983)
  local copies, waits for them, and re-layouts: 14.9 us -> 10.7 us
  Pallas kernels: 16.8 us -> 19.5 us
  blocking collectives: 82.8 us -> 80.2 us
    gather x2 -> x0, local copies, waits for them, and re-layouts: 5.49 us -> none  [the longest x1 3.29 us: on_device(): dkv_sorted.reshape(span_count, SPAN, 2 * width)[order]]
    pallas_call x1, Pallas kernels: 16.8 us -> 19.5 us  [local_attention(): pl.pallas_call(attention_kernel, out_shape=(jax.ShapeDtypeStruct((rows, w...]
    all_to_all x1, blocking collectives: 62.8 us -> 60.2 us  [on_device(): row_parts = lax.all_to_all(dkv_all, 'y', 1, 1, tiled=False)]
    reshape x0 -> x1, local copies, waits for them, and re-layouts: none -> 1.94 us  [on_device(): dkv_all = dkv_placed.reshape(outer, inner, 2 * SPAN, 2 * width)]
  transfers between devices with their start and end apart: 8 -> 8, of which waited for: 4 -> 5; matrix products, arithmetic and copies ran while one was open for 6% -> 6% of each run, Pallas kernels for 0% -> 0%
where the time goes in v8:
time: 169 us
  blocking collectives  80.2 us (47%)
  starting transfers between devices  26.7 us (16%)
  waiting for transfers between devices  21.8 us (13%)
  Pallas kernels  19.5 us (12%)
  local copies, waits for them, and re-layouts  10.7 us (6%)
  other arithmetic  6.12 us (4%)
  between operations  3.46 us (2%)
    all_to_all x1, blocking collectives, on_device(): row_parts = lax.all_to_all(dkv_all, 'y', 1, 1, tiled=False)  60.2 us
    ppermute x7, starting transfers between devices, shifted(): lax.ppermute(array, axis, [(i, (i + by) % length) for i in range(length)])  23.3 us
    all_gather x1, blocking collectives, on_device(): column = lax.all_gather(kv_local, 'zh', axis=0, tiled=True)  20 us
    pallas_call x1, Pallas kernels, local_attention(): pl.pallas_call(attention_kernel, out_shape=(jax.ShapeDtypeStruct((rows, w...  19.5 us
    ppermute x7, waiting for transfers between devices, shifted(): lax.ppermute(array, axis, [(i, (i + by) % length) for i in range(length)])  13.1 us
    all_to_all x1, waiting for transfers between devices, on_device(): lax.all_to_all(row_sums.astype(jnp.bfloat16), 'zh', 0, 0, tiled=False)  8.71 us
    all_to_all x1, starting transfers between devices, on_device(): lax.all_to_all(row_sums.astype(jnp.bfloat16), 'zh', 0, 0, tiled=False)  3.48 us
  transfers between devices with their start and end apart: 8, of which 5 were waited for; matrix products, arithmetic and copies ran while one was open for 6% of the time, Pallas kernels for 0%

profile of v8, /device:TPU:6, one launch (start us, length us, event | category | flops | bytes accessed | tf_op | source)
XLA Modules:
  0.0 168.6 jit_solution(6969982051048682543)
XLA Ops:
  0.6 0.8 pad_maximum_fusion
  1.4 20.0 %all_gather.3 = bf16[640,256]{1,0:T(8,128)(2,1)S(1)} all-gather(bf16[160,256]{1,0:T(8,128)(2,1)S(1)} %pad_maximum_fusion), channel_id=1, replica_groups=mesh['zh'=4,'y'=8,'head'=16] {'zh'}, dimensions={0}, use_global_device_ids=true | all-gather | bytes 409600 | tf_op jit(solution)/shard_map/all_gather | solution.py:200
  21.4 5.4 %collective-permute-start = (bf16[640,256]{1,0:T(8,128)(2,1)S(1)}, bf16[640,256]{1,0:T(8,128)(2,1)S(1)}, u32[]{:S(2)}, u32[]{:S(2)}) collective-permute-start(bf16[640,256]{1,0:T(8,128)(2,1)S(1)} %all_gather.3), channel_id=1, source_target_pairs={{0,112},{16,0},{32,16},{48,32},{64,48},{80,64},{96,80},{112,96},{1... | collective-permute-start | bytes 983048 | tf_op jit(solution)/shard_map/ppermute | solution.py:143
  26.8 1.9 %collective-permute-start.3 = (bf16[640,256]{1,0:T(8,128)(2,1)S(1)}, bf16[640,256]{1,0:T(8,128)(2,1)S(1)}, u32[]{:S(2)}, u32[]{:S(2)}) collective-permute-start(bf16[640,256]{1,0:T(8,128)(2,1)S(1)} %all_gather.3), channel_id=1, source_target_pairs={{0,16},{16,32},{32,48},{48,64},{64,80},{80,96},{96,112},{112,0},{1... | collective-permute-start | bytes 983048 | tf_op jit(solution)/shard_map/ppermute | solution.py:143
  28.7 0.7 dynamic_slice.3
  32.7 1.0 reshape.97
  35.2 1.0 reshape.99
  36.2 0.9 reshape.116.qpos_ref
  37.1 0.8 scatter_custom_fusion.target_ref
  37.9 2.0 %collective-permute-start.4 = (bf16[640,256]{1,0:T(8,128)(2,1)S(1)}, bf16[640,256]{1,0:T(8,128)(2,1)S(1)}, u32[]{:S(2)}, u32[]{:S(2)}) collective-permute-start(bf16[640,256]{1,0:T(8,128)(2,1)S(1)} %collective-permute-done.3), channel_id=1, source_target_pairs={{0,16},{16,32},{32,48},{48,64},{64,80},{80,96},{96,112},{112,0},{1... | collective-permute-start | bytes 983048 | tf_op jit(solution)/shard_map/ppermute | solution.py:143
  40.6 5.0 %collective-permute-start.1 = (bf16[640,256]{1,0:T(8,128)(2,1)S(1)}, bf16[640,256]{1,0:T(8,128)(2,1)S(1)}, u32[]{:S(2)}, u32[]{:S(2)}) collective-permute-start(bf16[640,256]{1,0:T(8,128)(2,1)S(1)} %collective-permute-done), channel_id=1, source_target_pairs={{0,112},{16,0},{32,16},{48,32},{64,48},{80,64},{96,80},{112,96},{1... | collective-permute-start | bytes 983048 | tf_op jit(solution)/shard_map/ppermute | solution.py:143
  45.7 3.0 %collective-permute-done.4 = bf16[640,256]{1,0:T(8,128)(2,1)S(1)} collective-permute-done((bf16[640,256]{1,0:T(8,128)(2,1)S(1)}, bf16[640,256]{1,0:T(8,128)(2,1)S(1)}, u32[]{:S(2)}, u32[]{:S(2)}) %collective-permute-start.4) | collective-permute-done | bytes 327712 | tf_op jit(solution)/shard_map/ppermute | solution.py:143
  48.7 1.9 %collective-permute-start.5 = (bf16[640,256]{1,0:T(8,128)(2,1)S(1)}, bf16[640,256]{1,0:T(8,128)(2,1)S(1)}, u32[]{:S(2)}, u32[]{:S(2)}) collective-permute-start(bf16[640,256]{1,0:T(8,128)(2,1)S(1)} %collective-permute-done.4), channel_id=1, source_target_pairs={{0,16},{16,32},{32,48},{48,64},{64,80},{80,96},{96,112},{112,0},{1... | collective-permute-start | bytes 983048 | tf_op jit(solution)/shard_map/ppermute | solution.py:143
  51.3 5.1 %collective-permute-start.2 = (bf16[640,256]{1,0:T(8,128)(2,1)S(1)}, bf16[640,256]{1,0:T(8,128)(2,1)S(1)}, u32[]{:S(2)}, u32[]{:S(2)}) collective-permute-start(bf16[640,256]{1,0:T(8,128)(2,1)S(1)} %collective-permute-done.1), channel_id=1, source_target_pairs={{0,112},{16,0},{32,16},{48,32},{64,48},{80,64},{96,80},{112,96},{1... | collective-permute-start | bytes 983048 | tf_op jit(solution)/shard_map/ppermute | solution.py:143
  57.0 1.9 %collective-permute-done.5 = bf16[640,256]{1,0:T(8,128)(2,1)S(1)} collective-permute-done((bf16[640,256]{1,0:T(8,128)(2,1)S(1)}, bf16[640,256]{1,0:T(8,128)(2,1)S(1)}, u32[]{:S(2)}, u32[]{:S(2)}) %collective-permute-start.5) | collective-permute-done | bytes 327712 | tf_op jit(solution)/shard_map/ppermute | solution.py:143
  58.9 1.9 %collective-permute-start.6 = (bf16[640,256]{1,0:T(8,128)(2,1)S(1)}, bf16[640,256]{1,0:T(8,128)(2,1)S(1)}, u32[]{:S(2)}, u32[]{:S(2)}) collective-permute-start(bf16[640,256]{1,0:T(8,128)(2,1)S(1)} %collective-permute-done.5), channel_id=1, source_target_pairs={{0,16},{16,32},{32,48},{48,64},{64,80},{80,96},{96,112},{112,0},{1... | collective-permute-start | bytes 983048 | tf_op jit(solution)/shard_map/ppermute | solution.py:143
  61.0 8.1 %collective-permute-done.6 = bf16[640,256]{1,0:T(8,128)(2,1)S(1)} collective-permute-done((bf16[640,256]{1,0:T(8,128)(2,1)S(1)}, bf16[640,256]{1,0:T(8,128)(2,1)S(1)}, u32[]{:S(2)}, u32[]{:S(2)}) %collective-permute-start.6) | collective-permute-done | bytes 327712 | tf_op jit(solution)/shard_map/ppermute | solution.py:143
  69.2 1.5 copy-done.2
  70.7 19.5 %shard_map.84 = (bf16[640,128]{1,0:T(8,128)(2,1)}, bf16[640,128]{1,0:T(8,128)(2,1)}, bf16[5120,256]{1,0:T(8,128)(2,1)}) custom-call(s32[4]{0:T(128)} %pad_add_fusion.limits_ref, s32[64]{0:T(128)} %fusion.1.source_ref, s32[64]{0:T(128)} %copy-done.3, bf16[640,128]{1,0:T(8,128)(2,1)} %bitcast.31, bf16[640,128]{1,0:T(8,128)(2,1)} %bitcast.32, ...), custom_call_target="tpu_custom_call" | custom-call | flops 2936012800 | bytes 7864320 | tf_op jit(solution)/shard_map/pallas_call | solution.py:151
  90.1 1.9 %copy.37 = bf16[4,8,160,256]{3,2,0,1:T(8,128)(2,1)S(1)} copy(bf16[4,8,160,256]{3,2,1,0:T(8,128)(2,1)} %bitcast.28) | data formatting | bytes 5242880 | tf_op jit(solution)/shard_map/reshape | solution.py:246
  92.1 60.2 %all_to_all.10 = bf16[4,8,160,256]{3,2,0,1:T(8,128)(2,1)S(1)} all-to-all(bf16[4,8,160,256]{3,2,0,1:T(8,128)(2,1)S(1)} %copy.37), channel_id=1, replica_groups=mesh['zh'=4,'y'=8,'head'=16] {'y'}, dimensions={1} | all-to-all | bytes 5242880 | tf_op jit(solution)/shard_map/all_to_all | solution.py:247
  152.3 1.2 reduce_sum.21
  153.5 3.5 %all-to-all-start.1 = ((bf16[4,160,256]{2,1,0:T(8,128)(2,1)}), bf16[4,160,256]{2,1,0:T(8,128)(2,1)S(1)}, u32[]{:S(2)}, u32[]{:S(2)}) async-start(bf16[4,160,256]{2,1,0:T(8,128)(2,1)} %reduce_sum.21), calls=%async_computation.1 | async-start | bytes 655360 | tf_op jit(solution)/shard_map/all_to_all | solution.py:249
  158.6 8.7 %all-to-all-done.1 = bf16[4,160,256]{2,1,0:T(8,128)(2,1)S(1)} async-done(((bf16[4,160,256]{2,1,0:T(8,128)(2,1)}), bf16[4,160,256]{2,1,0:T(8,128)(2,1)S(1)}, u32[]{:S(2)}, u32[]{:S(2)}) %all-to-all-start.1) | async-done | bytes 327712 | tf_op jit(solution)/shard_map/all_to_all | solution.py:249
  (39 shorter events, 7.2 us)
Async XLA Ops:
  21.4 19.2 %collective-permute-start = (bf16[640,256]{1,0:T(8,128)(2,1)S(1)}, bf16[640,256]{1,0:T(8,128)(2,1)S(1)}, u32[]{:S(2)}, u32[]{:S(2)}) collective-permute-start(bf16[640,256]{1,0:T(8,128)(2,1)S(1)} %all_gather.3), channel_id=1, source_target_pairs={{0,112},{16,0},{32,16},{48,32},{64,48},{80,64},{96,80},{112,96},{1... | collective-permute-start | bytes 983048 | tf_op jit(solution)/shard_map/ppermute | solution.py:143
  26.8 11.0 %collective-permute-start.3 = (bf16[640,256]{1,0:T(8,128)(2,1)S(1)}, bf16[640,256]{1,0:T(8,128)(2,1)S(1)}, u32[]{:S(2)}, u32[]{:S(2)}) collective-permute-start(bf16[640,256]{1,0:T(8,128)(2,1)S(1)} %all_gather.3), channel_id=1, source_target_pairs={{0,16},{16,32},{32,48},{48,64},{64,80},{80,96},{96,112},{112,0},{1... | collective-permute-start | bytes 983048 | tf_op jit(solution)/shard_map/ppermute | solution.py:143
  37.8 31.3 %copy-start.3 = (s32[64]{0:T(128)}, s32[64]{0:T(128)S(1)}, u32[]{:S(2)}) copy-start(s32[64]{0:T(128)S(1)} %scatter_custom_fusion.target_ref) | copy-start | bytes 772
  37.9 10.8 %collective-permute-start.4 = (bf16[640,256]{1,0:T(8,128)(2,1)S(1)}, bf16[640,256]{1,0:T(8,128)(2,1)S(1)}, u32[]{:S(2)}, u32[]{:S(2)}) collective-permute-start(bf16[640,256]{1,0:T(8,128)(2,1)S(1)} %collective-permute-done.3), channel_id=1, source_target_pairs={{0,16},{16,32},{32,48},{48,64},{64,80},{80,96},{96,112},{112,0},{1... | collective-permute-start | bytes 983048 | tf_op jit(solution)/shard_map/ppermute | solution.py:143
  40.6 10.6 %collective-permute-start.1 = (bf16[640,256]{1,0:T(8,128)(2,1)S(1)}, bf16[640,256]{1,0:T(8,128)(2,1)S(1)}, u32[]{:S(2)}, u32[]{:S(2)}) collective-permute-start(bf16[640,256]{1,0:T(8,128)(2,1)S(1)} %collective-permute-done), channel_id=1, source_target_pairs={{0,112},{16,0},{32,16},{48,32},{64,48},{80,64},{96,80},{112,96},{1... | collective-permute-start | bytes 983048 | tf_op jit(solution)/shard_map/ppermute | solution.py:143
  48.7 10.2 %collective-permute-start.5 = (bf16[640,256]{1,0:T(8,128)(2,1)S(1)}, bf16[640,256]{1,0:T(8,128)(2,1)S(1)}, u32[]{:S(2)}, u32[]{:S(2)}) collective-permute-start(bf16[640,256]{1,0:T(8,128)(2,1)S(1)} %collective-permute-done.4), channel_id=1, source_target_pairs={{0,16},{16,32},{32,48},{48,64},{64,80},{80,96},{96,112},{112,0},{1... | collective-permute-start | bytes 983048 | tf_op jit(solution)/shard_map/ppermute | solution.py:143
  51.3 9.7 %collective-permute-start.2 = (bf16[640,256]{1,0:T(8,128)(2,1)S(1)}, bf16[640,256]{1,0:T(8,128)(2,1)S(1)}, u32[]{:S(2)}, u32[]{:S(2)}) collective-permute-start(bf16[640,256]{1,0:T(8,128)(2,1)S(1)} %collective-permute-done.1), channel_id=1, source_target_pairs={{0,112},{16,0},{32,16},{48,32},{64,48},{80,64},{96,80},{112,96},{1... | collective-permute-start | bytes 983048 | tf_op jit(solution)/shard_map/ppermute | solution.py:143
  58.9 10.2 %collective-permute-start.6 = (bf16[640,256]{1,0:T(8,128)(2,1)S(1)}, bf16[640,256]{1,0:T(8,128)(2,1)S(1)}, u32[]{:S(2)}, u32[]{:S(2)}) collective-permute-start(bf16[640,256]{1,0:T(8,128)(2,1)S(1)} %collective-permute-done.5), channel_id=1, source_target_pairs={{0,16},{16,32},{32,48},{48,64},{64,80},{80,96},{96,112},{112,0},{1... | collective-permute-start | bytes 983048 | tf_op jit(solution)/shard_map/ppermute | solution.py:143
  69.2 1.5 copy-start.2
  152.3 4.6 %copy-start = (bf16[640,128]{1,0:T(8,128)(2,1)S(1)}, bf16[640,128]{1,0:T(8,128)(2,1)}, u32[]{:S(2)}) copy-start(bf16[640,128]{1,0:T(8,128)(2,1)} %get-tuple-element.7) | copy-start | bytes 491524
  152.3 4.6 %copy-start.1 = (bf16[640,128]{1,0:T(8,128)(2,1)S(1)}, bf16[640,128]{1,0:T(8,128)(2,1)}, u32[]{:S(2)}) copy-start(bf16[640,128]{1,0:T(8,128)(2,1)} %get-tuple-element.8) | copy-start | bytes 491524
  153.5 13.8 %all-to-all-start.1 = ((bf16[4,160,256]{2,1,0:T(8,128)(2,1)}), bf16[4,160,256]{2,1,0:T(8,128)(2,1)S(1)}, u32[]{:S(2)}, u32[]{:S(2)}) async-start(bf16[4,160,256]{2,1,0:T(8,128)(2,1)} %reduce_sum.21), calls=%async_computation.1 | async-start | bytes 655360 | tf_op jit(solution)/shard_map/all_to_all | solution.py:249

commit v9 on v8

--- a/solution.py
+++ b/solution.py
@@ -211,6 +211,7 @@
     holder = inverse // 2
     distance = (holder % inner - my_y + inner) % inner
     gathered_at = 2 * (distance * outer + holder // inner) + inverse % 2
+    placed_at = 2 * ((holder % inner) * outer + holder // inner) + inverse % 2
 
     pair = lax.dynamic_slice_in_dim(order, 2 * my_index, 2)
     low_first = pair[0] < pair[1]
@@ -241,11 +242,11 @@
     q_pos = jnp.broadcast_to(span_pos[:, None, :], (2, q_heads, SPAN)).reshape(-1, 1)
 
     attention_rows, dq_rows, dkv_placed = local_attention(
-        limits, gathered_at, inverse, to_rows(queries), to_rows(out_grad), kv_all, q_pos
-    )
-    dkv_all = dkv_placed.reshape(outer, inner, 2 * SPAN, 2 * width)
-    row_parts = lax.all_to_all(dkv_all, "y", 1, 1, tiled=False)
-    row_sums = jnp.sum(row_parts.astype(jnp.float32), axis=1)
+        limits, gathered_at, placed_at, to_rows(queries), to_rows(out_grad), kv_all, q_pos
+    )
+    dkv_all = dkv_placed.reshape(inner, outer, 2 * SPAN, 2 * width)
+    row_parts = lax.all_to_all(dkv_all, "y", 0, 0, tiled=False)
+    row_sums = jnp.sum(row_parts.astype(jnp.float32), axis=0)
     dkv_parts = lax.all_to_all(row_sums.astype(jnp.bfloat16), "zh", 0, 0, tiled=False)
     dkv_mine = jnp.sum(dkv_parts.astype(jnp.float32), axis=0)
     grad_keys = (score_scale * dkv_mine[:, :width]).astype(jnp.bfloat16)

time: 169 us -> 169 us (level)
  blocking collectives: 80.2 us -> 83 us
  Pallas kernels: 19.5 us -> 17.2 us
  local copies, waits for them, and re-layouts: 10.7 us -> 8.8 us
    all_to_all x1, blocking collectives: 60.2 us -> 63 us  [on_device(): row_parts = lax.all_to_all(dkv_all, 'y', 0, 0, tiled=False)]
    pallas_call x1, Pallas kernels: 19.5 us -> 17.2 us  [local_attention(): pl.pallas_call(attention_kernel, out_shape=(jax.ShapeDtypeStruct((rows, w...]
    reshape x1 -> x0, local copies, waits for them, and re-layouts: 1.94 us -> none  [on_device(): dkv_all = dkv_placed.reshape(outer, inner, 2 * SPAN, 2 * width)]
  transfers between devices with their start and end apart: 8 -> 8, of which waited for: 5 -> 4; matrix products, arithmetic and copies ran while one was open for 6% -> 6% of each run, Pallas kernels for 0% -> 0%
where the time goes in v9:
time: 169 us; the launch traced here: 168 us
  blocking collectives  83 us (49%)
  starting transfers between devices  27.2 us (16%)
  waiting for transfers between devices  21.6 us (13%)
  Pallas kernels  17.2 us (10%)
  local copies, waits for them, and re-layouts  8.8 us (5%)
  other arithmetic  6.67 us (4%)
  between operations  3.43 us (2%)
    all_to_all x1, blocking collectives, on_device(): row_parts = lax.all_to_all(dkv_all, 'y', 0, 0, tiled=False)  63 us
    ppermute x7, starting transfers between devices, shifted(): lax.ppermute(array, axis, [(i, (i + by) % length) for i in range(length)])  23.3 us
    all_gather x1, blocking collectives, on_device(): column = lax.all_gather(kv_local, 'zh', axis=0, tiled=True)  20 us
    pallas_call x1, Pallas kernels, local_attention(): pl.pallas_call(attention_kernel, out_shape=(jax.ShapeDtypeStruct((rows, w...  17.2 us
    ppermute x7, waiting for transfers between devices, shifted(): lax.ppermute(array, axis, [(i, (i + by) % length) for i in range(length)])  13.3 us
    all_to_all x1, waiting for transfers between devices, on_device(): lax.all_to_all(row_sums.astype(jnp.bfloat16), 'zh', 0, 0, tiled=False)  8.29 us
    all_to_all x1, starting transfers between devices, on_device(): lax.all_to_all(row_sums.astype(jnp.bfloat16), 'zh', 0, 0, tiled=False)  3.98 us
  transfers between devices with their start and end apart: 8, of which 4 were waited for; matrix products, arithmetic and copies ran while one was open for 6% of the time, Pallas kernels for 0%

profile of v9, /device:TPU:6, one launch (start us, length us, event | category | flops | bytes accessed | tf_op | source)
XLA Modules:
  0.0 167.9 jit_solution(6979285461959865711)
XLA Ops:
  0.6 0.8 pad_maximum_fusion
  1.4 20.0 %all_gather.3 = bf16[640,256]{1,0:T(8,128)(2,1)S(1)} all-gather(bf16[160,256]{1,0:T(8,128)(2,1)S(1)} %pad_maximum_fusion), channel_id=1, replica_groups=mesh['zh'=4,'y'=8,'head'=16] {'zh'}, dimensions={0}, use_global_device_ids=true | all-gather | bytes 409600 | tf_op jit(solution)/shard_map/all_gather | solution.py:200
  21.4 5.4 %collective-permute-start = (bf16[640,256]{1,0:T(8,128)(2,1)S(1)}, bf16[640,256]{1,0:T(8,128)(2,1)S(1)}, u32[]{:S(2)}, u32[]{:S(2)}) collective-permute-start(bf16[640,256]{1,0:T(8,128)(2,1)S(1)} %all_gather.3), channel_id=1, source_target_pairs={{0,112},{16,0},{32,16},{48,32},{64,48},{80,64},{96,80},{112,96},{1... | collective-permute-start | bytes 983048 | tf_op jit(solution)/shard_map/ppermute | solution.py:143
  26.8 1.9 %collective-permute-start.3 = (bf16[640,256]{1,0:T(8,128)(2,1)S(1)}, bf16[640,256]{1,0:T(8,128)(2,1)S(1)}, u32[]{:S(2)}, u32[]{:S(2)}) collective-permute-start(bf16[640,256]{1,0:T(8,128)(2,1)S(1)} %all_gather.3), channel_id=1, source_target_pairs={{0,16},{16,32},{32,48},{48,64},{64,80},{80,96},{96,112},{112,0},{1... | collective-permute-start | bytes 983048 | tf_op jit(solution)/shard_map/ppermute | solution.py:143
  28.7 0.7 dynamic_slice.3
  32.7 1.0 reshape.97
  33.7 1.0 reshape.99
  34.7 0.7 reverse_select_fusion.3
  36.9 0.9 reshape.116.qpos_ref
  37.8 0.8 scatter_custom_fusion
  38.6 2.0 %collective-permute-start.4 = (bf16[640,256]{1,0:T(8,128)(2,1)S(1)}, bf16[640,256]{1,0:T(8,128)(2,1)S(1)}, u32[]{:S(2)}, u32[]{:S(2)}) collective-permute-start(bf16[640,256]{1,0:T(8,128)(2,1)S(1)} %collective-permute-done.3), channel_id=1, source_target_pairs={{0,16},{16,32},{32,48},{48,64},{64,80},{80,96},{96,112},{112,0},{1... | collective-permute-start | bytes 983048 | tf_op jit(solution)/shard_map/ppermute | solution.py:143
  41.2 5.0 %collective-permute-start.1 = (bf16[640,256]{1,0:T(8,128)(2,1)S(1)}, bf16[640,256]{1,0:T(8,128)(2,1)S(1)}, u32[]{:S(2)}, u32[]{:S(2)}) collective-permute-start(bf16[640,256]{1,0:T(8,128)(2,1)S(1)} %collective-permute-done), channel_id=1, source_target_pairs={{0,112},{16,0},{32,16},{48,32},{64,48},{80,64},{96,80},{112,96},{1... | collective-permute-start | bytes 983048 | tf_op jit(solution)/shard_map/ppermute | solution.py:143
  46.3 3.1 %collective-permute-done.4 = bf16[640,256]{1,0:T(8,128)(2,1)S(1)} collective-permute-done((bf16[640,256]{1,0:T(8,128)(2,1)S(1)}, bf16[640,256]{1,0:T(8,128)(2,1)S(1)}, u32[]{:S(2)}, u32[]{:S(2)}) %collective-permute-start.4) | collective-permute-done | bytes 327712 | tf_op jit(solution)/shard_map/ppermute | solution.py:143
  49.4 1.9 %collective-permute-start.5 = (bf16[640,256]{1,0:T(8,128)(2,1)S(1)}, bf16[640,256]{1,0:T(8,128)(2,1)S(1)}, u32[]{:S(2)}, u32[]{:S(2)}) collective-permute-start(bf16[640,256]{1,0:T(8,128)(2,1)S(1)} %collective-permute-done.4), channel_id=1, source_target_pairs={{0,16},{16,32},{32,48},{48,64},{64,80},{80,96},{96,112},{112,0},{1... | collective-permute-start | bytes 983048 | tf_op jit(solution)/shard_map/ppermute | solution.py:143
  51.9 5.1 %collective-permute-start.2 = (bf16[640,256]{1,0:T(8,128)(2,1)S(1)}, bf16[640,256]{1,0:T(8,128)(2,1)S(1)}, u32[]{:S(2)}, u32[]{:S(2)}) collective-permute-start(bf16[640,256]{1,0:T(8,128)(2,1)S(1)} %collective-permute-done.1), channel_id=1, source_target_pairs={{0,112},{16,0},{32,16},{48,32},{64,48},{80,64},{96,80},{112,96},{1... | collective-permute-start | bytes 983048 | tf_op jit(solution)/shard_map/ppermute | solution.py:143
  57.6 2.0 %collective-permute-done.5 = bf16[640,256]{1,0:T(8,128)(2,1)S(1)} collective-permute-done((bf16[640,256]{1,0:T(8,128)(2,1)S(1)}, bf16[640,256]{1,0:T(8,128)(2,1)S(1)}, u32[]{:S(2)}, u32[]{:S(2)}) %collective-permute-start.5) | collective-permute-done | bytes 327712 | tf_op jit(solution)/shard_map/ppermute | solution.py:143
  59.6 1.9 %collective-permute-start.6 = (bf16[640,256]{1,0:T(8,128)(2,1)S(1)}, bf16[640,256]{1,0:T(8,128)(2,1)S(1)}, u32[]{:S(2)}, u32[]{:S(2)}) collective-permute-start(bf16[640,256]{1,0:T(8,128)(2,1)S(1)} %collective-permute-done.5), channel_id=1, source_target_pairs={{0,16},{16,32},{32,48},{48,64},{64,80},{80,96},{96,112},{112,0},{1... | collective-permute-start | bytes 983048 | tf_op jit(solution)/shard_map/ppermute | solution.py:143
  61.6 8.1 %collective-permute-done.6 = bf16[640,256]{1,0:T(8,128)(2,1)S(1)} collective-permute-done((bf16[640,256]{1,0:T(8,128)(2,1)S(1)}, bf16[640,256]{1,0:T(8,128)(2,1)S(1)}, u32[]{:S(2)}, u32[]{:S(2)}) %collective-permute-start.6) | collective-permute-done | bytes 327712 | tf_op jit(solution)/shard_map/ppermute | solution.py:143
  69.9 1.5 copy-done.2
  71.4 17.2 %shard_map.84 = (bf16[640,128]{1,0:T(8,128)(2,1)}, bf16[640,128]{1,0:T(8,128)(2,1)}, bf16[5120,256]{1,0:T(8,128)(2,1)}) custom-call(s32[4]{0:T(128)} %pad_add_fusion.limits_ref, s32[64]{0:T(128)} %multiply_add_fusion.1.source_ref, s32[64]{0:T(128)} %get-tuple-element.10.target_ref, bf16[640,128]{1,0:T(8,128)(2,1)} %bitcast.31, bf16[640,128]{1,0:T(8,128)(2,1)} %bitcast.32, ...), custom_call_target="tpu_custom_call" | custom-call | flops 2936012800 | bytes 7864320 | tf_op jit(solution)/shard_map/pallas_call | solution.py:151
  88.5 63.0 %all_to_all.10 = bf16[8,4,160,256]{3,2,1,0:T(8,128)(2,1)S(1)} all-to-all(bf16[8,4,160,256]{3,2,1,0:T(8,128)(2,1)} %bitcast.28), channel_id=1, replica_groups=mesh['zh'=4,'y'=8,'head'=16] {'y'}, dimensions={0} | all-to-all | bytes 5242880 | tf_op jit(solution)/shard_map/all_to_all | solution.py:248
  151.6 1.2 reduce_sum.21
  152.7 4.0 %all-to-all-start.1 = ((bf16[4,160,256]{2,1,0:T(8,128)(2,1)}), bf16[4,160,256]{2,1,0:T(8,128)(2,1)S(1)}, u32[]{:S(2)}, u32[]{:S(2)}) async-start(bf16[4,160,256]{2,1,0:T(8,128)(2,1)} %reduce_sum.21), calls=%async_computation.1 | async-start | bytes 655360 | tf_op jit(solution)/shard_map/all_to_all | solution.py:250
  158.3 8.3 %all-to-all-done.1 = bf16[4,160,256]{2,1,0:T(8,128)(2,1)S(1)} async-done(((bf16[4,160,256]{2,1,0:T(8,128)(2,1)}), bf16[4,160,256]{2,1,0:T(8,128)(2,1)S(1)}, u32[]{:S(2)}, u32[]{:S(2)}) %all-to-all-start.1) | async-done | bytes 327712 | tf_op jit(solution)/shard_map/all_to_all | solution.py:250
  (37 shorter events, 7.0 us)
Async XLA Ops:
  21.4 19.8 %collective-permute-start = (bf16[640,256]{1,0:T(8,128)(2,1)S(1)}, bf16[640,256]{1,0:T(8,128)(2,1)S(1)}, u32[]{:S(2)}, u32[]{:S(2)}) collective-permute-start(bf16[640,256]{1,0:T(8,128)(2,1)S(1)} %all_gather.3), channel_id=1, source_target_pairs={{0,112},{16,0},{32,16},{48,32},{64,48},{80,64},{96,80},{112,96},{1... | collective-permute-start | bytes 983048 | tf_op jit(solution)/shard_map/ppermute | solution.py:143
  26.8 11.7 %collective-permute-start.3 = (bf16[640,256]{1,0:T(8,128)(2,1)S(1)}, bf16[640,256]{1,0:T(8,128)(2,1)S(1)}, u32[]{:S(2)}, u32[]{:S(2)}) collective-permute-start(bf16[640,256]{1,0:T(8,128)(2,1)S(1)} %all_gather.3), channel_id=1, source_target_pairs={{0,16},{16,32},{32,48},{48,64},{64,80},{80,96},{96,112},{112,0},{1... | collective-permute-start | bytes 983048 | tf_op jit(solution)/shard_map/ppermute | solution.py:143
  38.6 10.8 %collective-permute-start.4 = (bf16[640,256]{1,0:T(8,128)(2,1)S(1)}, bf16[640,256]{1,0:T(8,128)(2,1)S(1)}, u32[]{:S(2)}, u32[]{:S(2)}) collective-permute-start(bf16[640,256]{1,0:T(8,128)(2,1)S(1)} %collective-permute-done.3), channel_id=1, source_target_pairs={{0,16},{16,32},{32,48},{48,64},{64,80},{80,96},{96,112},{112,0},{1... | collective-permute-start | bytes 983048 | tf_op jit(solution)/shard_map/ppermute | solution.py:143
  41.2 10.7 %collective-permute-start.1 = (bf16[640,256]{1,0:T(8,128)(2,1)S(1)}, bf16[640,256]{1,0:T(8,128)(2,1)S(1)}, u32[]{:S(2)}, u32[]{:S(2)}) collective-permute-start(bf16[640,256]{1,0:T(8,128)(2,1)S(1)} %collective-permute-done), channel_id=1, source_target_pairs={{0,112},{16,0},{32,16},{48,32},{64,48},{80,64},{96,80},{112,96},{1... | collective-permute-start | bytes 983048 | tf_op jit(solution)/shard_map/ppermute | solution.py:143
  49.4 10.2 %collective-permute-start.5 = (bf16[640,256]{1,0:T(8,128)(2,1)S(1)}, bf16[640,256]{1,0:T(8,128)(2,1)S(1)}, u32[]{:S(2)}, u32[]{:S(2)}) collective-permute-start(bf16[640,256]{1,0:T(8,128)(2,1)S(1)} %collective-permute-done.4), channel_id=1, source_target_pairs={{0,16},{16,32},{32,48},{48,64},{64,80},{80,96},{96,112},{112,0},{1... | collective-permute-start | bytes 983048 | tf_op jit(solution)/shard_map/ppermute | solution.py:143
  51.9 9.7 %collective-permute-start.2 = (bf16[640,256]{1,0:T(8,128)(2,1)S(1)}, bf16[640,256]{1,0:T(8,128)(2,1)S(1)}, u32[]{:S(2)}, u32[]{:S(2)}) collective-permute-start(bf16[640,256]{1,0:T(8,128)(2,1)S(1)} %collective-permute-done.1), channel_id=1, source_target_pairs={{0,112},{16,0},{32,16},{48,32},{64,48},{80,64},{96,80},{112,96},{1... | collective-permute-start | bytes 983048 | tf_op jit(solution)/shard_map/ppermute | solution.py:143
  59.6 10.2 %collective-permute-start.6 = (bf16[640,256]{1,0:T(8,128)(2,1)S(1)}, bf16[640,256]{1,0:T(8,128)(2,1)S(1)}, u32[]{:S(2)}, u32[]{:S(2)}) collective-permute-start(bf16[640,256]{1,0:T(8,128)(2,1)S(1)} %collective-permute-done.5), channel_id=1, source_target_pairs={{0,16},{16,32},{32,48},{48,64},{64,80},{80,96},{96,112},{112,0},{1... | collective-permute-start | bytes 983048 | tf_op jit(solution)/shard_map/ppermute | solution.py:143
  69.9 1.5 copy-start.2
  151.6 5.1 %copy-start = (bf16[640,128]{1,0:T(8,128)(2,1)S(1)}, bf16[640,128]{1,0:T(8,128)(2,1)}, u32[]{:S(2)}) copy-start(bf16[640,128]{1,0:T(8,128)(2,1)} %get-tuple-element.7) | copy-start | bytes 491524
  151.6 5.1 %copy-start.1 = (bf16[640,128]{1,0:T(8,128)(2,1)S(1)}, bf16[640,128]{1,0:T(8,128)(2,1)}, u32[]{:S(2)}) copy-start(bf16[640,128]{1,0:T(8,128)(2,1)} %get-tuple-element.8) | copy-start | bytes 491524
  152.7 13.9 %all-to-all-start.1 = ((bf16[4,160,256]{2,1,0:T(8,128)(2,1)}), bf16[4,160,256]{2,1,0:T(8,128)(2,1)S(1)}, u32[]{:S(2)}, u32[]{:S(2)}) async-start(bf16[4,160,256]{2,1,0:T(8,128)(2,1)} %reduce_sum.21), calls=%async_computation.1 | async-start | bytes 655360 | tf_op jit(solution)/shard_map/all_to_all | solution.py:250

commit v10 on v9

--- a/solution.py
+++ b/solution.py
@@ -197,7 +197,8 @@
     outer = lax.axis_size("zh")
     inner = lax.axis_size("y")
     kv_local = jnp.concatenate([keys, values], axis=1)
-    column = lax.all_gather(kv_local, "zh", axis=0, tiled=True)
+    copies = jnp.broadcast_to(kv_local[None], (outer,) + kv_local.shape)
+    column = lax.all_to_all(copies, "zh", 0, 0, tiled=False).reshape(outer * 2 * SPAN, 2 * width)
     rightward = [column]
     leftward = [column]
     for _ in range(inner // 2):

time: 169 us -> 170 us (level)
  blocking collectives: 83 us -> 60.8 us
  starting transfers between devices: 27.2 us -> 42.2 us
  waiting for transfers between devices: 21.6 us -> 27.5 us
    all_gather x1 -> x0, blocking collectives: 20 us -> none  [on_device(): column = lax.all_gather(kv_local, 'zh', axis=0, tiled=True)]
    all_to_all x0 -> x1, starting transfers between devices: none -> 10.3 us  [on_device(): lax.all_to_all(copies, 'zh', 0, 0, tiled=False)]
    all_to_all x0 -> x1, waiting for transfers between devices: none -> 5.02 us  [on_device(): lax.all_to_all(copies, 'zh', 0, 0, tiled=False)]
    all_to_all x1, starting transfers between devices: 3.98 us -> 8.3 us  [on_device(): lax.all_to_all(row_sums.astype(jnp.bfloat16), 'zh', 0, 0, tiled=False)]
    all_to_all x1, blocking collectives: 63 us -> 60.8 us  [on_device(): row_parts = lax.all_to_all(dkv_all, 'y', 0, 0, tiled=False)]
  transfers between devices with their start and end apart: 8 -> 9, of which waited for: 4 -> 6; matrix products, arithmetic and copies ran while one was open for 6% -> 6% of each run, Pallas kernels for 0% -> 0%
where the time goes in v10:
time: 170 us; the launch traced here: 167 us
  blocking collectives  60.8 us (36%)
  starting transfers between devices  42.2 us (25%)
  waiting for transfers between devices  27.5 us (16%)
  Pallas kernels  17.6 us (10%)
  local copies, waits for them, and re-layouts  9.55 us (6%)
  other arithmetic  6.04 us (4%)
  between operations  3.51 us (2%)
    all_to_all x1, blocking collectives, on_device(): row_parts = lax.all_to_all(dkv_all, 'y', 0, 0, tiled=False)  60.8 us
    ppermute x7, starting transfers between devices, shifted(): lax.ppermute(array, axis, [(i, (i + by) % length) for i in range(length)])  23.6 us
    pallas_call x1, Pallas kernels, local_attention(): pl.pallas_call(attention_kernel, out_shape=(jax.ShapeDtypeStruct((rows, w...  17.6 us
    ppermute x7, waiting for transfers between devices, shifted(): lax.ppermute(array, axis, [(i, (i + by) % length) for i in range(length)])  14.6 us
    all_to_all x1, starting transfers between devices, on_device(): lax.all_to_all(copies, 'zh', 0, 0, tiled=False)  10.3 us
    all_to_all x1, starting transfers between devices, on_device(): lax.all_to_all(row_sums.astype(jnp.bfloat16), 'zh', 0, 0, tiled=False)  8.3 us
    all_to_all x1, waiting for transfers between devices, on_device(): lax.all_to_all(row_sums.astype(jnp.bfloat16), 'zh', 0, 0, tiled=False)  7.89 us
    all_to_all x1, waiting for transfers between devices, on_device(): lax.all_to_all(copies, 'zh', 0, 0, tiled=False)  5.02 us
  transfers between devices with their start and end apart: 9, of which 6 were waited for; matrix products, arithmetic and copies ran while one was open for 6% of the time, Pallas kernels for 0%

profile of v10, /device:TPU:6, one launch (start us, length us, event | category | flops | bytes accessed | tf_op | source)
XLA Modules:
  0.0 167.3 jit_solution(8522380722185069058)
XLA Ops:
  0.6 0.8 pad_maximum_fusion
  2.2 10.3 %all-to-all-start = ((bf16[4,160,256]{2,1,0:T(8,128)(2,1)}), bf16[4,160,256]{2,1,0:T(8,128)(2,1)S(1)}, u32[]{:S(2)}, u32[]{:S(2)}) async-start(bf16[4,160,256]{2,1,0:T(8,128)(2,1)} %broadcast_in_dim.7), calls=%async_computation | async-start | bytes 655360 | tf_op jit(solution)/shard_map/all_to_all | solution.py:201
  16.5 1.0 reshape.101
  17.5 1.0 reshape.103
  19.9 5.0 %all-to-all-done = bf16[4,160,256]{2,1,0:T(8,128)(2,1)S(1)} async-done(((bf16[4,160,256]{2,1,0:T(8,128)(2,1)}), bf16[4,160,256]{2,1,0:T(8,128)(2,1)S(1)}, u32[]{:S(2)}, u32[]{:S(2)}) %all-to-all-start) | async-done | bytes 327712 | tf_op jit(solution)/shard_map/all_to_all | solution.py:201
  24.9 3.5 %collective-permute-start.3 = (bf16[640,256]{1,0:T(8,128)(2,1)S(1)}, bf16[640,256]{1,0:T(8,128)(2,1)S(1)}, u32[]{:S(2)}, u32[]{:S(2)}) collective-permute-start(bf16[640,256]{1,0:T(8,128)(2,1)S(1)} %bitcast.30), channel_id=1, source_target_pairs={{0,16},{16,32},{32,48},{48,64},{64,80},{80,96},{96,112},{112,0},{1... | collective-permute-start | bytes 983048 | tf_op jit(solution)/shard_map/ppermute | solution.py:143
  28.5 3.8 %collective-permute-start = (bf16[640,256]{1,0:T(8,128)(2,1)S(1)}, bf16[640,256]{1,0:T(8,128)(2,1)S(1)}, u32[]{:S(2)}, u32[]{:S(2)}) collective-permute-start(bf16[640,256]{1,0:T(8,128)(2,1)S(1)} %bitcast.31), channel_id=1, source_target_pairs={{0,112},{16,0},{32,16},{48,32},{64,48},{80,64},{96,80},{112,96},{1... | collective-permute-start | bytes 983048 | tf_op jit(solution)/shard_map/ppermute | solution.py:143
  32.4 0.9 reshape.121.qpos_ref
  33.3 0.8 scatter_custom_fusion
  34.0 1.3 collective-permute-done.3
  35.3 2.0 %collective-permute-start.4 = (bf16[640,256]{1,0:T(8,128)(2,1)S(1)}, bf16[640,256]{1,0:T(8,128)(2,1)S(1)}, u32[]{:S(2)}, u32[]{:S(2)}) collective-permute-start(bf16[640,256]{1,0:T(8,128)(2,1)S(1)} %collective-permute-done.3), channel_id=1, source_target_pairs={{0,16},{16,32},{32,48},{48,64},{64,80},{80,96},{96,112},{112,0},{1... | collective-permute-start | bytes 983048 | tf_op jit(solution)/shard_map/ppermute | solution.py:143
  38.0 5.0 %collective-permute-start.1 = (bf16[640,256]{1,0:T(8,128)(2,1)S(1)}, bf16[640,256]{1,0:T(8,128)(2,1)S(1)}, u32[]{:S(2)}, u32[]{:S(2)}) collective-permute-start(bf16[640,256]{1,0:T(8,128)(2,1)S(1)} %collective-permute-done), channel_id=1, source_target_pairs={{0,112},{16,0},{32,16},{48,32},{64,48},{80,64},{96,80},{112,96},{1... | collective-permute-start | bytes 983048 | tf_op jit(solution)/shard_map/ppermute | solution.py:143
  43.6 1.9 %collective-permute-done.4 = bf16[640,256]{1,0:T(8,128)(2,1)S(1)} collective-permute-done((bf16[640,256]{1,0:T(8,128)(2,1)S(1)}, bf16[640,256]{1,0:T(8,128)(2,1)S(1)}, u32[]{:S(2)}, u32[]{:S(2)}) %collective-permute-start.4) | collective-permute-done | bytes 327712 | tf_op jit(solution)/shard_map/ppermute | solution.py:143
  45.5 1.9 %collective-permute-start.5 = (bf16[640,256]{1,0:T(8,128)(2,1)S(1)}, bf16[640,256]{1,0:T(8,128)(2,1)S(1)}, u32[]{:S(2)}, u32[]{:S(2)}) collective-permute-start(bf16[640,256]{1,0:T(8,128)(2,1)S(1)} %collective-permute-done.4), channel_id=1, source_target_pairs={{0,16},{16,32},{32,48},{48,64},{64,80},{80,96},{96,112},{112,0},{1... | collective-permute-start | bytes 983048 | tf_op jit(solution)/shard_map/ppermute | solution.py:143
  48.0 5.5 %collective-permute-start.2 = (bf16[640,256]{1,0:T(8,128)(2,1)S(1)}, bf16[640,256]{1,0:T(8,128)(2,1)S(1)}, u32[]{:S(2)}, u32[]{:S(2)}) collective-permute-start(bf16[640,256]{1,0:T(8,128)(2,1)S(1)} %collective-permute-done.1), channel_id=1, source_target_pairs={{0,112},{16,0},{32,16},{48,32},{64,48},{80,64},{96,80},{112,96},{1... | collective-permute-start | bytes 983048 | tf_op jit(solution)/shard_map/ppermute | solution.py:143
  53.5 3.3 %collective-permute-done.5 = bf16[640,256]{1,0:T(8,128)(2,1)S(1)} collective-permute-done((bf16[640,256]{1,0:T(8,128)(2,1)S(1)}, bf16[640,256]{1,0:T(8,128)(2,1)S(1)}, u32[]{:S(2)}, u32[]{:S(2)}) %collective-permute-start.5) | collective-permute-done | bytes 327712 | tf_op jit(solution)/shard_map/ppermute | solution.py:143
  56.8 1.9 %collective-permute-start.6 = (bf16[640,256]{1,0:T(8,128)(2,1)S(1)}, bf16[640,256]{1,0:T(8,128)(2,1)S(1)}, u32[]{:S(2)}, u32[]{:S(2)}) collective-permute-start(bf16[640,256]{1,0:T(8,128)(2,1)S(1)} %collective-permute-done.5), channel_id=1, source_target_pairs={{0,16},{16,32},{32,48},{48,64},{64,80},{80,96},{96,112},{112,0},{1... | collective-permute-start | bytes 983048 | tf_op jit(solution)/shard_map/ppermute | solution.py:143
  58.8 8.1 %collective-permute-done.6 = bf16[640,256]{1,0:T(8,128)(2,1)S(1)} collective-permute-done((bf16[640,256]{1,0:T(8,128)(2,1)S(1)}, bf16[640,256]{1,0:T(8,128)(2,1)S(1)}, u32[]{:S(2)}, u32[]{:S(2)}) %collective-permute-start.6) | collective-permute-done | bytes 327712 | tf_op jit(solution)/shard_map/ppermute | solution.py:143
  67.1 1.5 copy-done.2
  68.6 17.6 %shard_map.84 = (bf16[640,128]{1,0:T(8,128)(2,1)}, bf16[640,128]{1,0:T(8,128)(2,1)}, bf16[5120,256]{1,0:T(8,128)(2,1)}) custom-call(s32[4]{0:T(128)} %pad_add_fusion.limits_ref, s32[64]{0:T(128)} %multiply_add_fusion.1.source_ref, s32[64]{0:T(128)} %get-tuple-element.10.target_ref, bf16[640,128]{1,0:T(8,128)(2,1)} %bitcast.35, bf16[640,128]{1,0:T(8,128)(2,1)} %bitcast.36, ...), custom_call_target="tpu_custom_call" | custom-call | flops 2936012800 | bytes 7864320 | tf_op jit(solution)/shard_map/pallas_call | solution.py:151
  86.2 60.8 %all_to_all.15 = bf16[8,4,160,256]{3,2,1,0:T(8,128)(2,1)S(1)} all-to-all(bf16[8,4,160,256]{3,2,1,0:T(8,128)(2,1)} %bitcast.29), channel_id=1, replica_groups=mesh['zh'=4,'y'=8,'head'=16] {'y'}, dimensions={0} | all-to-all | bytes 5242880 | tf_op jit(solution)/shard_map/all_to_all | solution.py:249
  147.0 1.2 reduce_sum.21
  148.2 8.3 %all-to-all-start.2 = ((bf16[4,160,256]{2,1,0:T(8,128)(2,1)}), bf16[4,160,256]{2,1,0:T(8,128)(2,1)S(1)}, u32[]{:S(2)}, u32[]{:S(2)}) async-start(bf16[4,160,256]{2,1,0:T(8,128)(2,1)} %reduce_sum.21), calls=%async_computation.2 | async-start | bytes 655360 | tf_op jit(solution)/shard_map/all_to_all | solution.py:251
  158.1 7.9 %all-to-all-done.2 = bf16[4,160,256]{2,1,0:T(8,128)(2,1)S(1)} async-done(((bf16[4,160,256]{2,1,0:T(8,128)(2,1)}), bf16[4,160,256]{2,1,0:T(8,128)(2,1)S(1)}, u32[]{:S(2)}, u32[]{:S(2)}) %all-to-all-start.2) | async-done | bytes 327712 | tf_op jit(solution)/shard_map/all_to_all | solution.py:251
  (41 shorter events, 8.5 us)
Async XLA Ops:
  0.6 31.6 %copy-start.3 = (s32[64]{0:T(128)S(1)}, s32[64]{0:T(128)}, u32[]{:S(2)}) copy-start(s32[64]{0:T(128)} %param.9) | copy-start | bytes 772
  2.2 22.7 %all-to-all-start = ((bf16[4,160,256]{2,1,0:T(8,128)(2,1)}), bf16[4,160,256]{2,1,0:T(8,128)(2,1)S(1)}, u32[]{:S(2)}, u32[]{:S(2)}) async-start(bf16[4,160,256]{2,1,0:T(8,128)(2,1)} %broadcast_in_dim.7), calls=%async_computation | async-start | bytes 655360 | tf_op jit(solution)/shard_map/all_to_all | solution.py:201
  24.9 10.4 %collective-permute-start.3 = (bf16[640,256]{1,0:T(8,128)(2,1)S(1)}, bf16[640,256]{1,0:T(8,128)(2,1)S(1)}, u32[]{:S(2)}, u32[]{:S(2)}) collective-permute-start(bf16[640,256]{1,0:T(8,128)(2,1)S(1)} %bitcast.30), channel_id=1, source_target_pairs={{0,16},{16,32},{32,48},{48,64},{64,80},{80,96},{96,112},{112,0},{1... | collective-permute-start | bytes 983048 | tf_op jit(solution)/shard_map/ppermute | solution.py:143
  28.5 9.5 %collective-permute-start = (bf16[640,256]{1,0:T(8,128)(2,1)S(1)}, bf16[640,256]{1,0:T(8,128)(2,1)S(1)}, u32[]{:S(2)}, u32[]{:S(2)}) collective-permute-start(bf16[640,256]{1,0:T(8,128)(2,1)S(1)} %bitcast.31), channel_id=1, source_target_pairs={{0,112},{16,0},{32,16},{48,32},{64,48},{80,64},{96,80},{112,96},{1... | collective-permute-start | bytes 983048 | tf_op jit(solution)/shard_map/ppermute | solution.py:143
  35.3 10.2 %collective-permute-start.4 = (bf16[640,256]{1,0:T(8,128)(2,1)S(1)}, bf16[640,256]{1,0:T(8,128)(2,1)S(1)}, u32[]{:S(2)}, u32[]{:S(2)}) collective-permute-start(bf16[640,256]{1,0:T(8,128)(2,1)S(1)} %collective-permute-done.3), channel_id=1, source_target_pairs={{0,16},{16,32},{32,48},{48,64},{64,80},{80,96},{96,112},{112,0},{1... | collective-permute-start | bytes 983048 | tf_op jit(solution)/shard_map/ppermute | solution.py:143
  38.0 10.0 %collective-permute-start.1 = (bf16[640,256]{1,0:T(8,128)(2,1)S(1)}, bf16[640,256]{1,0:T(8,128)(2,1)S(1)}, u32[]{:S(2)}, u32[]{:S(2)}) collective-permute-start(bf16[640,256]{1,0:T(8,128)(2,1)S(1)} %collective-permute-done), channel_id=1, source_target_pairs={{0,112},{16,0},{32,16},{48,32},{64,48},{80,64},{96,80},{112,96},{1... | collective-permute-start | bytes 983048 | tf_op jit(solution)/shard_map/ppermute | solution.py:143
  45.5 11.3 %collective-permute-start.5 = (bf16[640,256]{1,0:T(8,128)(2,1)S(1)}, bf16[640,256]{1,0:T(8,128)(2,1)S(1)}, u32[]{:S(2)}, u32[]{:S(2)}) collective-permute-start(bf16[640,256]{1,0:T(8,128)(2,1)S(1)} %collective-permute-done.4), channel_id=1, source_target_pairs={{0,16},{16,32},{32,48},{48,64},{64,80},{80,96},{96,112},{112,0},{1... | collective-permute-start | bytes 983048 | tf_op jit(solution)/shard_map/ppermute | solution.py:143
  48.0 10.8 %collective-permute-start.2 = (bf16[640,256]{1,0:T(8,128)(2,1)S(1)}, bf16[640,256]{1,0:T(8,128)(2,1)S(1)}, u32[]{:S(2)}, u32[]{:S(2)}) collective-permute-start(bf16[640,256]{1,0:T(8,128)(2,1)S(1)} %collective-permute-done.1), channel_id=1, source_target_pairs={{0,112},{16,0},{32,16},{48,32},{64,48},{80,64},{96,80},{112,96},{1... | collective-permute-start | bytes 983048 | tf_op jit(solution)/shard_map/ppermute | solution.py:143
  56.8 10.2 %collective-permute-start.6 = (bf16[640,256]{1,0:T(8,128)(2,1)S(1)}, bf16[640,256]{1,0:T(8,128)(2,1)S(1)}, u32[]{:S(2)}, u32[]{:S(2)}) collective-permute-start(bf16[640,256]{1,0:T(8,128)(2,1)S(1)} %collective-permute-done.5), channel_id=1, source_target_pairs={{0,16},{16,32},{32,48},{48,64},{64,80},{80,96},{96,112},{112,0},{1... | collective-permute-start | bytes 983048 | tf_op jit(solution)/shard_map/ppermute | solution.py:143
  67.1 1.5 copy-start.2
  147.0 9.5 %copy-start = (bf16[640,128]{1,0:T(8,128)(2,1)S(1)}, bf16[640,128]{1,0:T(8,128)(2,1)}, u32[]{:S(2)}) copy-start(bf16[640,128]{1,0:T(8,128)(2,1)} %get-tuple-element.7) | copy-start | bytes 491524
  147.0 9.5 %copy-start.1 = (bf16[640,128]{1,0:T(8,128)(2,1)S(1)}, bf16[640,128]{1,0:T(8,128)(2,1)}, u32[]{:S(2)}) copy-start(bf16[640,128]{1,0:T(8,128)(2,1)} %get-tuple-element.8) | copy-start | bytes 491524
  148.2 17.8 %all-to-all-start.2 = ((bf16[4,160,256]{2,1,0:T(8,128)(2,1)}), bf16[4,160,256]{2,1,0:T(8,128)(2,1)S(1)}, u32[]{:S(2)}, u32[]{:S(2)}) async-start(bf16[4,160,256]{2,1,0:T(8,128)(2,1)} %reduce_sum.21), calls=%async_computation.2 | async-start | bytes 655360 | tf_op jit(solution)/shard_map/all_to_all | solution.py:251

commit v11 on v9

--- a/solution.py
+++ b/solution.py
@@ -98,7 +98,13 @@
         g_ref[...].astype(jnp.float32) * attention.astype(jnp.float32), axis=1, keepdims=True
     )
     dqacc_ref[...] = jnp.zeros(dqacc_ref.shape, jnp.float32)
-    dkv_ref[...] = jnp.zeros(dkv_ref.shape, jnp.float32)
+
+    def clear_block(block, carry):
+        start = pl.multiple_of(block * KEY_BLOCK, KEY_BLOCK)
+        dkv_ref[pl.ds(start, KEY_BLOCK), :] = jnp.zeros((KEY_BLOCK, dkv_ref.shape[1]), jnp.float32)
+        return carry
+
+    lax.fori_loop(late_blocks, dkv_ref.shape[0] // KEY_BLOCK, clear_block, 0)
 
     def backward_masked(lo, count, start, masked):
         s = scores_of(lo, count, start, masked)
@@ -114,8 +120,8 @@
         dv = lax.dot_general(
             probs.astype(jnp.bfloat16), g, (((0,), (0,)), ((), ())), preferred_element_type=jnp.float32
         )
-        dkv_ref[pl.ds(start, KEY_BLOCK), 0:width] += dk
-        dkv_ref[pl.ds(start, KEY_BLOCK), width:2 * width] += dv
+        dkv_ref[pl.ds(start, KEY_BLOCK), 0:width] = dk
+        dkv_ref[pl.ds(start, KEY_BLOCK), width:2 * width] = dv
 
     def bwd_both(block, carry):
         split_by_mask(backward_masked, 0, rows, block, early_first)

time: 169 us -> 168 us (level)
  no operation moved by 1% of the time
where the time goes in v11:
time: 168 us
  blocking collectives  82.1 us (49%)
  starting transfers between devices  27.9 us (17%)
  waiting for transfers between devices  21.9 us (13%)
  Pallas kernels  17 us (10%)
  local copies, waits for them, and re-layouts  8.8 us (5%)
  other arithmetic  6.67 us (4%)
  between operations  3.43 us (2%)
    all_to_all x1, blocking collectives, on_device(): row_parts = lax.all_to_all(dkv_all, 'y', 0, 0, tiled=False)  62.1 us
    ppermute x7, starting transfers between devices, shifted(): lax.ppermute(array, axis, [(i, (i + by) % length) for i in range(length)])  23.3 us
    all_gather x1, blocking collectives, on_device(): column = lax.all_gather(kv_local, 'zh', axis=0, tiled=True)  20 us
    pallas_call x1, Pallas kernels, local_attention(): pl.pallas_call(attention_kernel, out_shape=(jax.ShapeDtypeStruct((rows, w...  17 us
    ppermute x7, waiting for transfers between devices, shifted(): lax.ppermute(array, axis, [(i, (i + by) % length) for i in range(length)])  13.3 us
    all_to_all x1, waiting for transfers between devices, on_device(): lax.all_to_all(row_sums.astype(jnp.bfloat16), 'zh', 0, 0, tiled=False)  8.61 us
    all_to_all x1, starting transfers between devices, on_device(): lax.all_to_all(row_sums.astype(jnp.bfloat16), 'zh', 0, 0, tiled=False)  4.67 us
  transfers between devices with their start and end apart: 8, of which 4 were waited for; matrix products, arithmetic and copies ran while one was open for 6% of the time, Pallas kernels for 0%

profile of v11, /device:TPU:6, one launch (start us, length us, event | category | flops | bytes accessed | tf_op | source)
XLA Modules:
  0.0 167.7 jit_solution(5577345501808214)
XLA Ops:
  0.6 0.8 pad_maximum_fusion
  1.4 20.0 %all_gather.3 = bf16[640,256]{1,0:T(8,128)(2,1)S(1)} all-gather(bf16[160,256]{1,0:T(8,128)(2,1)S(1)} %pad_maximum_fusion), channel_id=1, replica_groups=mesh['zh'=4,'y'=8,'head'=16] {'zh'}, dimensions={0}, use_global_device_ids=true | all-gather | bytes 409600 | tf_op jit(solution)/shard_map/all_gather | solution.py:206
  21.4 5.4 %collective-permute-start = (bf16[640,256]{1,0:T(8,128)(2,1)S(1)}, bf16[640,256]{1,0:T(8,128)(2,1)S(1)}, u32[]{:S(2)}, u32[]{:S(2)}) collective-permute-start(bf16[640,256]{1,0:T(8,128)(2,1)S(1)} %all_gather.3), channel_id=1, source_target_pairs={{0,112},{16,0},{32,16},{48,32},{64,48},{80,64},{96,80},{112,96},{1... | collective-permute-start | bytes 983048 | tf_op jit(solution)/shard_map/ppermute | solution.py:149
  26.8 1.9 %collective-permute-start.3 = (bf16[640,256]{1,0:T(8,128)(2,1)S(1)}, bf16[640,256]{1,0:T(8,128)(2,1)S(1)}, u32[]{:S(2)}, u32[]{:S(2)}) collective-permute-start(bf16[640,256]{1,0:T(8,128)(2,1)S(1)} %all_gather.3), channel_id=1, source_target_pairs={{0,16},{16,32},{32,48},{48,64},{64,80},{80,96},{96,112},{112,0},{1... | collective-permute-start | bytes 983048 | tf_op jit(solution)/shard_map/ppermute | solution.py:149
  28.7 0.7 dynamic_slice.3
  32.7 1.0 reshape.97
  33.7 1.0 reshape.99
  34.7 0.7 reverse_select_fusion.3
  36.9 0.9 reshape.116.qpos_ref
  37.8 0.8 scatter_custom_fusion
  38.6 2.0 %collective-permute-start.4 = (bf16[640,256]{1,0:T(8,128)(2,1)S(1)}, bf16[640,256]{1,0:T(8,128)(2,1)S(1)}, u32[]{:S(2)}, u32[]{:S(2)}) collective-permute-start(bf16[640,256]{1,0:T(8,128)(2,1)S(1)} %collective-permute-done.3), channel_id=1, source_target_pairs={{0,16},{16,32},{32,48},{48,64},{64,80},{80,96},{96,112},{112,0},{1... | collective-permute-start | bytes 983048 | tf_op jit(solution)/shard_map/ppermute | solution.py:149
  41.2 5.0 %collective-permute-start.1 = (bf16[640,256]{1,0:T(8,128)(2,1)S(1)}, bf16[640,256]{1,0:T(8,128)(2,1)S(1)}, u32[]{:S(2)}, u32[]{:S(2)}) collective-permute-start(bf16[640,256]{1,0:T(8,128)(2,1)S(1)} %collective-permute-done), channel_id=1, source_target_pairs={{0,112},{16,0},{32,16},{48,32},{64,48},{80,64},{96,80},{112,96},{1... | collective-permute-start | bytes 983048 | tf_op jit(solution)/shard_map/ppermute | solution.py:149
  46.3 3.1 %collective-permute-done.4 = bf16[640,256]{1,0:T(8,128)(2,1)S(1)} collective-permute-done((bf16[640,256]{1,0:T(8,128)(2,1)S(1)}, bf16[640,256]{1,0:T(8,128)(2,1)S(1)}, u32[]{:S(2)}, u32[]{:S(2)}) %collective-permute-start.4) | collective-permute-done | bytes 327712 | tf_op jit(solution)/shard_map/ppermute | solution.py:149
  49.4 1.9 %collective-permute-start.5 = (bf16[640,256]{1,0:T(8,128)(2,1)S(1)}, bf16[640,256]{1,0:T(8,128)(2,1)S(1)}, u32[]{:S(2)}, u32[]{:S(2)}) collective-permute-start(bf16[640,256]{1,0:T(8,128)(2,1)S(1)} %collective-permute-done.4), channel_id=1, source_target_pairs={{0,16},{16,32},{32,48},{48,64},{64,80},{80,96},{96,112},{112,0},{1... | collective-permute-start | bytes 983048 | tf_op jit(solution)/shard_map/ppermute | solution.py:149
  51.9 5.1 %collective-permute-start.2 = (bf16[640,256]{1,0:T(8,128)(2,1)S(1)}, bf16[640,256]{1,0:T(8,128)(2,1)S(1)}, u32[]{:S(2)}, u32[]{:S(2)}) collective-permute-start(bf16[640,256]{1,0:T(8,128)(2,1)S(1)} %collective-permute-done.1), channel_id=1, source_target_pairs={{0,112},{16,0},{32,16},{48,32},{64,48},{80,64},{96,80},{112,96},{1... | collective-permute-start | bytes 983048 | tf_op jit(solution)/shard_map/ppermute | solution.py:149
  57.6 2.0 %collective-permute-done.5 = bf16[640,256]{1,0:T(8,128)(2,1)S(1)} collective-permute-done((bf16[640,256]{1,0:T(8,128)(2,1)S(1)}, bf16[640,256]{1,0:T(8,128)(2,1)S(1)}, u32[]{:S(2)}, u32[]{:S(2)}) %collective-permute-start.5) | collective-permute-done | bytes 327712 | tf_op jit(solution)/shard_map/ppermute | solution.py:149
  59.6 1.9 %collective-permute-start.6 = (bf16[640,256]{1,0:T(8,128)(2,1)S(1)}, bf16[640,256]{1,0:T(8,128)(2,1)S(1)}, u32[]{:S(2)}, u32[]{:S(2)}) collective-permute-start(bf16[640,256]{1,0:T(8,128)(2,1)S(1)} %collective-permute-done.5), channel_id=1, source_target_pairs={{0,16},{16,32},{32,48},{48,64},{64,80},{80,96},{96,112},{112,0},{1... | collective-permute-start | bytes 983048 | tf_op jit(solution)/shard_map/ppermute | solution.py:149
  61.6 8.1 %collective-permute-done.6 = bf16[640,256]{1,0:T(8,128)(2,1)S(1)} collective-permute-done((bf16[640,256]{1,0:T(8,128)(2,1)S(1)}, bf16[640,256]{1,0:T(8,128)(2,1)S(1)}, u32[]{:S(2)}, u32[]{:S(2)}) %collective-permute-start.6) | collective-permute-done | bytes 327712 | tf_op jit(solution)/shard_map/ppermute | solution.py:149
  69.9 1.5 copy-done.2
  71.4 17.0 %shard_map.84 = (bf16[640,128]{1,0:T(8,128)(2,1)}, bf16[640,128]{1,0:T(8,128)(2,1)}, bf16[5120,256]{1,0:T(8,128)(2,1)}) custom-call(s32[4]{0:T(128)} %pad_add_fusion.limits_ref, s32[64]{0:T(128)} %multiply_add_fusion.1.source_ref, s32[64]{0:T(128)} %get-tuple-element.10.target_ref, bf16[640,128]{1,0:T(8,128)(2,1)} %bitcast.31, bf16[640,128]{1,0:T(8,128)(2,1)} %bitcast.32, ...), custom_call_target="tpu_custom_call" | custom-call | flops 2936012800 | bytes 7864320 | tf_op jit(solution)/shard_map/pallas_call | solution.py:157
  88.3 62.1 %all_to_all.10 = bf16[8,4,160,256]{3,2,1,0:T(8,128)(2,1)S(1)} all-to-all(bf16[8,4,160,256]{3,2,1,0:T(8,128)(2,1)} %bitcast.28), channel_id=1, replica_groups=mesh['zh'=4,'y'=8,'head'=16] {'y'}, dimensions={0} | all-to-all | bytes 5242880 | tf_op jit(solution)/shard_map/all_to_all | solution.py:254
  150.4 1.2 reduce_sum.21
  151.6 4.7 %all-to-all-start.1 = ((bf16[4,160,256]{2,1,0:T(8,128)(2,1)}), bf16[4,160,256]{2,1,0:T(8,128)(2,1)S(1)}, u32[]{:S(2)}, u32[]{:S(2)}) async-start(bf16[4,160,256]{2,1,0:T(8,128)(2,1)} %reduce_sum.21), calls=%async_computation.1 | async-start | bytes 655360 | tf_op jit(solution)/shard_map/all_to_all | solution.py:256
  157.8 8.6 %all-to-all-done.1 = bf16[4,160,256]{2,1,0:T(8,128)(2,1)S(1)} async-done(((bf16[4,160,256]{2,1,0:T(8,128)(2,1)}), bf16[4,160,256]{2,1,0:T(8,128)(2,1)S(1)}, u32[]{:S(2)}, u32[]{:S(2)}) %all-to-all-start.1) | async-done | bytes 327712 | tf_op jit(solution)/shard_map/all_to_all | solution.py:256
  (37 shorter events, 7.0 us)
Async XLA Ops:
  21.4 19.8 %collective-permute-start = (bf16[640,256]{1,0:T(8,128)(2,1)S(1)}, bf16[640,256]{1,0:T(8,128)(2,1)S(1)}, u32[]{:S(2)}, u32[]{:S(2)}) collective-permute-start(bf16[640,256]{1,0:T(8,128)(2,1)S(1)} %all_gather.3), channel_id=1, source_target_pairs={{0,112},{16,0},{32,16},{48,32},{64,48},{80,64},{96,80},{112,96},{1... | collective-permute-start | bytes 983048 | tf_op jit(solution)/shard_map/ppermute | solution.py:149
  26.8 11.7 %collective-permute-start.3 = (bf16[640,256]{1,0:T(8,128)(2,1)S(1)}, bf16[640,256]{1,0:T(8,128)(2,1)S(1)}, u32[]{:S(2)}, u32[]{:S(2)}) collective-permute-start(bf16[640,256]{1,0:T(8,128)(2,1)S(1)} %all_gather.3), channel_id=1, source_target_pairs={{0,16},{16,32},{32,48},{48,64},{64,80},{80,96},{96,112},{112,0},{1... | collective-permute-start | bytes 983048 | tf_op jit(solution)/shard_map/ppermute | solution.py:149
  38.6 10.8 %collective-permute-start.4 = (bf16[640,256]{1,0:T(8,128)(2,1)S(1)}, bf16[640,256]{1,0:T(8,128)(2,1)S(1)}, u32[]{:S(2)}, u32[]{:S(2)}) collective-permute-start(bf16[640,256]{1,0:T(8,128)(2,1)S(1)} %collective-permute-done.3), channel_id=1, source_target_pairs={{0,16},{16,32},{32,48},{48,64},{64,80},{80,96},{96,112},{112,0},{1... | collective-permute-start | bytes 983048 | tf_op jit(solution)/shard_map/ppermute | solution.py:149
  41.2 10.7 %collective-permute-start.1 = (bf16[640,256]{1,0:T(8,128)(2,1)S(1)}, bf16[640,256]{1,0:T(8,128)(2,1)S(1)}, u32[]{:S(2)}, u32[]{:S(2)}) collective-permute-start(bf16[640,256]{1,0:T(8,128)(2,1)S(1)} %collective-permute-done), channel_id=1, source_target_pairs={{0,112},{16,0},{32,16},{48,32},{64,48},{80,64},{96,80},{112,96},{1... | collective-permute-start | bytes 983048 | tf_op jit(solution)/shard_map/ppermute | solution.py:149
  49.4 10.2 %collective-permute-start.5 = (bf16[640,256]{1,0:T(8,128)(2,1)S(1)}, bf16[640,256]{1,0:T(8,128)(2,1)S(1)}, u32[]{:S(2)}, u32[]{:S(2)}) collective-permute-start(bf16[640,256]{1,0:T(8,128)(2,1)S(1)} %collective-permute-done.4), channel_id=1, source_target_pairs={{0,16},{16,32},{32,48},{48,64},{64,80},{80,96},{96,112},{112,0},{1... | collective-permute-start | bytes 983048 | tf_op jit(solution)/shard_map/ppermute | solution.py:149
  51.9 9.7 %collective-permute-start.2 = (bf16[640,256]{1,0:T(8,128)(2,1)S(1)}, bf16[640,256]{1,0:T(8,128)(2,1)S(1)}, u32[]{:S(2)}, u32[]{:S(2)}) collective-permute-start(bf16[640,256]{1,0:T(8,128)(2,1)S(1)} %collective-permute-done.1), channel_id=1, source_target_pairs={{0,112},{16,0},{32,16},{48,32},{64,48},{80,64},{96,80},{112,96},{1... | collective-permute-start | bytes 983048 | tf_op jit(solution)/shard_map/ppermute | solution.py:149
  59.6 10.2 %collective-permute-start.6 = (bf16[640,256]{1,0:T(8,128)(2,1)S(1)}, bf16[640,256]{1,0:T(8,128)(2,1)S(1)}, u32[]{:S(2)}, u32[]{:S(2)}) collective-permute-start(bf16[640,256]{1,0:T(8,128)(2,1)S(1)} %collective-permute-done.5), channel_id=1, source_target_pairs={{0,16},{16,32},{32,48},{48,64},{64,80},{80,96},{96,112},{112,0},{1... | collective-permute-start | bytes 983048 | tf_op jit(solution)/shard_map/ppermute | solution.py:149
  69.9 1.5 copy-start.2
  150.4 5.8 %copy-start = (bf16[640,128]{1,0:T(8,128)(2,1)S(1)}, bf16[640,128]{1,0:T(8,128)(2,1)}, u32[]{:S(2)}) copy-start(bf16[640,128]{1,0:T(8,128)(2,1)} %get-tuple-element.7) | copy-start | bytes 491524
  150.4 5.8 %copy-start.1 = (bf16[640,128]{1,0:T(8,128)(2,1)S(1)}, bf16[640,128]{1,0:T(8,128)(2,1)}, u32[]{:S(2)}) copy-start(bf16[640,128]{1,0:T(8,128)(2,1)} %get-tuple-element.8) | copy-start | bytes 491524
  151.6 14.9 %all-to-all-start.1 = ((bf16[4,160,256]{2,1,0:T(8,128)(2,1)}), bf16[4,160,256]{2,1,0:T(8,128)(2,1)S(1)}, u32[]{:S(2)}, u32[]{:S(2)}) async-start(bf16[4,160,256]{2,1,0:T(8,128)(2,1)} %reduce_sum.21), calls=%async_computation.1 | async-start | bytes 655360 | tf_op jit(solution)/shard_map/all_to_all | solution.py:256

commit v12 on v11

--- a/solution.py
+++ b/solution.py
@@ -101,7 +101,7 @@
 
     def clear_block(block, carry):
         start = pl.multiple_of(block * KEY_BLOCK, KEY_BLOCK)
-        dkv_ref[pl.ds(start, KEY_BLOCK), :] = jnp.zeros((KEY_BLOCK, dkv_ref.shape[1]), jnp.float32)
+        dkv_ref[pl.ds(start, KEY_BLOCK), :] = jnp.zeros((KEY_BLOCK, dkv_ref.shape[1]), jnp.bfloat16)
         return carry
 
     lax.fori_loop(late_blocks, dkv_ref.shape[0] // KEY_BLOCK, clear_block, 0)
@@ -120,8 +120,8 @@
         dv = lax.dot_general(
             probs.astype(jnp.bfloat16), g, (((0,), (0,)), ((), ())), preferred_element_type=jnp.float32
         )
-        dkv_ref[pl.ds(start, KEY_BLOCK), 0:width] = dk
-        dkv_ref[pl.ds(start, KEY_BLOCK), width:2 * width] = dv
+        dkv_ref[pl.ds(start, KEY_BLOCK), 0:width] = dk.astype(jnp.bfloat16)
+        dkv_ref[pl.ds(start, KEY_BLOCK), width:2 * width] = dv.astype(jnp.bfloat16)
 
     def bwd_both(block, carry):
         split_by_mask(backward_masked, 0, rows, block, early_first)
@@ -138,7 +138,7 @@
     def place_span(span, carry):
         target = pl.multiple_of(target_ref[span] * SPAN, 16)
         block = dkv_ref[pl.ds(pl.multiple_of(span * SPAN, 16), SPAN), :]
-        dkv_out_ref[pl.ds(target, SPAN), :] = block.astype(jnp.bfloat16)
+        dkv_out_ref[pl.ds(target, SPAN), :] = block
         return carry
 
     lax.fori_loop(0, spans, place_span, 0)
@@ -183,7 +183,7 @@
             pltpu.VMEM((rows, 1), jnp.float32),
             pltpu.VMEM((rows, width), jnp.float32),
             pltpu.VMEM((keys, 2 * width), jnp.bfloat16),
-            pltpu.VMEM((keys, 2 * width), jnp.float32),
+            pltpu.VMEM((keys, 2 * width), jnp.bfloat16),
         ],
         cost_estimate=pl.CostEstimate(
             flops=flops, transcendentals=rows * keys, bytes_accessed=keys * width * 12

time: 168 us -> 168 us (level)
  no operation moved by 1% of the time
where the time goes in v12:
time: 168 us; the launch traced here: 167 us
  blocking collectives  82.6 us (49%)
  starting transfers between devices  26.8 us (16%)
  waiting for transfers between devices  21.7 us (13%)
  Pallas kernels  17.3 us (10%)
  local copies, waits for them, and re-layouts  8.8 us (5%)
  other arithmetic  6.67 us (4%)
  between operations  3.43 us (2%)
    all_to_all x1, blocking collectives, on_device(): row_parts = lax.all_to_all(dkv_all, 'y', 0, 0, tiled=False)  62.6 us
    ppermute x7, starting transfers between devices, shifted(): lax.ppermute(array, axis, [(i, (i + by) % length) for i in range(length)])  23.3 us
    all_gather x1, blocking collectives, on_device(): column = lax.all_gather(kv_local, 'zh', axis=0, tiled=True)  20 us
    pallas_call x1, Pallas kernels, local_attention(): pl.pallas_call(attention_kernel, out_shape=(jax.ShapeDtypeStruct((rows, w...  17.3 us
    ppermute x7, waiting for transfers between devices, shifted(): lax.ppermute(array, axis, [(i, (i + by) % length) for i in range(length)])  13.3 us
    all_to_all x1, waiting for transfers between devices, on_device(): lax.all_to_all(row_sums.astype(jnp.bfloat16), 'zh', 0, 0, tiled=False)  8.47 us
    all_to_all x1, starting transfers between devices, on_device(): lax.all_to_all(row_sums.astype(jnp.bfloat16), 'zh', 0, 0, tiled=False)  3.53 us
  transfers between devices with their start and end apart: 8, of which 4 were waited for; matrix products, arithmetic and copies ran while one was open for 6% of the time, Pallas kernels for 0%

profile of v12, /device:TPU:6, one launch (start us, length us, event | category | flops | bytes accessed | tf_op | source)
XLA Modules:
  0.0 167.4 jit_solution(12177893726872897671)
XLA Ops:
  0.6 0.8 pad_maximum_fusion
  1.4 20.0 %all_gather.3 = bf16[640,256]{1,0:T(8,128)(2,1)S(1)} all-gather(bf16[160,256]{1,0:T(8,128)(2,1)S(1)} %pad_maximum_fusion), channel_id=1, replica_groups=mesh['zh'=4,'y'=8,'head'=16] {'zh'}, dimensions={0}, use_global_device_ids=true | all-gather | bytes 409600 | tf_op jit(solution)/shard_map/all_gather | solution.py:206
  21.4 5.4 %collective-permute-start = (bf16[640,256]{1,0:T(8,128)(2,1)S(1)}, bf16[640,256]{1,0:T(8,128)(2,1)S(1)}, u32[]{:S(2)}, u32[]{:S(2)}) collective-permute-start(bf16[640,256]{1,0:T(8,128)(2,1)S(1)} %all_gather.3), channel_id=1, source_target_pairs={{0,112},{16,0},{32,16},{48,32},{64,48},{80,64},{96,80},{112,96},{1... | collective-permute-start | bytes 983048 | tf_op jit(solution)/shard_map/ppermute | solution.py:149
  26.8 1.9 %collective-permute-start.3 = (bf16[640,256]{1,0:T(8,128)(2,1)S(1)}, bf16[640,256]{1,0:T(8,128)(2,1)S(1)}, u32[]{:S(2)}, u32[]{:S(2)}) collective-permute-start(bf16[640,256]{1,0:T(8,128)(2,1)S(1)} %all_gather.3), channel_id=1, source_target_pairs={{0,16},{16,32},{32,48},{48,64},{64,80},{80,96},{96,112},{112,0},{1... | collective-permute-start | bytes 983048 | tf_op jit(solution)/shard_map/ppermute | solution.py:149
  28.7 0.7 dynamic_slice.3
  32.7 1.0 reshape.97
  33.7 1.0 reshape.99
  34.7 0.7 reverse_select_fusion.3
  36.9 0.9 reshape.116.qpos_ref
  37.8 0.8 scatter_custom_fusion
  38.6 2.0 %collective-permute-start.4 = (bf16[640,256]{1,0:T(8,128)(2,1)S(1)}, bf16[640,256]{1,0:T(8,128)(2,1)S(1)}, u32[]{:S(2)}, u32[]{:S(2)}) collective-permute-start(bf16[640,256]{1,0:T(8,128)(2,1)S(1)} %collective-permute-done.3), channel_id=1, source_target_pairs={{0,16},{16,32},{32,48},{48,64},{64,80},{80,96},{96,112},{112,0},{1... | collective-permute-start | bytes 983048 | tf_op jit(solution)/shard_map/ppermute | solution.py:149
  41.2 5.0 %collective-permute-start.1 = (bf16[640,256]{1,0:T(8,128)(2,1)S(1)}, bf16[640,256]{1,0:T(8,128)(2,1)S(1)}, u32[]{:S(2)}, u32[]{:S(2)}) collective-permute-start(bf16[640,256]{1,0:T(8,128)(2,1)S(1)} %collective-permute-done), channel_id=1, source_target_pairs={{0,112},{16,0},{32,16},{48,32},{64,48},{80,64},{96,80},{112,96},{1... | collective-permute-start | bytes 983048 | tf_op jit(solution)/shard_map/ppermute | solution.py:149
  46.3 3.1 %collective-permute-done.4 = bf16[640,256]{1,0:T(8,128)(2,1)S(1)} collective-permute-done((bf16[640,256]{1,0:T(8,128)(2,1)S(1)}, bf16[640,256]{1,0:T(8,128)(2,1)S(1)}, u32[]{:S(2)}, u32[]{:S(2)}) %collective-permute-start.4) | collective-permute-done | bytes 327712 | tf_op jit(solution)/shard_map/ppermute | solution.py:149
  49.4 1.9 %collective-permute-start.5 = (bf16[640,256]{1,0:T(8,128)(2,1)S(1)}, bf16[640,256]{1,0:T(8,128)(2,1)S(1)}, u32[]{:S(2)}, u32[]{:S(2)}) collective-permute-start(bf16[640,256]{1,0:T(8,128)(2,1)S(1)} %collective-permute-done.4), channel_id=1, source_target_pairs={{0,16},{16,32},{32,48},{48,64},{64,80},{80,96},{96,112},{112,0},{1... | collective-permute-start | bytes 983048 | tf_op jit(solution)/shard_map/ppermute | solution.py:149
  51.9 5.1 %collective-permute-start.2 = (bf16[640,256]{1,0:T(8,128)(2,1)S(1)}, bf16[640,256]{1,0:T(8,128)(2,1)S(1)}, u32[]{:S(2)}, u32[]{:S(2)}) collective-permute-start(bf16[640,256]{1,0:T(8,128)(2,1)S(1)} %collective-permute-done.1), channel_id=1, source_target_pairs={{0,112},{16,0},{32,16},{48,32},{64,48},{80,64},{96,80},{112,96},{1... | collective-permute-start | bytes 983048 | tf_op jit(solution)/shard_map/ppermute | solution.py:149
  57.6 2.0 %collective-permute-done.5 = bf16[640,256]{1,0:T(8,128)(2,1)S(1)} collective-permute-done((bf16[640,256]{1,0:T(8,128)(2,1)S(1)}, bf16[640,256]{1,0:T(8,128)(2,1)S(1)}, u32[]{:S(2)}, u32[]{:S(2)}) %collective-permute-start.5) | collective-permute-done | bytes 327712 | tf_op jit(solution)/shard_map/ppermute | solution.py:149
  59.6 1.9 %collective-permute-start.6 = (bf16[640,256]{1,0:T(8,128)(2,1)S(1)}, bf16[640,256]{1,0:T(8,128)(2,1)S(1)}, u32[]{:S(2)}, u32[]{:S(2)}) collective-permute-start(bf16[640,256]{1,0:T(8,128)(2,1)S(1)} %collective-permute-done.5), channel_id=1, source_target_pairs={{0,16},{16,32},{32,48},{48,64},{64,80},{80,96},{96,112},{112,0},{1... | collective-permute-start | bytes 983048 | tf_op jit(solution)/shard_map/ppermute | solution.py:149
  61.6 8.1 %collective-permute-done.6 = bf16[640,256]{1,0:T(8,128)(2,1)S(1)} collective-permute-done((bf16[640,256]{1,0:T(8,128)(2,1)S(1)}, bf16[640,256]{1,0:T(8,128)(2,1)S(1)}, u32[]{:S(2)}, u32[]{:S(2)}) %collective-permute-start.6) | collective-permute-done | bytes 327712 | tf_op jit(solution)/shard_map/ppermute | solution.py:149
  69.9 1.5 copy-done.2
  71.4 17.3 %shard_map.84 = (bf16[640,128]{1,0:T(8,128)(2,1)}, bf16[640,128]{1,0:T(8,128)(2,1)}, bf16[5120,256]{1,0:T(8,128)(2,1)}) custom-call(s32[4]{0:T(128)} %pad_add_fusion.limits_ref, s32[64]{0:T(128)} %multiply_add_fusion.1.source_ref, s32[64]{0:T(128)} %get-tuple-element.10.target_ref, bf16[640,128]{1,0:T(8,128)(2,1)} %bitcast.31, bf16[640,128]{1,0:T(8,128)(2,1)} %bitcast.32, ...), custom_call_target="tpu_custom_call" | custom-call | flops 2936012800 | bytes 7864320 | tf_op jit(solution)/shard_map/pallas_call | solution.py:157
  88.7 62.6 %all_to_all.10 = bf16[8,4,160,256]{3,2,1,0:T(8,128)(2,1)S(1)} all-to-all(bf16[8,4,160,256]{3,2,1,0:T(8,128)(2,1)} %bitcast.28), channel_id=1, replica_groups=mesh['zh'=4,'y'=8,'head'=16] {'y'}, dimensions={0} | all-to-all | bytes 5242880 | tf_op jit(solution)/shard_map/all_to_all | solution.py:254
  151.3 1.2 reduce_sum.21
  152.5 3.5 %all-to-all-start.1 = ((bf16[4,160,256]{2,1,0:T(8,128)(2,1)}), bf16[4,160,256]{2,1,0:T(8,128)(2,1)S(1)}, u32[]{:S(2)}, u32[]{:S(2)}) async-start(bf16[4,160,256]{2,1,0:T(8,128)(2,1)} %reduce_sum.21), calls=%async_computation.1 | async-start | bytes 655360 | tf_op jit(solution)/shard_map/all_to_all | solution.py:256
  157.6 8.5 %all-to-all-done.1 = bf16[4,160,256]{2,1,0:T(8,128)(2,1)S(1)} async-done(((bf16[4,160,256]{2,1,0:T(8,128)(2,1)}), bf16[4,160,256]{2,1,0:T(8,128)(2,1)S(1)}, u32[]{:S(2)}, u32[]{:S(2)}) %all-to-all-start.1) | async-done | bytes 327712 | tf_op jit(solution)/shard_map/all_to_all | solution.py:256
  (37 shorter events, 7.0 us)
Async XLA Ops:
  21.4 19.8 %collective-permute-start = (bf16[640,256]{1,0:T(8,128)(2,1)S(1)}, bf16[640,256]{1,0:T(8,128)(2,1)S(1)}, u32[]{:S(2)}, u32[]{:S(2)}) collective-permute-start(bf16[640,256]{1,0:T(8,128)(2,1)S(1)} %all_gather.3), channel_id=1, source_target_pairs={{0,112},{16,0},{32,16},{48,32},{64,48},{80,64},{96,80},{112,96},{1... | collective-permute-start | bytes 983048 | tf_op jit(solution)/shard_map/ppermute | solution.py:149
  26.8 11.7 %collective-permute-start.3 = (bf16[640,256]{1,0:T(8,128)(2,1)S(1)}, bf16[640,256]{1,0:T(8,128)(2,1)S(1)}, u32[]{:S(2)}, u32[]{:S(2)}) collective-permute-start(bf16[640,256]{1,0:T(8,128)(2,1)S(1)} %all_gather.3), channel_id=1, source_target_pairs={{0,16},{16,32},{32,48},{48,64},{64,80},{80,96},{96,112},{112,0},{1... | collective-permute-start | bytes 983048 | tf_op jit(solution)/shard_map/ppermute | solution.py:149
  38.6 10.8 %collective-permute-start.4 = (bf16[640,256]{1,0:T(8,128)(2,1)S(1)}, bf16[640,256]{1,0:T(8,128)(2,1)S(1)}, u32[]{:S(2)}, u32[]{:S(2)}) collective-permute-start(bf16[640,256]{1,0:T(8,128)(2,1)S(1)} %collective-permute-done.3), channel_id=1, source_target_pairs={{0,16},{16,32},{32,48},{48,64},{64,80},{80,96},{96,112},{112,0},{1... | collective-permute-start | bytes 983048 | tf_op jit(solution)/shard_map/ppermute | solution.py:149
  41.2 10.7 %collective-permute-start.1 = (bf16[640,256]{1,0:T(8,128)(2,1)S(1)}, bf16[640,256]{1,0:T(8,128)(2,1)S(1)}, u32[]{:S(2)}, u32[]{:S(2)}) collective-permute-start(bf16[640,256]{1,0:T(8,128)(2,1)S(1)} %collective-permute-done), channel_id=1, source_target_pairs={{0,112},{16,0},{32,16},{48,32},{64,48},{80,64},{96,80},{112,96},{1... | collective-permute-start | bytes 983048 | tf_op jit(solution)/shard_map/ppermute | solution.py:149
  49.4 10.2 %collective-permute-start.5 = (bf16[640,256]{1,0:T(8,128)(2,1)S(1)}, bf16[640,256]{1,0:T(8,128)(2,1)S(1)}, u32[]{:S(2)}, u32[]{:S(2)}) collective-permute-start(bf16[640,256]{1,0:T(8,128)(2,1)S(1)} %collective-permute-done.4), channel_id=1, source_target_pairs={{0,16},{16,32},{32,48},{48,64},{64,80},{80,96},{96,112},{112,0},{1... | collective-permute-start | bytes 983048 | tf_op jit(solution)/shard_map/ppermute | solution.py:149
  51.9 9.7 %collective-permute-start.2 = (bf16[640,256]{1,0:T(8,128)(2,1)S(1)}, bf16[640,256]{1,0:T(8,128)(2,1)S(1)}, u32[]{:S(2)}, u32[]{:S(2)}) collective-permute-start(bf16[640,256]{1,0:T(8,128)(2,1)S(1)} %collective-permute-done.1), channel_id=1, source_target_pairs={{0,112},{16,0},{32,16},{48,32},{64,48},{80,64},{96,80},{112,96},{1... | collective-permute-start | bytes 983048 | tf_op jit(solution)/shard_map/ppermute | solution.py:149
  59.6 10.2 %collective-permute-start.6 = (bf16[640,256]{1,0:T(8,128)(2,1)S(1)}, bf16[640,256]{1,0:T(8,128)(2,1)S(1)}, u32[]{:S(2)}, u32[]{:S(2)}) collective-permute-start(bf16[640,256]{1,0:T(8,128)(2,1)S(1)} %collective-permute-done.5), channel_id=1, source_target_pairs={{0,16},{16,32},{32,48},{48,64},{64,80},{80,96},{96,112},{112,0},{1... | collective-permute-start | bytes 983048 | tf_op jit(solution)/shard_map/ppermute | solution.py:149
  69.9 1.5 copy-start.2
  151.3 4.7 %copy-start = (bf16[640,128]{1,0:T(8,128)(2,1)S(1)}, bf16[640,128]{1,0:T(8,128)(2,1)}, u32[]{:S(2)}) copy-start(bf16[640,128]{1,0:T(8,128)(2,1)} %get-tuple-element.7) | copy-start | bytes 491524
  151.3 4.7 %copy-start.1 = (bf16[640,128]{1,0:T(8,128)(2,1)S(1)}, bf16[640,128]{1,0:T(8,128)(2,1)}, u32[]{:S(2)}) copy-start(bf16[640,128]{1,0:T(8,128)(2,1)} %get-tuple-element.8) | copy-start | bytes 491524
  152.5 13.6 %all-to-all-start.1 = ((bf16[4,160,256]{2,1,0:T(8,128)(2,1)}), bf16[4,160,256]{2,1,0:T(8,128)(2,1)S(1)}, u32[]{:S(2)}, u32[]{:S(2)}) async-start(bf16[4,160,256]{2,1,0:T(8,128)(2,1)} %reduce_sum.21), calls=%async_computation.1 | async-start | bytes 655360 | tf_op jit(solution)/shard_map/all_to_all | solution.py:256

commit v13 on v11

--- a/solution.py
+++ b/solution.py
@@ -97,7 +97,6 @@
     dot_ref[...] = jnp.sum(
         g_ref[...].astype(jnp.float32) * attention.astype(jnp.float32), axis=1, keepdims=True
     )
-    dqacc_ref[...] = jnp.zeros(dqacc_ref.shape, jnp.float32)
 
     def clear_block(block, carry):
         start = pl.multiple_of(block * KEY_BLOCK, KEY_BLOCK)
@@ -106,7 +105,7 @@
 
     lax.fori_loop(late_blocks, dkv_ref.shape[0] // KEY_BLOCK, clear_block, 0)
 
-    def backward_masked(lo, count, start, masked):
+    def backward_masked(lo, count, start, masked, first=False):
         s = scores_of(lo, count, start, masked)
         probs = jnp.exp(s - lse_ref[lo:lo + count, :])
         g = g_ref[lo:lo + count, :]
@@ -114,7 +113,11 @@
         v = kv_ref[pl.ds(start, KEY_BLOCK), width:2 * width]
         grad_probs = lax.dot_general(g, v, (((1,), (1,)), ((), ())), preferred_element_type=jnp.float32)
         grad_scores = (probs * (grad_probs - dot_ref[lo:lo + count, :])).astype(jnp.bfloat16)
-        dqacc_ref[lo:lo + count, :] += jnp.dot(grad_scores, k, preferred_element_type=jnp.float32)
+        dq_part = jnp.dot(grad_scores, k, preferred_element_type=jnp.float32)
+        if first:
+            dqacc_ref[lo:lo + count, :] = dq_part
+        else:
+            dqacc_ref[lo:lo + count, :] += dq_part
         q = q_ref[lo:lo + count, :]
         dk = lax.dot_general(grad_scores, q, (((0,), (0,)), ((), ())), preferred_element_type=jnp.float32)
         dv = lax.dot_general(
@@ -131,7 +134,11 @@
         split_by_mask(backward_masked, half, half, block, late_first)
         return carry
 
-    lax.fori_loop(0, early_blocks, bwd_both, 0)
+    def backward_first(lo, count, start, masked):
+        backward_masked(lo, count, start, masked, first=True)
+
+    split_by_mask(backward_first, 0, rows, 0, early_first)
+    lax.fori_loop(1, early_blocks, bwd_both, 0)
     lax.fori_loop(early_blocks, late_blocks, bwd_late, 0)
     dq_ref[...] = (dqacc_ref[...] * scale).astype(jnp.bfloat16)
 

time: 168 us -> 168 us (level)
  no operation moved by 1% of the time
where the time goes in v13:
time: 168 us; the launch traced here: 167 us
  blocking collectives  83 us (49%)
  starting transfers between devices  26.8 us (16%)
  waiting for transfers between devices  21.6 us (13%)
  Pallas kernels  17 us (10%)
  local copies, waits for them, and re-layouts  8.8 us (5%)
  other arithmetic  6.67 us (4%)
  between operations  3.43 us (2%)
    all_to_all x1, blocking collectives, on_device(): row_parts = lax.all_to_all(dkv_all, 'y', 0, 0, tiled=False)  63 us
    ppermute x7, starting transfers between devices, shifted(): lax.ppermute(array, axis, [(i, (i + by) % length) for i in range(length)])  23.3 us
    all_gather x1, blocking collectives, on_device(): column = lax.all_gather(kv_local, 'zh', axis=0, tiled=True)  20 us
    pallas_call x1, Pallas kernels, local_attention(): pl.pallas_call(attention_kernel, out_shape=(jax.ShapeDtypeStruct((rows, w...  17 us
    ppermute x7, waiting for transfers between devices, shifted(): lax.ppermute(array, axis, [(i, (i + by) % length) for i in range(length)])  13.3 us
    all_to_all x1, waiting for transfers between devices, on_device(): lax.all_to_all(row_sums.astype(jnp.bfloat16), 'zh', 0, 0, tiled=False)  8.32 us
    all_to_all x1, starting transfers between devices, on_device(): lax.all_to_all(row_sums.astype(jnp.bfloat16), 'zh', 0, 0, tiled=False)  3.56 us
  transfers between devices with their start and end apart: 8, of which 4 were waited for; matrix products, arithmetic and copies ran while one was open for 6% of the time, Pallas kernels for 0%

profile of v13, /device:TPU:6, one launch (start us, length us, event | category | flops | bytes accessed | tf_op | source)
XLA Modules:
  0.0 167.3 jit_solution(11636352392377604673)
XLA Ops:
  0.6 0.8 pad_maximum_fusion
  1.4 20.0 %all_gather.3 = bf16[640,256]{1,0:T(8,128)(2,1)S(1)} all-gather(bf16[160,256]{1,0:T(8,128)(2,1)S(1)} %pad_maximum_fusion), channel_id=1, replica_groups=mesh['zh'=4,'y'=8,'head'=16] {'zh'}, dimensions={0}, use_global_device_ids=true | all-gather | bytes 409600 | tf_op jit(solution)/shard_map/all_gather | solution.py:213
  21.4 5.4 %collective-permute-start = (bf16[640,256]{1,0:T(8,128)(2,1)S(1)}, bf16[640,256]{1,0:T(8,128)(2,1)S(1)}, u32[]{:S(2)}, u32[]{:S(2)}) collective-permute-start(bf16[640,256]{1,0:T(8,128)(2,1)S(1)} %all_gather.3), channel_id=1, source_target_pairs={{0,112},{16,0},{32,16},{48,32},{64,48},{80,64},{96,80},{112,96},{1... | collective-permute-start | bytes 983048 | tf_op jit(solution)/shard_map/ppermute | solution.py:156
  26.8 1.9 %collective-permute-start.3 = (bf16[640,256]{1,0:T(8,128)(2,1)S(1)}, bf16[640,256]{1,0:T(8,128)(2,1)S(1)}, u32[]{:S(2)}, u32[]{:S(2)}) collective-permute-start(bf16[640,256]{1,0:T(8,128)(2,1)S(1)} %all_gather.3), channel_id=1, source_target_pairs={{0,16},{16,32},{32,48},{48,64},{64,80},{80,96},{96,112},{112,0},{1... | collective-permute-start | bytes 983048 | tf_op jit(solution)/shard_map/ppermute | solution.py:156
  28.7 0.7 dynamic_slice.3
  32.7 1.0 reshape.97
  33.7 1.0 reshape.99
  34.7 0.7 reverse_select_fusion.3
  36.9 0.9 reshape.116.qpos_ref
  37.8 0.8 scatter_custom_fusion
  38.6 2.0 %collective-permute-start.4 = (bf16[640,256]{1,0:T(8,128)(2,1)S(1)}, bf16[640,256]{1,0:T(8,128)(2,1)S(1)}, u32[]{:S(2)}, u32[]{:S(2)}) collective-permute-start(bf16[640,256]{1,0:T(8,128)(2,1)S(1)} %collective-permute-done.3), channel_id=1, source_target_pairs={{0,16},{16,32},{32,48},{48,64},{64,80},{80,96},{96,112},{112,0},{1... | collective-permute-start | bytes 983048 | tf_op jit(solution)/shard_map/ppermute | solution.py:156
  41.2 5.0 %collective-permute-start.1 = (bf16[640,256]{1,0:T(8,128)(2,1)S(1)}, bf16[640,256]{1,0:T(8,128)(2,1)S(1)}, u32[]{:S(2)}, u32[]{:S(2)}) collective-permute-start(bf16[640,256]{1,0:T(8,128)(2,1)S(1)} %collective-permute-done), channel_id=1, source_target_pairs={{0,112},{16,0},{32,16},{48,32},{64,48},{80,64},{96,80},{112,96},{1... | collective-permute-start | bytes 983048 | tf_op jit(solution)/shard_map/ppermute | solution.py:156
  46.3 3.1 %collective-permute-done.4 = bf16[640,256]{1,0:T(8,128)(2,1)S(1)} collective-permute-done((bf16[640,256]{1,0:T(8,128)(2,1)S(1)}, bf16[640,256]{1,0:T(8,128)(2,1)S(1)}, u32[]{:S(2)}, u32[]{:S(2)}) %collective-permute-start.4) | collective-permute-done | bytes 327712 | tf_op jit(solution)/shard_map/ppermute | solution.py:156
  49.4 1.9 %collective-permute-start.5 = (bf16[640,256]{1,0:T(8,128)(2,1)S(1)}, bf16[640,256]{1,0:T(8,128)(2,1)S(1)}, u32[]{:S(2)}, u32[]{:S(2)}) collective-permute-start(bf16[640,256]{1,0:T(8,128)(2,1)S(1)} %collective-permute-done.4), channel_id=1, source_target_pairs={{0,16},{16,32},{32,48},{48,64},{64,80},{80,96},{96,112},{112,0},{1... | collective-permute-start | bytes 983048 | tf_op jit(solution)/shard_map/ppermute | solution.py:156
  51.9 5.1 %collective-permute-start.2 = (bf16[640,256]{1,0:T(8,128)(2,1)S(1)}, bf16[640,256]{1,0:T(8,128)(2,1)S(1)}, u32[]{:S(2)}, u32[]{:S(2)}) collective-permute-start(bf16[640,256]{1,0:T(8,128)(2,1)S(1)} %collective-permute-done.1), channel_id=1, source_target_pairs={{0,112},{16,0},{32,16},{48,32},{64,48},{80,64},{96,80},{112,96},{1... | collective-permute-start | bytes 983048 | tf_op jit(solution)/shard_map/ppermute | solution.py:156
  57.6 2.0 %collective-permute-done.5 = bf16[640,256]{1,0:T(8,128)(2,1)S(1)} collective-permute-done((bf16[640,256]{1,0:T(8,128)(2,1)S(1)}, bf16[640,256]{1,0:T(8,128)(2,1)S(1)}, u32[]{:S(2)}, u32[]{:S(2)}) %collective-permute-start.5) | collective-permute-done | bytes 327712 | tf_op jit(solution)/shard_map/ppermute | solution.py:156
  59.6 1.9 %collective-permute-start.6 = (bf16[640,256]{1,0:T(8,128)(2,1)S(1)}, bf16[640,256]{1,0:T(8,128)(2,1)S(1)}, u32[]{:S(2)}, u32[]{:S(2)}) collective-permute-start(bf16[640,256]{1,0:T(8,128)(2,1)S(1)} %collective-permute-done.5), channel_id=1, source_target_pairs={{0,16},{16,32},{32,48},{48,64},{64,80},{80,96},{96,112},{112,0},{1... | collective-permute-start | bytes 983048 | tf_op jit(solution)/shard_map/ppermute | solution.py:156
  61.6 8.1 %collective-permute-done.6 = bf16[640,256]{1,0:T(8,128)(2,1)S(1)} collective-permute-done((bf16[640,256]{1,0:T(8,128)(2,1)S(1)}, bf16[640,256]{1,0:T(8,128)(2,1)S(1)}, u32[]{:S(2)}, u32[]{:S(2)}) %collective-permute-start.6) | collective-permute-done | bytes 327712 | tf_op jit(solution)/shard_map/ppermute | solution.py:156
  69.9 1.5 copy-done.2
  71.4 17.0 %shard_map.84 = (bf16[640,128]{1,0:T(8,128)(2,1)}, bf16[640,128]{1,0:T(8,128)(2,1)}, bf16[5120,256]{1,0:T(8,128)(2,1)}) custom-call(s32[4]{0:T(128)} %pad_add_fusion.limits_ref, s32[64]{0:T(128)} %multiply_add_fusion.1.source_ref, s32[64]{0:T(128)} %get-tuple-element.10.target_ref, bf16[640,128]{1,0:T(8,128)(2,1)} %bitcast.31, bf16[640,128]{1,0:T(8,128)(2,1)} %bitcast.32, ...), custom_call_target="tpu_custom_call" | custom-call | flops 2936012800 | bytes 7864320 | tf_op jit(solution)/shard_map/pallas_call | solution.py:164
  88.4 63.0 %all_to_all.10 = bf16[8,4,160,256]{3,2,1,0:T(8,128)(2,1)S(1)} all-to-all(bf16[8,4,160,256]{3,2,1,0:T(8,128)(2,1)} %bitcast.28), channel_id=1, replica_groups=mesh['zh'=4,'y'=8,'head'=16] {'y'}, dimensions={0} | all-to-all | bytes 5242880 | tf_op jit(solution)/shard_map/all_to_all | solution.py:261
  151.3 1.2 reduce_sum.21
  152.5 3.6 %all-to-all-start.1 = ((bf16[4,160,256]{2,1,0:T(8,128)(2,1)}), bf16[4,160,256]{2,1,0:T(8,128)(2,1)S(1)}, u32[]{:S(2)}, u32[]{:S(2)}) async-start(bf16[4,160,256]{2,1,0:T(8,128)(2,1)} %reduce_sum.21), calls=%async_computation.1 | async-start | bytes 655360 | tf_op jit(solution)/shard_map/all_to_all | solution.py:263
  157.7 8.3 %all-to-all-done.1 = bf16[4,160,256]{2,1,0:T(8,128)(2,1)S(1)} async-done(((bf16[4,160,256]{2,1,0:T(8,128)(2,1)}), bf16[4,160,256]{2,1,0:T(8,128)(2,1)S(1)}, u32[]{:S(2)}, u32[]{:S(2)}) %all-to-all-start.1) | async-done | bytes 327712 | tf_op jit(solution)/shard_map/all_to_all | solution.py:263
  (37 shorter events, 7.0 us)
Async XLA Ops:
  21.4 19.8 %collective-permute-start = (bf16[640,256]{1,0:T(8,128)(2,1)S(1)}, bf16[640,256]{1,0:T(8,128)(2,1)S(1)}, u32[]{:S(2)}, u32[]{:S(2)}) collective-permute-start(bf16[640,256]{1,0:T(8,128)(2,1)S(1)} %all_gather.3), channel_id=1, source_target_pairs={{0,112},{16,0},{32,16},{48,32},{64,48},{80,64},{96,80},{112,96},{1... | collective-permute-start | bytes 983048 | tf_op jit(solution)/shard_map/ppermute | solution.py:156
  26.8 11.7 %collective-permute-start.3 = (bf16[640,256]{1,0:T(8,128)(2,1)S(1)}, bf16[640,256]{1,0:T(8,128)(2,1)S(1)}, u32[]{:S(2)}, u32[]{:S(2)}) collective-permute-start(bf16[640,256]{1,0:T(8,128)(2,1)S(1)} %all_gather.3), channel_id=1, source_target_pairs={{0,16},{16,32},{32,48},{48,64},{64,80},{80,96},{96,112},{112,0},{1... | collective-permute-start | bytes 983048 | tf_op jit(solution)/shard_map/ppermute | solution.py:156
  38.6 10.8 %collective-permute-start.4 = (bf16[640,256]{1,0:T(8,128)(2,1)S(1)}, bf16[640,256]{1,0:T(8,128)(2,1)S(1)}, u32[]{:S(2)}, u32[]{:S(2)}) collective-permute-start(bf16[640,256]{1,0:T(8,128)(2,1)S(1)} %collective-permute-done.3), channel_id=1, source_target_pairs={{0,16},{16,32},{32,48},{48,64},{64,80},{80,96},{96,112},{112,0},{1... | collective-permute-start | bytes 983048 | tf_op jit(solution)/shard_map/ppermute | solution.py:156
  41.2 10.7 %collective-permute-start.1 = (bf16[640,256]{1,0:T(8,128)(2,1)S(1)}, bf16[640,256]{1,0:T(8,128)(2,1)S(1)}, u32[]{:S(2)}, u32[]{:S(2)}) collective-permute-start(bf16[640,256]{1,0:T(8,128)(2,1)S(1)} %collective-permute-done), channel_id=1, source_target_pairs={{0,112},{16,0},{32,16},{48,32},{64,48},{80,64},{96,80},{112,96},{1... | collective-permute-start | bytes 983048 | tf_op jit(solution)/shard_map/ppermute | solution.py:156
  49.4 10.2 %collective-permute-start.5 = (bf16[640,256]{1,0:T(8,128)(2,1)S(1)}, bf16[640,256]{1,0:T(8,128)(2,1)S(1)}, u32[]{:S(2)}, u32[]{:S(2)}) collective-permute-start(bf16[640,256]{1,0:T(8,128)(2,1)S(1)} %collective-permute-done.4), channel_id=1, source_target_pairs={{0,16},{16,32},{32,48},{48,64},{64,80},{80,96},{96,112},{112,0},{1... | collective-permute-start | bytes 983048 | tf_op jit(solution)/shard_map/ppermute | solution.py:156
  51.9 9.7 %collective-permute-start.2 = (bf16[640,256]{1,0:T(8,128)(2,1)S(1)}, bf16[640,256]{1,0:T(8,128)(2,1)S(1)}, u32[]{:S(2)}, u32[]{:S(2)}) collective-permute-start(bf16[640,256]{1,0:T(8,128)(2,1)S(1)} %collective-permute-done.1), channel_id=1, source_target_pairs={{0,112},{16,0},{32,16},{48,32},{64,48},{80,64},{96,80},{112,96},{1... | collective-permute-start | bytes 983048 | tf_op jit(solution)/shard_map/ppermute | solution.py:156
  59.6 10.2 %collective-permute-start.6 = (bf16[640,256]{1,0:T(8,128)(2,1)S(1)}, bf16[640,256]{1,0:T(8,128)(2,1)S(1)}, u32[]{:S(2)}, u32[]{:S(2)}) collective-permute-start(bf16[640,256]{1,0:T(8,128)(2,1)S(1)} %collective-permute-done.5), channel_id=1, source_target_pairs={{0,16},{16,32},{32,48},{48,64},{64,80},{80,96},{96,112},{112,0},{1... | collective-permute-start | bytes 983048 | tf_op jit(solution)/shard_map/ppermute | solution.py:156
  69.9 1.5 copy-start.2
  151.3 4.7 %copy-start = (bf16[640,128]{1,0:T(8,128)(2,1)S(1)}, bf16[640,128]{1,0:T(8,128)(2,1)}, u32[]{:S(2)}) copy-start(bf16[640,128]{1,0:T(8,128)(2,1)} %get-tuple-element.7) | copy-start | bytes 491524
  151.3 4.7 %copy-start.1 = (bf16[640,128]{1,0:T(8,128)(2,1)S(1)}, bf16[640,128]{1,0:T(8,128)(2,1)}, u32[]{:S(2)}) copy-start(bf16[640,128]{1,0:T(8,128)(2,1)} %get-tuple-element.8) | copy-start | bytes 491524
  152.5 13.5 %all-to-all-start.1 = ((bf16[4,160,256]{2,1,0:T(8,128)(2,1)}), bf16[4,160,256]{2,1,0:T(8,128)(2,1)S(1)}, u32[]{:S(2)}, u32[]{:S(2)}) async-start(bf16[4,160,256]{2,1,0:T(8,128)(2,1)} %reduce_sum.21), calls=%async_computation.1 | async-start | bytes 655360 | tf_op jit(solution)/shard_map/all_to_all | solution.py:263
